TPU v7x, 32 devices: a whole 2x2x4 slice. The times are simulated.
32 devices in a mesh: dp: 16 (over z, y, x), fsdp: 2 (over core).
Axes of the slice: x: 2, y: 2, z: 4, core: 2. Of those that a mesh axis runs over, the one named last changes fastest.
Arguments:
- tokens: bfloat16 [16384, 768], P(('dp', 'fsdp')), may hold values from -6 to 6
- segments: int32 [16384], P(('dp', 'fsdp')), may hold values from -1 to 15, as said below
- mask_flags: int32 [16384], P(('dp', 'fsdp')), may hold values from 0 to 1, as said below
- targets: int32 [16384], P(('dp', 'fsdp')), may hold values from 0 to 50175
- cotangent: bfloat16 [16384, 768], P(('dp', 'fsdp')), may hold values from -6 to 6
- qkv_weight: bfloat16 [768, 2304], P(('dp', 'fsdp')), may hold values from -0.21875 to 0.21875
- attn_bias: bfloat16 [1536], P(('dp', 'fsdp')), may hold values from -4 to 4
- out_weight: bfloat16 [768, 768], P(('dp', 'fsdp')), may hold values from -0.875 to 0.875
- out_bias: bfloat16 [768], P(('dp', 'fsdp')), may hold values from -4 to 4
- attn_gain: bfloat16 [768], P(('dp', 'fsdp')), may hold values from 0.25 to 1.75
- attn_shift: bfloat16 [768], P(('dp', 'fsdp')), may hold values from -4 to 4
- up_weight: bfloat16 [768, 3072], P(('dp', 'fsdp')), may hold values from -0.21875 to 0.21875
- up_bias: bfloat16 [3072], P(('dp', 'fsdp')), may hold values from -4 to 4
- down_weight: bfloat16 [3072, 768], P(('dp', 'fsdp')), may hold values from -0.15625 to 0.15625
- down_bias: bfloat16 [768], P(('dp', 'fsdp')), may hold values from -4 to 4
- ffn_gain: bfloat16 [768], P(('dp', 'fsdp')), may hold values from 0.25 to 1.75
- ffn_shift: bfloat16 [768], P(('dp', 'fsdp')), may hold values from -4 to 4
- dense_weight: bfloat16 [768, 768], P(('dp', 'fsdp')), may hold values from -0.21875 to 0.21875
- dense_bias: bfloat16 [768], P(('dp', 'fsdp')), may hold values from -4 to 4
- head_gain: bfloat16 [768], P(('dp', 'fsdp')), may hold values from 0.25 to 1.75
- head_shift: bfloat16 [768], P(('dp', 'fsdp')), may hold values from -4 to 4
- decoder: bfloat16 [50176, 768], P(('dp', 'fsdp')), may hold values from -0.4375 to 0.4375
- vocab_bias: bfloat16 [50176], P(('dp', 'fsdp')), may hold values from 0.5 to 2.5
Outputs:
- output: bfloat16 [16384, 768], P(('dp', 'fsdp'))
- mean_loss: float32 [], replicated
- tokens_grad: float32 [16384, 768], P(('dp', 'fsdp'))
- qkv_weight_grad: float32 [768, 2304], P(('dp', 'fsdp'))
- attn_bias_grad: float32 [1536], P(('dp', 'fsdp'))
- out_weight_grad: float32 [768, 768], P(('dp', 'fsdp'))
- out_bias_grad: float32 [768], P(('dp', 'fsdp'))
- attn_gain_grad: float32 [768], P(('dp', 'fsdp'))
- attn_shift_grad: float32 [768], P(('dp', 'fsdp'))
- up_weight_grad: float32 [768, 3072], P(('dp', 'fsdp'))
- up_bias_grad: float32 [3072], P(('dp', 'fsdp'))
- down_weight_grad: float32 [3072, 768], P(('dp', 'fsdp'))
- down_bias_grad: float32 [768], P(('dp', 'fsdp'))
- ffn_gain_grad: float32 [768], P(('dp', 'fsdp'))
- ffn_shift_grad: float32 [768], P(('dp', 'fsdp'))
- dense_weight_grad: float32 [768, 768], P(('dp', 'fsdp'))
- dense_bias_grad: float32 [768], P(('dp', 'fsdp'))
- head_gain_grad: float32 [768], P(('dp', 'fsdp'))
- head_shift_grad: float32 [768], P(('dp', 'fsdp'))
- decoder_grad: float32 [50176, 768], P(('dp', 'fsdp'))
- vocab_bias_grad: float32 [50176], P(('dp', 'fsdp'))
Inputs may be any that keep to these rules, and one draw needn't show every extreme that they name: `segments`: the rows of one device are one pack of 512 positions. Within a pack ids start at 0 and rise by one at each new sequence; every sequence has 32 to 512 positions; positions after the pack's last sequence, fewer than 32, hold -1. The first pack is one sequence of 512 positions; the second pack is 16 sequences of 32 positions. `mask_flags`: flags fall only on positions whose segment is not -1. The devices that share one fsdp index hold exactly 1024 flags together; each device holds at most 128, and in every draw a device of each fsdp index holds exactly 128.
All inputs are finite; a program needn't handle non-finite values.
Results may differ from a plain program's by a relative error of at most 0.014.
Values may be sent and summed in bfloat16 or wider, within the bound.
No kernel may reach another device: no remote copies, remote signals or barrier semaphores. Data moves between devices by JAX's collectives and lax.ppermute only.
A program may use at most 576 MiB of HBM per device.

v0:
```python
import jax
import jax.numpy as jnp
from jax import lax
from jax.sharding import PartitionSpec as P

HEADS = 12
HEAD_DIM = 64
MASK_DEV = 64
MAXM = 128


EPSILON = 1e-05
NEGATIVE = -1e30


def combined_all(value, axis, join):
    pieces = jax.tree.map(lambda part: lax.all_gather(part, axis), value)
    head = jax.tree.map(lambda part: part[0], pieces)
    tail = jax.tree.map(lambda part: part[1:], pieces)
    subtotal, _ = lax.scan(lambda subtotal, slab: (join(subtotal, slab), None), head, tail)
    return subtotal


def to_low(values):
    return values.astype(jnp.bfloat16)


def to_full(values):
    return values.astype(jnp.float32)


def layer_norm(values, gain_vector, shift_vector):
    center = values - jnp.mean(values, axis=-1, keepdims=True)
    spread = jnp.mean(center * center, axis=-1, keepdims=True)
    return center * lax.rsqrt(spread + EPSILON) * gain_vector + shift_vector


def gelu_exact(values):
    return jax.nn.gelu(values, approximate=False)


def head_tail(dense_out, gain_vector, shift_vector):
    return layer_norm(gelu_exact(dense_out), gain_vector, shift_vector)


def matmul(left_side, right_side):
    return jnp.dot(left_side, right_side, preferred_element_type=jnp.float32)


def matmul_tn(left_side, right_side):
    return lax.dot_general(
        left_side, right_side, (((0,), (0,)), ((), ())), preferred_element_type=jnp.float32
    )


def matmul_nt(left_side, right_side):
    return lax.dot_general(
        left_side, right_side, (((1,), (1,)), ((), ())), preferred_element_type=jnp.float32
    )


def attention_forward(tokens, segments, params):
    qkv_weight, attn_bias, out_weight, out_bias, attn_gain, attn_shift = params
    row_count, model_width = tokens.shape
    shaped = (row_count, HEADS, HEAD_DIM)
    score_scale = HEAD_DIM ** (-0.5)
    projected = matmul(tokens, qkv_weight)
    bias_full = to_full(attn_bias)
    queries = to_low(projected[:, :model_width] + bias_full[:model_width]).reshape(shaped)
    keys_low = to_low(projected[:, model_width : 2 * model_width]).reshape(shaped)
    values_low = to_low(projected[:, 2 * model_width :] + bias_full[model_width:]).reshape(shaped)
    scores = (
        jnp.einsum("qhd,khd->hqk", queries, keys_low, preferred_element_type=jnp.float32)
        * score_scale
    )
    same_doc = segments[:, None] == segments[None, :]
    scores = jnp.where(same_doc[None], scores, NEGATIVE)
    row_peak = jnp.max(scores, axis=-1, keepdims=True)
    exponent = jnp.exp(scores - row_peak)
    softmax = exponent / jnp.sum(exponent, axis=-1, keepdims=True)
    softmax_low = to_low(softmax)
    context = to_low(
        jnp.einsum(
            "hqk,khd->qhd", softmax_low, values_low, preferred_element_type=jnp.float32
        ).reshape(row_count, model_width)
    )
    summed = to_full(tokens) + matmul(context, out_weight) + to_full(out_bias)
    hidden = to_low(layer_norm(summed, to_full(attn_gain), to_full(attn_shift)))
    return (hidden, (queries, keys_low, values_low, softmax, softmax_low, context, summed))


def attention_backward(tokens, segments, params, hidden_grad):
    qkv_weight, attn_bias, out_weight, out_bias, attn_gain, attn_shift = params
    row_count, model_width = tokens.shape
    shaped = (row_count, HEADS, HEAD_DIM)
    score_scale = HEAD_DIM ** (-0.5)
    hidden, saved = attention_forward(tokens, segments, params)
    queries, keys_low, values_low, softmax, softmax_low, context, summed = saved
    _, norm_back = jax.vjp(layer_norm, summed, to_full(attn_gain), to_full(attn_shift))
    summed_grad, gain_grad, shift_grad = norm_back(hidden_grad)
    branch_grad = to_low(summed_grad)
    out_bias_grad = jnp.sum(to_full(branch_grad), axis=0)
    out_weight_grad = matmul_tn(context, branch_grad)
    context_grad = to_low(matmul_nt(branch_grad, out_weight)).reshape(shaped)
    softmax_grad = jnp.einsum(
        "qhd,khd->hqk", context_grad, values_low, preferred_element_type=jnp.float32
    )
    value_grad = jnp.einsum(
        "hqk,qhd->khd", softmax_low, context_grad, preferred_element_type=jnp.float32
    )
    score_grad = to_low(
        softmax * (softmax_grad - jnp.sum(softmax * softmax_grad, axis=-1, keepdims=True))
    )
    query_grad = (
        jnp.einsum("hqk,khd->qhd", score_grad, keys_low, preferred_element_type=jnp.float32)
        * score_scale
    )
    key_grad = (
        jnp.einsum("hqk,qhd->khd", score_grad, queries, preferred_element_type=jnp.float32)
        * score_scale
    )
    mixed_grad = to_low(
        jnp.concatenate(
            [
                query_grad.reshape(row_count, model_width),
                key_grad.reshape(row_count, model_width),
                value_grad.reshape(row_count, model_width),
            ],
            axis=1,
        )
    )
    qkv_grad = matmul_tn(tokens, mixed_grad)
    mixed_full = to_full(mixed_grad)
    bias_grad = jnp.concatenate(
        [
            jnp.sum(mixed_full[:, :model_width], axis=0),
            jnp.sum(mixed_full[:, 2 * model_width :], axis=0),
        ]
    )
    tokens_grad = summed_grad + matmul_nt(mixed_grad, qkv_weight)
    return (
        tokens_grad,
        (qkv_grad, bias_grad, out_weight_grad, out_bias_grad, gain_grad, shift_grad),
    )


def ffn_forward(hidden, params):
    up_weight, up_bias, down_weight, down_bias, ffn_gain, ffn_shift = params
    pre_act = matmul(hidden, up_weight) + to_full(up_bias)
    active = to_low(gelu_exact(pre_act))
    summed = to_full(hidden) + matmul(active, down_weight) + to_full(down_bias)
    result = to_low(layer_norm(summed, to_full(ffn_gain), to_full(ffn_shift)))
    return (result, (pre_act, active, summed))


def ffn_backward(hidden, params, result_grad):
    up_weight, up_bias, down_weight, down_bias, ffn_gain, ffn_shift = params
    _, saved = ffn_forward(hidden, params)
    pre_act, active, summed = saved
    _, norm_back = jax.vjp(layer_norm, summed, to_full(ffn_gain), to_full(ffn_shift))
    summed_grad, gain_grad, shift_grad = norm_back(result_grad)
    branch_grad = to_low(summed_grad)
    down_bias_grad = jnp.sum(to_full(branch_grad), axis=0)
    down_weight_grad = matmul_tn(active, branch_grad)
    active_grad = matmul_nt(branch_grad, down_weight)
    _, gelu_back = jax.vjp(gelu_exact, pre_act)
    pre_grad = to_low(gelu_back(active_grad)[0])
    up_bias_grad = jnp.sum(to_full(pre_grad), axis=0)
    up_weight_grad = matmul_tn(hidden, pre_grad)
    hidden_grad = summed_grad + matmul_nt(pre_grad, up_weight)
    return (
        hidden_grad,
        (up_weight_grad, up_bias_grad, down_weight_grad, down_bias_grad, gain_grad, shift_grad),
    )


def merge_stats(first_part, second_part):
    higher = jnp.maximum(first_part[0], second_part[0])
    totals = first_part[1] * jnp.exp(first_part[0] - higher) + second_part[1] * jnp.exp(
        second_part[0] - higher
    )
    return (higher, totals, first_part[2] + second_part[2])


def per_device(
    tokens,
    segments,
    mask_flags,
    targets,
    cotangent,
    qkv_weight,
    attn_bias,
    out_weight,
    out_bias,
    attn_gain,
    attn_shift,
    up_weight,
    up_bias,
    down_weight,
    down_bias,
    ffn_gain,
    ffn_shift,
    dense_weight,
    dense_bias,
    head_gain,
    head_shift,
    decoder,
    vocab_bias,
):
    attn_params = (
        lax.all_gather(qkv_weight, ("dp", "fsdp"), axis=0, tiled=True),
        lax.all_gather(attn_bias, ("dp", "fsdp"), axis=0, tiled=True),
        lax.all_gather(out_weight, ("dp", "fsdp"), axis=0, tiled=True),
        lax.all_gather(out_bias, ("dp", "fsdp"), axis=0, tiled=True),
        lax.all_gather(attn_gain, ("dp", "fsdp"), axis=0, tiled=True),
        lax.all_gather(attn_shift, ("dp", "fsdp"), axis=0, tiled=True),
    )
    later_params = (
        lax.all_gather(up_weight, ("dp", "fsdp"), axis=0, tiled=True),
        lax.all_gather(up_bias, ("dp", "fsdp"), axis=0, tiled=True),
        lax.all_gather(down_weight, ("dp", "fsdp"), axis=0, tiled=True),
        lax.all_gather(down_bias, ("dp", "fsdp"), axis=0, tiled=True),
        lax.all_gather(ffn_gain, ("dp", "fsdp"), axis=0, tiled=True),
        lax.all_gather(ffn_shift, ("dp", "fsdp"), axis=0, tiled=True),
        lax.all_gather(dense_weight, ("dp", "fsdp"), axis=0, tiled=True),
        lax.all_gather(dense_bias, ("dp", "fsdp"), axis=0, tiled=True),
        lax.all_gather(head_gain, ("dp", "fsdp"), axis=0, tiled=True),
        lax.all_gather(head_shift, ("dp", "fsdp"), axis=0, tiled=True),
    )
    ffn_params = later_params[:6]
    dense_full, dense_bias_full, head_gain_full, head_shift_full = later_params[6:]
    hidden, _ = attention_forward(tokens, segments, attn_params)
    output, _ = ffn_forward(hidden, ffn_params)
    flagged = mask_flags > 0
    mask_rank = jnp.cumsum(mask_flags) - 1
    slot_place = jnp.where(flagged, mask_rank, -1)
    picker = jnp.arange(MAXM)[:, None] == slot_place[None, :]
    own_rows = to_low(matmul(picker.astype(jnp.bfloat16), output))
    own_labels = jnp.where(
        jnp.any(picker, axis=1), jnp.sum(jnp.where(picker, targets[None, :], 0), axis=1), -1
    )
    dense = matmul(own_rows, dense_full) + to_full(dense_bias_full)
    normed, tail_back = jax.vjp(head_tail, dense, to_full(head_gain_full), to_full(head_shift_full))
    normed_low = to_low(normed)
    devices = lax.axis_size(("dp", "fsdp"))
    slice_rows, slice_bias = (decoder, vocab_bias)
    all_rows, all_labels = (
        lax.all_gather(normed_low, ("dp", "fsdp"), axis=0, tiled=True),
        lax.all_gather(own_labels, ("dp", "fsdp"), axis=0, tiled=True),
    )
    slice_index = lax.axis_index(("dp", "fsdp"))
    vocab_rows = slice_rows.shape[0]
    logits = matmul_nt(all_rows, slice_rows) + to_full(slice_bias)
    row_peak = jnp.max(logits, axis=1)
    exp_sums = jnp.sum(jnp.exp(logits - row_peak[:, None]), axis=1)
    local_label = all_labels - slice_index * vocab_rows
    label_hit = jnp.arange(vocab_rows)[None, :] == local_label[:, None]
    label_logit = jnp.sum(jnp.where(label_hit, logits, 0.0), axis=1)
    peak_all, total_all, label_all = combined_all(
        (row_peak, exp_sums, label_logit), ("dp", "fsdp"), merge_stats
    )
    log_total = peak_all + jnp.log(total_all)
    row_weight = (all_labels >= 0).astype(jnp.float32)
    loss_here = jnp.sum(row_weight * (log_total - label_all))
    logit_grad = to_low(
        row_weight[:, None] * (jnp.exp(logits - log_total[:, None]) - label_hit.astype(jnp.float32))
    )
    decoder_part = matmul_tn(logit_grad, all_rows)
    vocab_bias_part = jnp.sum(to_full(logit_grad), axis=0)
    decoder_grad, vocab_bias_grad = (decoder_part, vocab_bias_part)
    mean_loss = loss_here / (MASK_DEV * devices)
    normed_grad = lax.psum_scatter(
        matmul(logit_grad, slice_rows), ("dp", "fsdp"), scatter_dimension=0, tiled=True
    )
    dense_grad, head_gain_grad, head_shift_grad = tail_back(normed_grad)
    dense_grad_low = to_low(dense_grad)
    dense_weight_grad = matmul_tn(own_rows, dense_grad_low)
    dense_bias_grad = jnp.sum(to_full(dense_grad_low), axis=0)
    picked_grad = to_low(matmul_nt(dense_grad_low, dense_full))
    head_grads = (
        lax.psum_scatter(dense_weight_grad, ("dp", "fsdp"), scatter_dimension=0, tiled=True),
        lax.psum_scatter(dense_bias_grad, ("dp", "fsdp"), scatter_dimension=0, tiled=True),
        lax.psum_scatter(head_gain_grad, ("dp", "fsdp"), scatter_dimension=0, tiled=True),
        lax.psum_scatter(head_shift_grad, ("dp", "fsdp"), scatter_dimension=0, tiled=True),
    )
    token_grad = matmul_tn(picker.astype(jnp.bfloat16), picked_grad)
    output_grad = to_full(cotangent) + token_grad
    ffn_back_params = (
        lax.all_gather(up_weight, ("dp", "fsdp"), axis=0, tiled=True),
        lax.all_gather(up_bias, ("dp", "fsdp"), axis=0, tiled=True),
        lax.all_gather(down_weight, ("dp", "fsdp"), axis=0, tiled=True),
        lax.all_gather(down_bias, ("dp", "fsdp"), axis=0, tiled=True),
        lax.all_gather(ffn_gain, ("dp", "fsdp"), axis=0, tiled=True),
        lax.all_gather(ffn_shift, ("dp", "fsdp"), axis=0, tiled=True),
    )
    hidden_grad, ffn_terms = ffn_backward(hidden, ffn_back_params, output_grad)
    ffn_grads = (
        lax.psum_scatter(ffn_terms[0], ("dp", "fsdp"), scatter_dimension=0, tiled=True),
        lax.psum_scatter(ffn_terms[1], ("dp", "fsdp"), scatter_dimension=0, tiled=True),
        lax.psum_scatter(ffn_terms[2], ("dp", "fsdp"), scatter_dimension=0, tiled=True),
        lax.psum_scatter(ffn_terms[3], ("dp", "fsdp"), scatter_dimension=0, tiled=True),
        lax.psum_scatter(ffn_terms[4], ("dp", "fsdp"), scatter_dimension=0, tiled=True),
        lax.psum_scatter(ffn_terms[5], ("dp", "fsdp"), scatter_dimension=0, tiled=True),
    )
    attn_back_params = (
        lax.all_gather(qkv_weight, ("dp", "fsdp"), axis=0, tiled=True),
        lax.all_gather(attn_bias, ("dp", "fsdp"), axis=0, tiled=True),
        lax.all_gather(out_weight, ("dp", "fsdp"), axis=0, tiled=True),
        lax.all_gather(out_bias, ("dp", "fsdp"), axis=0, tiled=True),
        lax.all_gather(attn_gain, ("dp", "fsdp"), axis=0, tiled=True),
        lax.all_gather(attn_shift, ("dp", "fsdp"), axis=0, tiled=True),
    )
    tokens_grad, attn_terms = attention_backward(tokens, segments, attn_back_params, hidden_grad)
    attn_grads = (
        lax.psum_scatter(attn_terms[0], ("dp", "fsdp"), scatter_dimension=0, tiled=True),
        lax.psum_scatter(attn_terms[1], ("dp", "fsdp"), scatter_dimension=0, tiled=True),
        lax.psum_scatter(attn_terms[2], ("dp", "fsdp"), scatter_dimension=0, tiled=True),
        lax.psum_scatter(attn_terms[3], ("dp", "fsdp"), scatter_dimension=0, tiled=True),
        lax.psum_scatter(attn_terms[4], ("dp", "fsdp"), scatter_dimension=0, tiled=True),
        lax.psum_scatter(attn_terms[5], ("dp", "fsdp"), scatter_dimension=0, tiled=True),
    )
    return (
        output,
        mean_loss,
        tokens_grad,
        attn_grads[0],
        attn_grads[1],
        attn_grads[2],
        attn_grads[3],
        attn_grads[4],
        attn_grads[5],
        ffn_grads[0],
        ffn_grads[1],
        ffn_grads[2],
        ffn_grads[3],
        ffn_grads[4],
        ffn_grads[5],
        head_grads[0],
        head_grads[1],
        head_grads[2],
        head_grads[3],
        decoder_grad,
        vocab_bias_grad,
    )


def solution(mesh):
    return jax.shard_map(
        per_device,
        mesh=mesh,
        in_specs=(
            P(("dp", "fsdp"), None),
            P(("dp", "fsdp")),
            P(("dp", "fsdp")),
            P(("dp", "fsdp")),
            P(("dp", "fsdp"), None),
            P(("dp", "fsdp"), None),
            P(("dp", "fsdp")),
            P(("dp", "fsdp"), None),
            P(("dp", "fsdp")),
            P(("dp", "fsdp")),
            P(("dp", "fsdp")),
            P(("dp", "fsdp"), None),
            P(("dp", "fsdp")),
            P(("dp", "fsdp"), None),
            P(("dp", "fsdp")),
            P(("dp", "fsdp")),
            P(("dp", "fsdp")),
            P(("dp", "fsdp"), None),
            P(("dp", "fsdp")),
            P(("dp", "fsdp")),
            P(("dp", "fsdp")),
            P(("dp", "fsdp"), None),
            P(("dp", "fsdp")),
        ),
        out_specs=(
            P(("dp", "fsdp"), None),
            P(),
            P(("dp", "fsdp"), None),
            P(("dp", "fsdp"), None),
            P(("dp", "fsdp")),
            P(("dp", "fsdp"), None),
            P(("dp", "fsdp")),
            P(("dp", "fsdp")),
            P(("dp", "fsdp")),
            P(("dp", "fsdp"), None),
            P(("dp", "fsdp")),
            P(("dp", "fsdp"), None),
            P(("dp", "fsdp")),
            P(("dp", "fsdp")),
            P(("dp", "fsdp")),
            P(("dp", "fsdp"), None),
            P(("dp", "fsdp")),
            P(("dp", "fsdp")),
            P(("dp", "fsdp")),
            P(("dp", "fsdp"), None),
            P(("dp", "fsdp")),
        ),
        check_vma=False,
    )
```

profile of v0, /device:TPU:0, one launch (start us, length us, event | category | flops | bytes accessed | tf_op | source)
XLA Modules:
  0.0 1437.2 jit_solution(5840770729632625287)
XLA Ops:
  19.9 42.8 %all-reduce.23 = (bf16[1536]{0:T(1024)(128)(2,1)S(1)}, bf16[768]{0:T(1024)(128)(2,1)S(1)}, bf16[768]{0:T(1024)(128)(2,1)S(1)}, bf16[768]{0:T(1024)(128)(2,1)S(1)...) all-reduce(bf16[1536]{0:T(1024)(128)(2,1)S(1)} %dynamic-update-slic, ...), channel_id=1, replica_groups=mesh['dp'=16,'fsdp'=2] {'dp','fsdp'}, use_global_device_ids=true, to_apply=%add | all-reduce | flops 11520 | bytes 46080
  102.1 27.7 %all-gather.13.cloned.1.call-done = bf16[768,768]{1,0:T(8,128)(2,1)} async-done(((bf16[24,768]{1,0:T(8,128)(2,1)}), bf16[768,768]{1,0:T(8,128)(2,1)}) %all-gather.13.cloned.1.call-update) | async-done | bytes 1179664 | tf_op jit(solution)/shard_map/all_gather | solution.py:213
  133.7 61.6 %all-gather.15.cloned.1.call-done = bf16[768,3072]{1,0:T(8,128)(2,1)} async-done(((bf16[24,3072]{1,0:T(8,128)(2,1)}), bf16[768,3072]{1,0:T(8,128)(2,1)}) %all-gather.15.cloned.1.call-update) | async-done | bytes 4718608 | tf_op jit(solution)/shard_map/all_gather | solution.py:219
  195.4 21.0 %multiply_convert_fusion.2 = (bf16[512,3072]{1,0:T(8,128)(2,1)}, f32[512,3072]{1,0:T(8,128)}, f32[512,3072]{1,0:T(8,128)}) fusion(f32[3072]{0:T(1024)S(1)} %convert_element_type.157, bf16[768,3072]{1,0:T(8,128)(2,1)} %all-gather.15.cloned.1.call-done, f32[512,768]{1,0:T(8,128)} %copy-done.7, f32[768]{0:T(1024)S(1)} %convert_element_type.154, ...), kind=kOutput, calls=%fused_computation.20 | convolution fusion | flops 2521694208 | bytes 22042624 | tf_op jit(solution)/shard_map/dot_general | solution.py:47
  216.3 44.3 %all-gather.17.cloned.1.call-done = bf16[3072,768]{1,0:T(8,128)(2,1)} async-done(((bf16[96,768]{1,0:T(8,128)(2,1)}), bf16[3072,768]{1,0:T(8,128)(2,1)}) %all-gather.17.cloned.1.call-update) | async-done | bytes 4718608 | tf_op jit(solution)/shard_map/all_gather | solution.py:221
  269.9 46.4 %all-gather.19.cloned.1.call-done = bf16[768,768]{1,0:T(8,128)(2,1)} async-done(((bf16[24,768]{1,0:T(8,128)(2,1)}), bf16[768,768]{1,0:T(8,128)(2,1)}) %all-gather.19.cloned.1.call-update) | async-done | bytes 1179664 | tf_op jit(solution)/shard_map/all_gather | solution.py:225
  320.8 39.3 %all-gather.3 = s32[32,1,128]{2,1,0:T(1,128)S(1)} all-gather(s32[1,1,128]{2,1,0:T(1,128)S(1)} %select_bitcast_fusion), channel_id=1, replica_groups=mesh['dp'=16,'fsdp'=2] {'dp','fsdp'}, dimensions={0}, use_global_device_ids=true | all-gather | bytes 16896 | tf_op jit(solution)/shard_map/all_gather | solution.py:249
  360.7 28.3 %all-gather.21.cloned.1.call-done = bf16[4096,768]{1,0:T(8,128)(2,1)} async-done(((bf16[128,768]{1,0:T(8,128)(2,1)}), bf16[4096,768]{1,0:T(8,128)(2,1)}) %all-gather.21.cloned.1.call-update) | async-done | bytes 6291472 | tf_op jit(solution)/shard_map/all_gather | solution.py:248
  389.0 16.3 %add_reduce_fusion = (f32[4096]{0:T(1024)S(1)}, f32[4096,1568]{0,1:T(8,128)}) fusion(f32[1568]{0:T(1024)S(1)} %convert_element_type.168, bf16[4096,768]{1,0:T(8,128)(2,1)} %all-gather.21.cloned.1.call-done, bf16[1568,768]{1,0:T(8,128)(2,1)S(1)} %copy-done), kind=kOutput, calls=%fused_computation.10 | convolution fusion | flops 9877843968 | bytes 34412672 | tf_op jit(solution)/shard_map/dot_general | solution.py:57
  405.4 40.5 %all-gather = f32[131072]{0:T(1024)S(1)} all-gather(f32[4096]{0:T(1024)S(1)} %get-tuple-element.236), channel_id=2, replica_groups=mesh['dp'=16,'fsdp'=2] {'dp','fsdp'}, dimensions={0}, use_global_device_ids=true | all-gather | bytes 540672 | tf_op jit(solution)/shard_map/all_gather | solution.py:17
  446.8 13.0 select_reduce_fusion
  459.8 38.1 %all-gather.1 = f32[131072]{0:T(1024)S(1)} all-gather(f32[4096]{0:T(1024)S(1)} %get-tuple-element.148), channel_id=3, replica_groups=mesh['dp'=16,'fsdp'=2] {'dp','fsdp'}, dimensions={0}, use_global_device_ids=true | all-gather | bytes 540672 | tf_op jit(solution)/shard_map/all_gather | solution.py:17
  497.9 39.5 %all-gather.2 = f32[131072]{0:T(1024)S(1)} all-gather(f32[4096]{0:T(1024)S(1)} %get-tuple-element.147), channel_id=4, replica_groups=mesh['dp'=16,'fsdp'=2] {'dp','fsdp'}, dimensions={0}, use_global_device_ids=true | all-gather | bytes 540672 | tf_op jit(solution)/shard_map/all_gather | solution.py:17
  543.0 61.4 %while.14 = (s32[]{:T(128)}, f32[4096]{0:T(1024)S(1)}, f32[4096]{0:T(1024)S(1)}, f32[4096]{0:T(1024)S(1)}, f32[31,4096]{1,0:T(8,128)}, /*index=5*/f32[31,4096]{1,0:T(8,128)}, f32[31,4096]{1,0:T(8,128)}, s32[]{:T(128)}) while((s32[]{:T(128)}, f32[4096]{0:T(1024)S(1)}, f32[4096]{0:T(1024)S(1)}, f32[4096]{0:T(1024)S(1)}, ...), condition=%wide.region_16.17_spmd, body=%wide.region_15.16_spmd.sunk | while | flops 28674 | bytes 245861 | solution.py:20
  605.7 14.9 %convert_reduce_fusion = (f32[1568]{0:T(1024)}, bf16[4096,1568]{0,1:T(8,128)(2,1)S(1)}) fusion(s32[4096]{0:T(1024)} %bitcast.110, f32[4096]{0:T(1024)S(1)} %get-tuple-element.216, f32[4096,1568]{0,1:T(8,128)} %get-tuple-element.237, f32[1568]{0:T(1024)} %copy-done.27, f32[4096]{0:T(1024)} %get-tuple-element.213), kind=kLoop, calls=%fused_computation.5 | loop fusion | flops 57801184 | bytes 38596864 | tf_op jit(solution)/shard_map/reduce_sum | solution.py:269
  625.2 14.7 %fusion.53 = f32[4096,768]{1,0:T(8,128)} fusion(bf16[4096,1568]{0,1:T(8,128)(2,1)S(1)} %get-tuple-element.200, bf16[1568,768]{1,0:T(8,128)(2,1)S(1)} %copy-done), kind=kOutput, calls=%fused_computation.146 | convolution fusion | flops 9865003008 | bytes 27836416 | tf_op jit(solution)/shard_map/dot_general | solution.py:47
  640.1 151.6 %reduce-scatter.9.cloned.1.call-done = f32[128,768]{1,0:T(8,128)} async-done(((f32[4096,768]{1,0:T(8,128)}), f32[128,768]{1,0:T(8,128)}) %reduce-scatter.9.cloned.1.call-update) | async-done | bytes 393232 | tf_op jit(solution)/shard_map/reduce_scatter | solution.py:272
  833.8 12.3 multiply_convert_fusion.1
  882.6 16.9 %fusion.57 = f32[1568,768]{1,0:T(8,128)} fusion(bf16[4096,1568]{0,1:T(8,128)(2,1)} %copy-done.4, bf16[4096,768]{1,0:T(8,128)(2,1)} %all-gather.21.cloned.1.call-done), kind=kOutput, calls=%fused_computation.150 | convolution fusion | flops 9865003008 | bytes 23953408 | tf_op jit(solution)/shard_map/dot_general | solution.py:51
  900.5 41.1 %all-reduce.22 = (f32[1536]{0:T(1024)S(1)}, f32[768]{0:T(1024)S(1)}, f32[768]{0:T(1024)S(1)}, f32[768]{0:T(1024)S(1)}, f32[3072]{0:T(1024)S(1)}, /*index=5*/f32[...) all-reduce(f32[1536]{0:T(1024)S(1)} %pad_maximum_fusion.1, ...), channel_id=7, replica_groups=mesh['dp'=16,'fsdp'=2] {'dp','fsdp'}, use_global_device_ids=true, to_apply=%region_29.30.clone | all-reduce | flops 11520 | bytes 92160
  954.4 66.2 %reduce-scatter.17.cloned.1.call-done = f32[24,768]{1,0:T(8,128)} async-done(((f32[768,768]{1,0:T(8,128)}), f32[24,768]{1,0:T(8,128)}) %reduce-scatter.17.cloned.1.call-update) | async-done | bytes 73744 | tf_op jit(solution)/shard_map/reduce_scatter | solution.py:281
  1020.6 125.2 %reduce-scatter.19.cloned.1.call-done = f32[24,2304]{1,0:T(8,128)} async-done(((f32[768,2304]{1,0:T(8,128)}), f32[24,2304]{1,0:T(8,128)}) %reduce-scatter.19.cloned.1.call-update) | async-done | bytes 221200
  1145.9 141.2 %reduce-scatter.13.cloned.1.call-done = f32[24,3072]{1,0:T(8,128)} async-done(((f32[768,3072]{1,0:T(8,128)}), f32[24,3072]{1,0:T(8,128)}) %reduce-scatter.13.cloned.1.call-update) | async-done | bytes 294928 | tf_op jit(solution)/shard_map/reduce_scatter | solution.py:298
  1287.1 141.9 %reduce-scatter.15.cloned.1.call-done = f32[96,768]{1,0:T(8,128)} async-done(((f32[3072,768]{1,0:T(8,128)}), f32[96,768]{1,0:T(8,128)}) %reduce-scatter.15.cloned.1.call-update) | async-done | bytes 294928 | tf_op jit(solution)/shard_map/reduce_scatter | solution.py:300
  (412 shorter events, 234.1 us)
Async XLA Ops:
  7.2 381.8 %copy-start = (bf16[1568,768]{1,0:T(8,128)(2,1)S(1)}, bf16[1568,768]{1,0:T(8,128)(2,1)}, u32[]{:S(2)}) copy-start(bf16[1568,768]{1,0:T(8,128)(2,1)} %param.46) | copy-start | bytes 7225348
  7.2 66.9 %all-gather.11.cloned.1.call-start = ((), (), s32[]{:S(2)}) async-start(), calls=%async_computation.6 | async-start | bytes 3649536 | tf_op jit(solution)/shard_map/all_gather | solution.py:211
  7.9 121.9 %all-gather.13.cloned.1.call-start = ((), (), s32[]{:S(2)}) async-start(), calls=%async_computation.7 | async-start | bytes 1216512 | tf_op jit(solution)/shard_map/all_gather | solution.py:213
  8.7 186.7 %all-gather.15.cloned.1.call-start = ((), (), s32[]{:S(2)}) async-start(), calls=%async_computation.8 | async-start | bytes 4866048 | tf_op jit(solution)/shard_map/all_gather | solution.py:219
  9.4 251.2 %all-gather.17.cloned.1.call-start = ((), (), s32[]{:S(2)}) async-start(), calls=%async_computation.9 | async-start | bytes 4866048 | tf_op jit(solution)/shard_map/all_gather | solution.py:221
  10.0 306.2 %all-gather.19.cloned.1.call-start = ((), (), s32[]{:S(2)}) async-start(), calls=%async_computation.10 | async-start | bytes 1216512 | tf_op jit(solution)/shard_map/all_gather | solution.py:225
  10.6 378.4 %all-gather.21.cloned.1.call-start = ((), (), s32[]{:S(2)}) async-start(), calls=%async_computation.11 | async-start | bytes 6488064 | tf_op jit(solution)/shard_map/all_gather | solution.py:248
  63.7 196.9 %copy-start.56 = (f32[768]{0:T(1024)}, f32[768]{0:T(1024)S(1)}, u32[]{:S(2)}) copy-start(f32[768]{0:T(1024)S(1)} %convert_element_type.154) | copy-start | bytes 9220
  63.8 196.9 %copy-start.45 = (f32[768]{0:T(1024)}, f32[768]{0:T(1024)S(1)}, u32[]{:S(2)}) copy-start(f32[768]{0:T(1024)S(1)} %convert_element_type.153) | copy-start | bytes 9220
  63.8 203.7 %copy-start.28 = (f32[768]{0:T(1024)}, f32[768]{0:T(1024)S(1)}, u32[]{:S(2)}) copy-start(f32[768]{0:T(1024)S(1)} %convert_element_type.160) | copy-start | bytes 9220
  320.5 471.2 %reduce-scatter.9.cloned.1.call-start = ((), (), s32[]{:S(2)}) async-start(), calls=%async_computation.12 | async-start | bytes 12976128 | tf_op jit(solution)/shard_map/reduce_scatter | solution.py:272
  639.9 155.8 %copy-start.3 = (f32[512,768]{1,0:T(8,128)S(1)}, f32[512,768]{1,0:T(8,128)}, u32[]{:S(2)}) copy-start(f32[512,768]{1,0:T(8,128)} %copy-done.2) | copy-start | bytes 4718596
  639.9 155.8 %copy-start.15 = (bf16[512,768]{1,0:T(8,128)(2,1)S(1)}, bf16[512,768]{1,0:T(8,128)(2,1)}, u32[]{:S(2)}) copy-start(bf16[512,768]{1,0:T(8,128)(2,1)} %param.29) | copy-start | bytes 2359300
  640.0 155.8 %copy-start.29 = (f32[768]{0:T(1024)S(1)}, f32[768]{0:T(1024)}, u32[]{:S(2)}) copy-start(f32[768]{0:T(1024)} %copy-done.28) | copy-start | bytes 9220
  640.0 155.8 %copy-start.31 = (f32[512]{0:T(512)S(1)}, f32[512]{0:T(512)}, u32[]{:S(2)}) copy-start(f32[512]{0:T(512)} %copy-done.30) | copy-start | bytes 6148
  640.0 155.8 %copy-start.33 = (s32[512]{0:T(512)S(1)}, s32[512]{0:T(512)}, u32[]{:S(2)}) copy-start(s32[512]{0:T(512)} %bitcast_select_fusion) | copy-start | bytes 6148
  640.0 155.8 %copy-start.35 = (f32[512]{0:T(512)S(1)}, f32[512]{0:T(512)}, u32[]{:S(2)}) copy-start(f32[512]{0:T(512)} %copy-done.34) | copy-start | bytes 6148
  640.0 159.3 %copy-start.43 = (f32[512]{0:T(512)S(1)}, f32[512]{0:T(512)}, u32[]{:S(2)}) copy-start(f32[512]{0:T(512)} %copy-done.42) | copy-start | bytes 6148
  640.0 314.4 %reduce-scatter.11.cloned.1.call-start = ((), (), s32[]{:S(2)}) async-start(), calls=%async_computation.13 | async-start | bytes 2433024 | tf_op jit(solution)/shard_map/reduce_scatter | solution.py:317
  818.3 202.3 %reduce-scatter.17.cloned.1.call-start = ((), (), s32[]{:S(2)}) async-start(), calls=%async_computation.16 | async-start | bytes 2433024 | tf_op jit(solution)/shard_map/reduce_scatter | solution.py:281
  833.7 312.2 %reduce-scatter.19.cloned.1.call-start = ((), (), s32[]{:S(2)}) async-start(), calls=%async_computation.17 | async-start | bytes 7299072
  864.6 422.4 %reduce-scatter.13.cloned.1.call-start = ((), (), s32[]{:S(2)}) async-start(), calls=%async_computation.14 | async-start | bytes 9732096 | tf_op jit(solution)/shard_map/reduce_scatter | solution.py:298
  872.6 556.4 %reduce-scatter.15.cloned.1.call-start = ((), (), s32[]{:S(2)}) async-start(), calls=%async_computation.15 | async-start | bytes 9732096 | tf_op jit(solution)/shard_map/reduce_scatter | solution.py:300
  947.4 481.6 %copy-start.1 = (bf16[1568,768]{1,0:T(8,128)(2,1)S(1)}, bf16[1568,768]{1,0:T(8,128)(2,1)}, u32[]{:S(2)}) copy-start(bf16[1568,768]{1,0:T(8,128)(2,1)} %param.46) | copy-start | bytes 7225348
  (58 other events, 2299.2 us)
Sparse Core Ops, SparseCore 0:
  10.9 63.1 all-gather.10
  77.0 52.8 all-gather.12
  132.7 62.5 all-gather.14
  198.1 62.4 all-gather.16
  263.4 52.8 all-gather.18
  320.6 68.3 all-gather.20
  640.1 151.5 reduce-scatter.8
  818.4 98.2 reduce-scatter.10
  922.6 98.0 reduce-scatter.16
  1027.7 118.1 reduce-scatter.18
  1152.3 134.6 reduce-scatter.12
  1294.4 134.5 reduce-scatter.14
where the time goes:
time: 1440 us
  waiting for transfers between devices  844 us (59%)
  blocking collectives  241 us (17%)
  matrix products  166 us (12%)
  local copies, waits for them, and re-layouts  108 us (8%)
  other arithmetic  59.6 us (4%)
  between operations  17.3 us (1%)
    reduce_scatter x1, waiting for transfers between devices, per_device(): lax.psum_scatter(matmul(logit_grad, slice_rows), ('dp', 'fsdp'), scatter_...  152 us
    reduce_scatter x1, waiting for transfers between devices, per_device(): lax.psum_scatter(ffn_terms[2], ('dp', 'fsdp'), scatter_dimension=0, tiled...  142 us
    reduce_scatter x1, waiting for transfers between devices, per_device(): lax.psum_scatter(ffn_terms[0], ('dp', 'fsdp'), scatter_dimension=0, tiled...  141 us
    unnamed x13, waiting for transfers between devices  128 us
    all_gather x3, blocking collectives, combined_all(): pieces = jax.tree.map(lambda part: lax.all_gather(part, axis), value)  118 us
    unnamed x2, blocking collectives  84 us
    reduce_scatter x1, waiting for transfers between devices, per_device(): lax.psum_scatter(dense_weight_grad, ('dp', 'fsdp'), scatter_dimension=0,...  66.2 us
    all_gather x1, waiting for transfers between devices, per_device(): lax.all_gather(up_weight, ('dp', 'fsdp'), axis=0, tiled=True)  61.6 us
  transfers between devices with their start and end apart: 12, of which 11 were waited for; matrix products, arithmetic and copies ran while one was open for 12% of the time, Pallas kernels for 0%

commit v1 on v0

v1 whole, which is shorter than its diff:
```python
import jax
import jax.numpy as jnp
from jax import lax
from jax.sharding import PartitionSpec as P

HEADS = 12
HEAD_DIM = 64
MASK_DEV = 64
MAXM = 128

EPSILON = 1e-05
NEGATIVE = -1e30
AXES = ("dp", "fsdp")


def to_low(values):
    return values.astype(jnp.bfloat16)


def to_full(values):
    return values.astype(jnp.float32)


def layer_norm(values, gain_vector, shift_vector):
    center = values - jnp.mean(values, axis=-1, keepdims=True)
    spread = jnp.mean(center * center, axis=-1, keepdims=True)
    return center * lax.rsqrt(spread + EPSILON) * gain_vector + shift_vector


def gelu_exact(values):
    return jax.nn.gelu(values, approximate=False)


def head_tail(dense_out, gain_vector, shift_vector):
    return layer_norm(gelu_exact(dense_out), gain_vector, shift_vector)


def matmul(left_side, right_side):
    return jnp.dot(left_side, right_side, preferred_element_type=jnp.float32)


def matmul_tn(left_side, right_side):
    return lax.dot_general(
        left_side, right_side, (((0,), (0,)), ((), ())), preferred_element_type=jnp.float32
    )


def matmul_nt(left_side, right_side):
    return lax.dot_general(
        left_side, right_side, (((1,), (1,)), ((), ())), preferred_element_type=jnp.float32
    )


def attention_forward(tokens, segments, params):
    qkv_weight, attn_bias, out_weight, out_bias, attn_gain, attn_shift = params
    row_count, model_width = tokens.shape
    shaped = (row_count, HEADS, HEAD_DIM)
    score_scale = HEAD_DIM ** (-0.5)
    bias_full = to_full(attn_bias)
    queries = to_low(matmul(tokens, qkv_weight[0]) + bias_full[:model_width]).reshape(shaped)
    keys_low = to_low(matmul(tokens, qkv_weight[1])).reshape(shaped)
    values_low = to_low(matmul(tokens, qkv_weight[2]) + bias_full[model_width:]).reshape(shaped)
    scores = (
        jnp.einsum("qhd,khd->hqk", queries, keys_low, preferred_element_type=jnp.float32)
        * score_scale
    )
    same_doc = segments[:, None] == segments[None, :]
    scores = jnp.where(same_doc[None], scores, NEGATIVE)
    row_peak = jnp.max(scores, axis=-1, keepdims=True)
    exponent = jnp.exp(scores - row_peak)
    softmax = exponent / jnp.sum(exponent, axis=-1, keepdims=True)
    softmax_low = to_low(softmax)
    context = to_low(
        jnp.einsum(
            "hqk,khd->qhd", softmax_low, values_low, preferred_element_type=jnp.float32
        ).reshape(row_count, model_width)
    )
    summed = to_full(tokens) + matmul(context, out_weight) + to_full(out_bias)
    hidden = to_low(layer_norm(summed, to_full(attn_gain), to_full(attn_shift)))
    return (hidden, (queries, keys_low, values_low, softmax, softmax_low, context, summed))


def attention_backward(tokens, params, saved, hidden_grad):
    qkv_weight, attn_bias, out_weight, out_bias, attn_gain, attn_shift = params
    row_count, model_width = tokens.shape
    shaped = (row_count, HEADS, HEAD_DIM)
    score_scale = HEAD_DIM ** (-0.5)
    queries, keys_low, values_low, softmax, softmax_low, context, summed = saved
    _, norm_back = jax.vjp(layer_norm, summed, to_full(attn_gain), to_full(attn_shift))
    summed_grad, gain_grad, shift_grad = norm_back(hidden_grad)
    branch_grad = to_low(summed_grad)
    out_bias_grad = jnp.sum(to_full(branch_grad), axis=0)
    out_weight_grad = matmul_tn(context, branch_grad)
    context_grad = to_low(matmul_nt(branch_grad, out_weight)).reshape(shaped)
    softmax_grad = jnp.einsum(
        "qhd,khd->hqk", context_grad, values_low, preferred_element_type=jnp.float32
    )
    value_grad = jnp.einsum(
        "hqk,qhd->khd", softmax_low, context_grad, preferred_element_type=jnp.float32
    )
    score_grad = to_low(
        softmax * (softmax_grad - jnp.sum(softmax * softmax_grad, axis=-1, keepdims=True))
    )
    query_grad = (
        jnp.einsum("hqk,khd->qhd", score_grad, keys_low, preferred_element_type=jnp.float32)
        * score_scale
    )
    key_grad = (
        jnp.einsum("hqk,qhd->khd", score_grad, queries, preferred_element_type=jnp.float32)
        * score_scale
    )
    parts = [
        to_low(part.reshape(row_count, model_width)) for part in (query_grad, key_grad, value_grad)
    ]
    qkv_grad = [matmul_tn(tokens, part) for part in parts]
    bias_grad = jnp.concatenate(
        [jnp.sum(to_full(parts[0]), axis=0), jnp.sum(to_full(parts[2]), axis=0)]
    )
    tokens_grad = summed_grad
    for part, weight in zip(parts, qkv_weight):
        tokens_grad = tokens_grad + matmul_nt(part, weight)
    return (
        tokens_grad,
        (qkv_grad, bias_grad, out_weight_grad, out_bias_grad, gain_grad, shift_grad),
    )


def ffn_forward(hidden, params):
    up_weight, up_bias, down_weight, down_bias, ffn_gain, ffn_shift = params
    pre_act = matmul(hidden, up_weight) + to_full(up_bias)
    active = to_low(gelu_exact(pre_act))
    summed = to_full(hidden) + matmul(active, down_weight) + to_full(down_bias)
    result = to_low(layer_norm(summed, to_full(ffn_gain), to_full(ffn_shift)))
    return (result, (pre_act, active, summed))


def ffn_backward(hidden, params, saved, result_grad):
    up_weight, up_bias, down_weight, down_bias, ffn_gain, ffn_shift = params
    pre_act, active, summed = saved
    _, norm_back = jax.vjp(layer_norm, summed, to_full(ffn_gain), to_full(ffn_shift))
    summed_grad, gain_grad, shift_grad = norm_back(result_grad)
    branch_grad = to_low(summed_grad)
    down_bias_grad = jnp.sum(to_full(branch_grad), axis=0)
    down_weight_grad = matmul_tn(active, branch_grad)
    active_grad = matmul_nt(branch_grad, down_weight)
    _, gelu_back = jax.vjp(gelu_exact, pre_act)
    pre_grad = to_low(gelu_back(active_grad)[0])
    up_bias_grad = jnp.sum(to_full(pre_grad), axis=0)
    up_weight_grad = matmul_tn(hidden, pre_grad)
    hidden_grad = summed_grad + matmul_nt(pre_grad, up_weight)
    return (
        hidden_grad,
        (up_weight_grad, up_bias_grad, down_weight_grad, down_bias_grad, gain_grad, shift_grad),
    )


def column_blocks(matrix, width):
    return [matrix[:, k : k + width] for k in range(0, matrix.shape[1], width)]


def butterfly(value, join, count):
    index = 1
    while index < count:
        pairs = [(device, device ^ index) for device in range(count)]
        value = join(value, lax.ppermute(value, AXES, pairs))
        index *= 2
    return value


def pack_small(parts, count, width):
    flat = jnp.concatenate([part.reshape(count, -1) for part in parts], axis=1)
    flat = jnp.pad(flat, ((0, 0), (0, width - flat.shape[1])))
    return jnp.pad(flat[:, None, :], ((0, 0), (0, 7), (0, 0)))


def per_device(
    tokens,
    segments,
    mask_flags,
    targets,
    cotangent,
    qkv_weight,
    attn_bias,
    out_weight,
    out_bias,
    attn_gain,
    attn_shift,
    up_weight,
    up_bias,
    down_weight,
    down_bias,
    ffn_gain,
    ffn_shift,
    dense_weight,
    dense_bias,
    head_gain,
    head_shift,
    decoder,
    vocab_bias,
):
    count = lax.axis_size(AXES)
    width = tokens.shape[1]
    small = (
        attn_bias,
        out_bias,
        attn_gain,
        attn_shift,
        up_bias,
        down_bias,
        ffn_gain,
        ffn_shift,
        dense_bias,
        head_gain,
        head_shift,
    )
    qkv_blocks = column_blocks(qkv_weight, width)
    up_blocks = column_blocks(up_weight, width)
    matrices = [*qkv_blocks, out_weight, *up_blocks, down_weight, dense_weight]
    packed = jnp.concatenate([*matrices, pack_small(small, 1, width)[0]], axis=0)
    gathered = lax.all_gather(packed, AXES, axis=0)
    full = []
    offset = 0
    for matrix in matrices:
        rows = matrix.shape[0]
        full.append(gathered[:, offset : offset + rows].reshape(count * rows, width))
        offset += rows
    small_full = []
    start = 0
    for vector in small:
        share = vector.shape[0]
        small_full.append(gathered[:, offset, start : start + share].reshape(count * share))
        start += share
    blocks = len(qkv_blocks)
    qkv_full = full[:blocks]
    out_full = full[blocks]
    up_full = jnp.concatenate(full[blocks + 1 : blocks + 1 + len(up_blocks)], axis=1)
    down_full, dense_full = full[-2:]
    attn_params = (qkv_full, small_full[0], out_full, *small_full[1:4])
    ffn_params = (up_full, small_full[4], down_full, *small_full[5:8])
    dense_bias_full, head_gain_full, head_shift_full = small_full[8:]

    hidden, attn_saved = attention_forward(tokens, segments, attn_params)
    output, ffn_saved = ffn_forward(hidden, ffn_params)
    flagged = mask_flags > 0
    mask_rank = jnp.cumsum(mask_flags) - 1
    slot_place = jnp.where(flagged, mask_rank, -1)
    picker = jnp.arange(MAXM)[:, None] == slot_place[None, :]
    picker_low = picker.astype(jnp.bfloat16)
    own_rows = to_low(matmul(picker_low, output))
    own_labels = jnp.where(
        jnp.any(picker, axis=1), jnp.sum(jnp.where(picker, targets[None, :], 0), axis=1), -1
    )
    dense = matmul(own_rows, dense_full) + to_full(dense_bias_full)
    normed, tail_back = jax.vjp(head_tail, dense, to_full(head_gain_full), to_full(head_shift_full))
    normed_low = to_low(normed)
    shifted = own_labels + 1
    label_rows = jnp.stack([shifted // 256, shifted % 256]).astype(jnp.bfloat16)
    label_rows = jnp.pad(label_rows, ((0, 6), (0, width - MAXM)))
    rows_gathered = lax.all_gather(jnp.concatenate([normed_low, label_rows]), AXES, axis=0)
    all_rows = rows_gathered[:, :MAXM].reshape(count * MAXM, width)
    label_parts = rows_gathered[:, MAXM : MAXM + 2, :MAXM].astype(jnp.int32)
    all_labels = (label_parts[:, 0] * 256 + label_parts[:, 1] - 1).reshape(count * MAXM)
    slice_index = lax.axis_index(AXES)
    vocab_rows = decoder.shape[0]
    logits = matmul_nt(all_rows, decoder) + to_full(vocab_bias)
    row_peak = jnp.max(logits, axis=1)
    exp_sums = jnp.sum(jnp.exp(logits - row_peak[:, None]), axis=1)
    local_label = all_labels - slice_index * vocab_rows
    row_valid = all_labels >= 0
    label_hit = (jnp.arange(vocab_rows)[None, :] == local_label[:, None]) & row_valid[:, None]
    label_sum = jnp.sum(jnp.where(label_hit, logits, 0.0))
    local_total = (row_peak + jnp.log(exp_sums)).reshape(count, MAXM)
    stats = jnp.concatenate(
        [local_total, jnp.pad(label_sum[None, None], ((0, 7), (0, MAXM - 1)))], axis=0
    )

    def join(first, second):
        merged = jnp.maximum(first, second) + jnp.log1p(jnp.exp(-jnp.abs(first - second)))
        is_total = jnp.arange(first.shape[0])[:, None] < count
        return jnp.where(is_total, merged, first + second)

    stats = butterfly(stats, join, count)
    log_total = stats[:count].reshape(count * MAXM)
    row_weight = row_valid.astype(jnp.float32)
    mean_loss = (jnp.sum(row_weight * log_total) - stats[count, 0]) / (MASK_DEV * count)
    logit_grad = to_low(
        row_weight[:, None] * (jnp.exp(logits - log_total[:, None]) - label_hit.astype(jnp.float32))
    )
    rows_part = to_low(matmul(logit_grad, decoder))
    normed_grad = to_full(lax.psum_scatter(rows_part, AXES, scatter_dimension=0, tiled=True))
    decoder_grad = matmul_tn(logit_grad, all_rows)
    vocab_bias_grad = jnp.sum(to_full(logit_grad), axis=0)
    dense_grad, head_gain_grad, head_shift_grad = tail_back(normed_grad)
    dense_grad_low = to_low(dense_grad)
    dense_weight_grad = matmul_tn(own_rows, dense_grad_low)
    dense_bias_grad = jnp.sum(to_full(dense_grad_low), axis=0)
    picked_grad = to_low(matmul_nt(dense_grad_low, dense_full))
    token_grad = matmul_tn(picker_low, picked_grad)
    output_grad = to_full(cotangent) + token_grad
    hidden_grad, ffn_terms = ffn_backward(hidden, ffn_params, ffn_saved, output_grad)
    tokens_grad, attn_terms = attention_backward(tokens, attn_params, attn_saved, hidden_grad)

    small_grads = (
        *(attn_terms[k] for k in (1, 3, 4, 5)),
        *(ffn_terms[k] for k in (1, 3, 4, 5)),
        dense_bias_grad,
        head_gain_grad,
        head_shift_grad,
    )
    grad_matrices = [
        *attn_terms[0],
        attn_terms[2],
        *column_blocks(ffn_terms[0], width),
        ffn_terms[2],
        dense_weight_grad,
    ]
    grads_packed = jnp.concatenate(
        [to_low(matrix).reshape(count, -1, width) for matrix in grad_matrices]
        + [to_low(pack_small(small_grads, count, width))],
        axis=1,
    )
    grads = to_full(lax.psum_scatter(grads_packed, AXES, scatter_dimension=0, tiled=True)[0])
    pieces = []
    offset = 0
    for matrix in matrices:
        pieces.append(grads[offset : offset + matrix.shape[0]])
        offset += matrix.shape[0]
    small_pieces = []
    start = 0
    for vector in small:
        small_pieces.append(grads[offset, start : start + vector.shape[0]])
        start += vector.shape[0]
    return (
        output,
        mean_loss,
        tokens_grad,
        jnp.concatenate(pieces[:blocks], axis=1),
        small_pieces[0],
        pieces[blocks],
        *small_pieces[1:4],
        jnp.concatenate(pieces[blocks + 1 : blocks + 1 + len(up_blocks)], axis=1),
        small_pieces[4],
        pieces[-2],
        *small_pieces[5:8],
        pieces[-1],
        *small_pieces[8:],
        decoder_grad,
        vocab_bias_grad,
    )


def solution(mesh):
    matrix_spec = P(AXES, None)
    vector_spec = P(AXES)
    m, v = matrix_spec, vector_spec
    return jax.shard_map(
        per_device,
        mesh=mesh,
        in_specs=(m, v, v, v, m, m, v, m, v, v, v, m, v, m, v, v, v, m, v, v, v, m, v),
        out_specs=(m, P(), m, m, v, m, v, v, v, m, v, m, v, v, v, m, v, v, v, m, v),
        check_vma=False,
    )
```

time: 1440 us -> 764 us (0.53)
  waiting for transfers between devices: 844 us -> 449 us
  blocking collectives: 241 us -> 0 us
  local copies, waits for them, and re-layouts: 108 us -> 62 us
    reduce_scatter x5 -> x2, waiting for transfers between devices: 501 us -> 260 us  [the longest x1 147 us: per_device(): lax.psum_scatter(grads_packed, AXES, scatter_dimension=0, tiled=True)[0]]
    all_gather x4 -> x0, blocking collectives: 157 us -> none  [the longest x3 118 us: combined_all(): pieces = jax.tree.map(lambda part: lax.all_gather(part, axis), value)]
    unnamed x13 -> x4, waiting for transfers between devices: 128 us -> 0.07 us
    unnamed x2 -> x0, blocking collectives: 84 us -> none
    dynamic_slice x62 -> x0, local copies, waits for them, and re-layouts: 59.6 us -> none  [combined_all(): lax.scan(lambda subtotal, slab: (join(subtotal, slab), None), head, tail)]
    all_gather x6 -> x2, waiting for transfers between devices: 214 us -> 178 us  [the longest x1 109 us: per_device(): gathered = lax.all_gather(packed, AXES, axis=0)]
    slice x13 -> x11, local copies, waits for them, and re-layouts: 8.96 us -> 24.4 us  [the longest x2 12.7 us: per_device(): full.append(gathered[:, offset:offset + rows].reshape(count * rows, width))]
    dot_general x7 -> x9, matrix products: 44.8 us -> 40.5 us  [matmul_tn(): lax.dot_general(left_side, right_side, (((0,), (0,)), ((), ())), preferre...]
  transfers between devices with their start and end apart: 12 -> 9, of which waited for: 11 -> 9; matrix products, arithmetic and copies ran while one was open for 12% -> 3% of each run, Pallas kernels for 0% -> 0%
where the time goes in v1:
time: 764 us; the launch traced here: 760 us
  waiting for transfers between devices  449 us (59%)
  matrix products  167 us (22%)
  local copies, waits for them, and re-layouts  62 us (8%)
  other arithmetic  57.4 us (8%)
  between operations  17.6 us (2%)
    reduce_scatter x1, waiting for transfers between devices, per_device(): lax.psum_scatter(grads_packed, AXES, scatter_dimension=0, tiled=True)[0]  147 us
    reduce_scatter x1, waiting for transfers between devices, per_device(): lax.psum_scatter(rows_part, AXES, scatter_dimension=0, tiled=True)  113 us
    all_gather x1, waiting for transfers between devices, per_device(): gathered = lax.all_gather(packed, AXES, axis=0)  109 us
    all_gather x1, waiting for transfers between devices, per_device(): lax.all_gather(jnp.concatenate([normed_low, label_rows]), AXES, axis=0)  69.4 us
    dot_general x9, matrix products, matmul(): return jnp.dot(left_side, right_side, preferred_element_type=jnp.float32)  49 us
    dot_general x7, matrix products, matmul_nt(): lax.dot_general(left_side, right_side, (((1,), (1,)), ((), ())), preferre...  40.5 us
    dot_general x9, matrix products, matmul_tn(): lax.dot_general(left_side, right_side, (((0,), (0,)), ((), ())), preferre...  40.5 us
    unnamed x169, local copies, waits for them, and re-layouts  30.2 us
  transfers between devices with their start and end apart: 9, of which 9 were waited for; matrix products, arithmetic and copies ran while one was open for 3% of the time, Pallas kernels for 0%

profile of v1, /device:TPU:0, one launch (start us, length us, event | category | flops | bytes accessed | tf_op | source)
XLA Modules:
  0.0 759.8 jit_solution(8117505802608069291)
XLA Ops:
  20.9 109.0 %all-gather.5.cloned.1.call-done = bf16[10240,768]{1,0:T(8,128)(2,1)} async-done(((bf16[320,768]{1,0:T(8,128)(2,1)}), bf16[10240,768]{1,0:T(8,128)(2,1)}) %all-gather.5.cloned.1.call-update) | async-done | bytes 15728656 | tf_op jit(solution)/shard_map/all_gather | solution.py:220
  133.3 4.8 slice.320
  138.1 7.8 %fusion.66 = (bf16[32,24,768]{2,1,0:T(8,128)(2,1)}, bf16[32,24,768]{2,1,0:T(8,128)(2,1)}, bf16[32,24,768]{2,1,0:T(8,128)(2,1)}, bf16[32,24,768]{2,1,0:T(8,128)(2...) fusion(bf16[32,320,768]{2,1,0:T(8,128)(2,1)} %bitcast.225), kind=kLoop, calls=%fused_computation.240 | loop fusion | bytes 21233664 | tf_op jit(solution)/shard_map/slice | solution.py:225
  150.8 3.5 add_convert_fusion.3
  156.0 10.2 %fusion.68 = (f32[12,512]{1,0:T(8,128)S(1)}, f32[12,512,512]{1,2,0:T(8,128)}) fusion(pred[512,512]{0,1:T(8,128)(4,1)S(1)} %broadcast_compare_fusion, bf16[512,12,64]{0,2,1:T(8,128)(2,1)} %bitcast.274, bf16[512,12,64]{0,2,1:T(8,128)(2,1)S(1)} %bitcast.248), kind=kOutput, calls=%fused_computation.242 | convolution fusion | flops 415236608 | bytes 14442496 | tf_op jit(solution)/shard_map/sub | solution.py:70
  166.3 6.2 fusion.16
  175.7 20.3 %multiply_convert_fusion.2 = (bf16[512,3072]{1,0:T(8,128)(2,1)S(1)}, f32[512,3072]{1,0:T(8,128)}, f32[512,3072]{1,0:T(8,128)}) fusion(f32[3072]{0:T(1024)S(1)} %reshape.643, bf16[768,768]{1,0:T(8,128)(2,1)S(1)} %bitcast.262, bf16[768,768]{1,0:T(8,128)(2,1)S(1)} %bitcast.264, bf16[768,768]{1,0:T(8,128)(2,1)S(1)} %bitcast.266, ...), kind=kOutput, calls=%fused_computation.17 | convolution fusion | flops 2540568576 | bytes 22042624 | tf_op jit(solution)/shard_map/dot_general | solution.py:39
  204.1 69.4 %all-gather.7.cloned.1.call-done = bf16[4352,768]{1,0:T(8,128)(2,1)} async-done(((bf16[136,768]{1,0:T(8,128)(2,1)}), bf16[4352,768]{1,0:T(8,128)(2,1)}) %all-gather.7.cloned.1.call-update) | async-done | bytes 6684688 | tf_op jit(solution)/shard_map/all_gather | solution.py:259
  277.6 23.4 %add_reduce_fusion = (f32[4096]{0:T(1024)S(1)}, f32[4096,1568]{0,1:T(8,128)}) fusion(f32[1568]{0:T(1024)S(1)} %convert_element_type.357, bf16[4096,768]{1,0:T(8,128)(2,1)S(1)} %bitcast.228, bf16[1568,768]{1,0:T(8,128)(2,1)S(1)} %copy-done), kind=kOutput, calls=%fused_computation.7 | convolution fusion | flops 9877843968 | bytes 34412672 | tf_op jit(solution)/shard_map/dot_general | solution.py:49
  301.0 17.1 %exponential_reduce_fusion = (f32[4096]{0:T(1024)S(1)}, f32[]{:T(128)}) fusion(f32[4096,1568]{0,1:T(8,128)} %get-tuple-element.110, f32[4096]{0:T(1024)S(1)} %get-tuple-element.109, f32[1568]{0:T(1024)S(1)} %convert_element_type.357, pred[4096]{0:T(1024)(128)(4,1)S(1)} %bitcast.278, s32[4096]{0:T(1024)S(1)} %subtract_bitcast_fusion), kind=kLoop, calls=%fused_computation.5 | loop fusion | flops 44953600 | bytes 25749636 | tf_op jit(solution)/shard_map/reduce_sum | solution.py:267
  337.8 13.7 %convert_reduce_fusion = (f32[1568]{0:T(1024)}, bf16[4096,1568]{0,1:T(8,128)(2,1)S(1)}) fusion(pred[4096]{0:T(1024)(128)(4,1)S(1)} %bitcast.279, s32[4096]{0:T(1024)S(1)} %subtract_bitcast_fusion, f32[4096]{0:T(1024)S(1)} %get-tuple-element.97, f32[4096,1568]{0,1:T(8,128)S(1)} %copy-done.2, f32[1568]{0:T(1024)S(1)} %convert_element_type.357, ...), kind=kLoop, calls=%fused_computation.1 | loop fusion | flops 64223712 | bytes 38600960 | tf_op jit(solution)/shard_map/reduce_sum | solution.py:292
  351.5 4.7 copy-done.7
  356.2 15.1 %convolution_convert_fusion = bf16[4096,768]{1,0:T(8,128)(2,1)} fusion(bf16[4096,1568]{0,1:T(8,128)(2,1)S(1)} %get-tuple-element.34, bf16[1568,768]{1,0:T(8,128)(2,1)S(1)} %copy-done), kind=kOutput, calls=%fused_computation.14 | convolution fusion | flops 9868148736 | bytes 21544960 | tf_op jit(solution)/shard_map/dot_general | solution.py:39
  371.5 112.9 %reduce-scatter.3.cloned.1.call-done = bf16[128,768]{1,0:T(8,128)(2,1)} async-done(((bf16[4096,768]{1,0:T(8,128)(2,1)}), bf16[128,768]{1,0:T(8,128)(2,1)}) %reduce-scatter.3.cloned.1.call-update) | async-done | bytes 196624 | tf_op jit(solution)/shard_map/reduce_scatter | solution.py:290
  489.9 3.5 multiply_reduce_fusion.1
  495.7 9.3 %fusion.58 = (bf16[3072]{0:T(1024)(128)(2,1)S(1)}, bf16[512,3072]{1,0:T(8,128)(2,1)S(1)}) fusion(f32[512,3072]{1,0:T(8,128)} %get-tuple-element.53, f32[512,3072]{1,0:T(8,128)} %get-tuple-element.105, f32[3072]{0:T(1024)S(1)} %copy-done.48, bf16[512,768]{1,0:T(8,128)(2,1)S(1)} %get-tuple-element.38, bf16[3072,768]{1,0:T(8,128)(2,1)} %bitcast.236), kind=kOutput, calls=%fused_computation.234 | convolution fusion | flops 2441081856 | bytes 21252096 | tf_op jit(solution)/shard_map/dot_general | solution.py:49
  508.3 4.8 convolution_convert_fusion.2
  516.9 4.3 convolution_convert_fusion.1
  521.5 7.7 %bitcast_reduce_fusion = (bf16[12,64]{1,0:T(8,128)(2,1)S(1)}, bf16[12,64,512]{2,1,0:T(8,128)(2,1)}) fusion(bf16[512,12,64]{0,2,1:T(8,128)(2,1)S(1)} %bitcast.272, f32[12,512,512]{1,2,0:T(8,128)} %get-tuple-element.102, f32[12,512]{1,0:T(8,128)S(1)} %copy-done.40), kind=kOutput, calls=%fused_computation.77 | convolution fusion | flops 409730304 | bytes 14181888 | tf_op jit(solution)/shard_map/hqk,qhd->khd/dot_general | solution.py:98
  529.2 9.0 %multiply_reduce_fusion = (f32[12,512]{1,0:T(8,128)S(1)}, f32[12,512,512]{1,2,0:T(8,128)}) fusion(f32[12,512,512]{1,2,0:T(8,128)} %get-tuple-element.102, f32[12,512]{1,0:T(8,128)S(1)} %copy-done.40, bf16[512,12,64]{0,2,1:T(8,128)(2,1)S(1)} %bitcast.273, bf16[512,12,64]{0,2,1:T(8,128)(2,1)S(1)} %bitcast.293), kind=kOutput, calls=%fused_computation.9 | convolution fusion | flops 412084224 | bytes 26787840 | tf_op jit(solution)/shard_map/qhd,khd->hqk/dot_general | solution.py:95
  538.3 7.0 multiply_convert_fusion.1
  549.9 4.1 fusion.67
  578.0 17.0 %fusion.73 = f32[1568,768]{1,0:T(8,128)} fusion(bf16[4096,1568]{0,1:T(8,128)(2,1)} %copy-done.7, bf16[4096,768]{1,0:T(8,128)(2,1)} %bitcast.229), kind=kOutput, calls=%fused_computation.247 | convolution fusion | flops 9865003008 | bytes 23953408 | tf_op jit(solution)/shard_map/dot_general | solution.py:43
  599.5 146.7 %reduce-scatter.5.cloned.1.call-done = bf16[1,320,768]{2,1,0:T(8,128)(2,1)} async-done(((bf16[32,320,768]{2,1,0:T(8,128)(2,1)}), bf16[1,320,768]{2,1,0:T(8,128)(2,1)}) %reduce-scatter.5.cloned.1.call-update) | async-done | bytes 491536 | tf_op jit(solution)/shard_map/reduce_scatter | solution.py:322
  (307 shorter events, 110.5 us)
Async XLA Ops:
  7.2 270.4 %copy-start = (bf16[1568,768]{1,0:T(8,128)(2,1)S(1)}, bf16[1568,768]{1,0:T(8,128)(2,1)}, u32[]{:S(2)}) copy-start(bf16[1568,768]{1,0:T(8,128)(2,1)} %param.44) | copy-start | bytes 7225348
  7.2 122.7 %all-gather.5.cloned.1.call-start = ((), (), s32[]{:S(2)}) async-start(), calls=%async_computation.4 | async-start | bytes 16220160 | tf_op jit(solution)/shard_map/all_gather | solution.py:220
  17.0 256.5 %all-gather.7.cloned.1.call-start = ((), (), s32[]{:S(2)}) async-start(), calls=%async_computation.5 | async-start | bytes 6893568 | tf_op jit(solution)/shard_map/all_gather | solution.py:259
  146.0 27.8 %copy-start.47 = (f32[3072]{0:T(1024)}, f32[3072]{0:T(1024)S(1)}, u32[]{:S(2)}) copy-start(f32[3072]{0:T(1024)S(1)} %reshape.643) | copy-start | bytes 36868
  148.2 47.9 %copy-start.54 = (f32[768]{0:T(1024)}, f32[768]{0:T(1024)S(1)}, u32[]{:S(2)}) copy-start(f32[768]{0:T(1024)S(1)} %reshape.642) | copy-start | bytes 9220
  148.2 47.8 %copy-start.43 = (f32[768]{0:T(1024)}, f32[768]{0:T(1024)S(1)}, u32[]{:S(2)}) copy-start(f32[768]{0:T(1024)S(1)} %reshape.641) | copy-start | bytes 9220
  172.5 23.5 %slice-start.3 = ((s8[4718592]{0:T(1024)(128)(4,1)}), s8[4194304]{0:T(1024)(128)(4,1)S(1)}, s32[]{:S(2)}) async-start(s8[4718592]{0:T(1024)(128)(4,1)} %bitcast.237), calls=%async_computation.9 | async-start | bytes 8388608
  202.9 70.6 %copy-start.45 = (f32[128]{0:T(128)}, f32[128]{0:T(128)S(1)}, u32[]{:S(2)}) copy-start(f32[128]{0:T(128)S(1)} %broadcast_multiply_fusion.2) | copy-start | bytes 1540
  203.1 74.5 %copy-start.58 = (f32[128]{0:T(128)}, f32[128]{0:T(128)S(1)}, u32[]{:S(2)}) copy-start(f32[128]{0:T(128)S(1)} %multiply_reduce_fusion.7) | copy-start | bytes 1540
  203.1 70.4 %copy-start.51 = (f32[128]{0:T(128)}, f32[128]{0:T(128)S(1)}, u32[]{:S(2)}) copy-start(f32[128]{0:T(128)S(1)} %fusion.51) | copy-start | bytes 1540
  204.0 280.4 %reduce-scatter.3.cloned.1.call-start = ((), (), s32[]{:S(2)}) async-start(), calls=%async_computation.2 | async-start | bytes 6488064 | tf_op jit(solution)/shard_map/reduce_scatter | solution.py:290
  301.0 36.8 %copy-start.2 = (f32[4096,1568]{0,1:T(8,128)S(1)}, f32[4096,1568]{0,1:T(8,128)}, u32[]{:S(2)}) copy-start(f32[4096,1568]{0,1:T(8,128)} %get-tuple-element.110) | copy-start | bytes 77070336
  318.8 1.3 collective-permute-start
  320.8 3.8 collective-permute-start.1
  324.7 3.8 collective-permute-start.2
  328.5 3.8 collective-permute-start.3
  332.4 4.7 collective-permute-start.4
  371.4 113.0 %copy-start.46 = (f32[128]{0:T(128)S(1)}, f32[128]{0:T(128)}, u32[]{:S(2)}) copy-start(f32[128]{0:T(128)} %copy-done.45) | copy-start | bytes 1540
  371.4 114.1 %copy-start.59 = (f32[128]{0:T(128)S(1)}, f32[128]{0:T(128)}, u32[]{:S(2)}) copy-start(f32[128]{0:T(128)} %copy-done.58) | copy-start | bytes 1540
  371.4 114.2 %copy-start.52 = (f32[128]{0:T(128)S(1)}, f32[128]{0:T(128)}, u32[]{:S(2)}) copy-start(f32[128]{0:T(128)} %copy-done.51) | copy-start | bytes 1540
  371.4 118.6 %copy-start.4 = (f32[512,768]{1,0:T(8,128)S(1)}, f32[512,768]{1,0:T(8,128)}, u32[]{:S(2)}) copy-start(f32[512,768]{1,0:T(8,128)} %copy-done.3) | copy-start | bytes 4718596
  371.4 118.6 %copy-start.35 = (bf16[512,768]{1,0:T(8,128)(2,1)S(1)}, bf16[512,768]{1,0:T(8,128)(2,1)}, u32[]{:S(2)}) copy-start(bf16[512,768]{1,0:T(8,128)(2,1)} %param.27) | copy-start | bytes 2359300
  371.4 374.8 %reduce-scatter.5.cloned.1.call-start = ((), (), s32[]{:S(2)}) async-start(), calls=%async_computation.3 | async-start | bytes 16220160 | tf_op jit(solution)/shard_map/reduce_scatter | solution.py:322
  597.3 154.7 %copy-start.1 = (bf16[1568,768]{1,0:T(8,128)(2,1)S(1)}, bf16[1568,768]{1,0:T(8,128)(2,1)}, u32[]{:S(2)}) copy-start(bf16[1568,768]{1,0:T(8,128)(2,1)} %param.44) | copy-start | bytes 7225348
  (59 other events, 454.9 us)
Sparse Core Ops, SparseCore 0:
  17.1 112.7 all-gather.4
  204.1 69.3 all-gather.6
  371.5 112.7 reduce-scatter.2
  576.3 169.8 reduce-scatter.4

commit v2 on v1

--- a/solution.py
+++ b/solution.py
@@ -1,6 +1,10 @@
+import functools
+
 import jax
 import jax.numpy as jnp
 from jax import lax
+from jax.experimental import pallas as pl
+from jax.experimental.pallas import tpu as pltpu
 from jax.sharding import PartitionSpec as P
 
 HEADS = 12
@@ -80,51 +84,6 @@
     return (hidden, (queries, keys_low, values_low, softmax, softmax_low, context, summed))
 
 
-def attention_backward(tokens, params, saved, hidden_grad):
-    qkv_weight, attn_bias, out_weight, out_bias, attn_gain, attn_shift = params
-    row_count, model_width = tokens.shape
-    shaped = (row_count, HEADS, HEAD_DIM)
-    score_scale = HEAD_DIM ** (-0.5)
-    queries, keys_low, values_low, softmax, softmax_low, context, summed = saved
-    _, norm_back = jax.vjp(layer_norm, summed, to_full(attn_gain), to_full(attn_shift))
-    summed_grad, gain_grad, shift_grad = norm_back(hidden_grad)
-    branch_grad = to_low(summed_grad)
-    out_bias_grad = jnp.sum(to_full(branch_grad), axis=0)
-    out_weight_grad = matmul_tn(context, branch_grad)
-    context_grad = to_low(matmul_nt(branch_grad, out_weight)).reshape(shaped)
-    softmax_grad = jnp.einsum(
-        "qhd,khd->hqk", context_grad, values_low, preferred_element_type=jnp.float32
-    )
-    value_grad = jnp.einsum(
-        "hqk,qhd->khd", softmax_low, context_grad, preferred_element_type=jnp.float32
-    )
-    score_grad = to_low(
-        softmax * (softmax_grad - jnp.sum(softmax * softmax_grad, axis=-1, keepdims=True))
-    )
-    query_grad = (
-        jnp.einsum("hqk,khd->qhd", score_grad, keys_low, preferred_element_type=jnp.float32)
-        * score_scale
-    )
-    key_grad = (
-        jnp.einsum("hqk,qhd->khd", score_grad, queries, preferred_element_type=jnp.float32)
-        * score_scale
-    )
-    parts = [
-        to_low(part.reshape(row_count, model_width)) for part in (query_grad, key_grad, value_grad)
-    ]
-    qkv_grad = [matmul_tn(tokens, part) for part in parts]
-    bias_grad = jnp.concatenate(
-        [jnp.sum(to_full(parts[0]), axis=0), jnp.sum(to_full(parts[2]), axis=0)]
-    )
-    tokens_grad = summed_grad
-    for part, weight in zip(parts, qkv_weight):
-        tokens_grad = tokens_grad + matmul_nt(part, weight)
-    return (
-        tokens_grad,
-        (qkv_grad, bias_grad, out_weight_grad, out_bias_grad, gain_grad, shift_grad),
-    )
-
-
 def ffn_forward(hidden, params):
     up_weight, up_bias, down_weight, down_bias, ffn_gain, ffn_shift = params
     pre_act = matmul(hidden, up_weight) + to_full(up_bias)
@@ -134,28 +93,173 @@
     return (result, (pre_act, active, summed))
 
 
-def ffn_backward(hidden, params, saved, result_grad):
-    up_weight, up_bias, down_weight, down_bias, ffn_gain, ffn_shift = params
-    pre_act, active, summed = saved
-    _, norm_back = jax.vjp(layer_norm, summed, to_full(ffn_gain), to_full(ffn_shift))
-    summed_grad, gain_grad, shift_grad = norm_back(result_grad)
-    branch_grad = to_low(summed_grad)
-    down_bias_grad = jnp.sum(to_full(branch_grad), axis=0)
-    down_weight_grad = matmul_tn(active, branch_grad)
-    active_grad = matmul_nt(branch_grad, down_weight)
-    _, gelu_back = jax.vjp(gelu_exact, pre_act)
-    pre_grad = to_low(gelu_back(active_grad)[0])
-    up_bias_grad = jnp.sum(to_full(pre_grad), axis=0)
-    up_weight_grad = matmul_tn(hidden, pre_grad)
-    hidden_grad = summed_grad + matmul_nt(pre_grad, up_weight)
-    return (
-        hidden_grad,
-        (up_weight_grad, up_bias_grad, down_weight_grad, down_bias_grad, gain_grad, shift_grad),
-    )
-
-
 def column_blocks(matrix, width):
     return [matrix[:, k : k + width] for k in range(0, matrix.shape[1], width)]
+
+
+def take(value, axis, index):
+    return lax.dynamic_index_in_dim(value, index, axis, keepdims=False)
+
+
+def add_low(first, second):
+    return to_low(to_full(first) + to_full(second))
+
+
+def halve(value, axis, stride):
+    chips = lax.axis_size("dp")
+    bit = (lax.axis_index("dp") // stride) % 2
+    pairs = [(chip, chip ^ stride) for chip in range(chips)]
+    arrived = lax.ppermute(take(value, axis, 1 - bit), "dp", pairs)
+    return add_low(take(value, axis, bit), arrived)
+
+
+def core_halves(value, chips):
+    split = value.reshape(chips, 2, -1, value.shape[-1])
+    core = lax.axis_index("fsdp")
+    return take(split, 1, 1 - core), take(split, 1, core)
+
+
+def core_stage(matrices):
+    chips = lax.axis_size("dp")
+    halves = [core_halves(matrix, chips) for matrix in matrices]
+    away = jnp.concatenate([half[0] for half in halves], axis=1)
+    kept = jnp.concatenate([half[1] for half in halves], axis=1)
+    return core_swap(away, kept)
+
+
+def core_swap(away, kept):
+    return add_low(kept, lax.ppermute(away, "fsdp", [(0, 1), (1, 0)]))
+
+
+def first_plane_stage(value):
+    rows, width = value.shape[1:]
+    value = value.reshape(-1, 2, 2, rows, width)
+    return halve(value[..., : width // 2], 2, 1), halve(value[..., width // 2 :], 1, 2)
+
+
+def second_plane_stage(value):
+    left, right = value
+    return jnp.concatenate([halve(left, 1, 2), halve(right, 1, 1)], axis=-1)
+
+
+def level_stage(value):
+    levels, rows, width = value.shape
+    return halve(value.reshape(2, levels // 2, rows, width), 0, 2 * levels)
+
+
+def level_stages(value):
+    while value.shape[0] > 1:
+        value = level_stage(value)
+    return to_full(value[0])
+
+
+def level_exchange(value):
+    levels = value.shape[0]
+    groups = [[place + 4 * level for level in range(levels)] for place in range(4)]
+    value = lax.all_to_all(value, "dp", 0, 0, axis_index_groups=groups, tiled=True)
+    return jnp.sum(to_full(value), axis=0)
+
+
+def tie(value, *others):
+    return lax.optimization_barrier((value, *others))
+
+
+def window_base(start, total, window):
+    return pl.multiple_of(jnp.minimum((start // 16) * 16, total - window), 16)
+
+
+def compact_kernel(places, counts, gathered_ref, out_ref, picked_ref, *, window, slots):
+    step = pl.program_id(0)
+
+    @pl.when(step == 0)
+    def _():
+        out_ref[...] = jnp.zeros_like(out_ref)
+        picked_ref[...] = jnp.zeros_like(picked_ref)
+
+    batch = gathered_ref.shape[0]
+    total = out_ref.shape[0]
+    for lane in range(batch):
+        source = step * batch + lane
+        start = places[source]
+        base = window_base(start, total, window)
+        row = lax.broadcasted_iota(jnp.int32, (window, slots), 0) + (base - start)
+        column = lax.broadcasted_iota(jnp.int32, (window, slots), 1)
+        chosen = jnp.where((row == column) & (column < counts[source]), 1.0, 0.0)
+        chosen = chosen.astype(jnp.bfloat16)
+        span = pl.ds(base, window)
+        moved = jnp.dot(chosen, gathered_ref[lane, :slots, :], preferred_element_type=jnp.float32)
+        out_ref[span, :] += moved.astype(jnp.bfloat16)
+        picked_ref[span, :] += lax.dot_general(
+            chosen,
+            gathered_ref[lane, slots:, :slots],
+            (((1,), (1,)), ((), ())),
+            preferred_element_type=jnp.float32,
+        )
+
+
+def compact(places, counts, gathered, slots, total):
+    sources, depth, width = gathered.shape
+    batch = 4
+    return pl.pallas_call(
+        functools.partial(compact_kernel, window=slots + 16, slots=slots),
+        grid_spec=pltpu.PrefetchScalarGridSpec(
+            num_scalar_prefetch=2,
+            grid=(sources // batch,),
+            in_specs=[pl.BlockSpec((batch, depth, width), lambda i, p, c: (i, 0, 0))],
+            out_specs=[
+                pl.BlockSpec((total, width), lambda i, p, c: (0, 0)),
+                pl.BlockSpec((total, depth - slots), lambda i, p, c: (0, 0)),
+            ],
+        ),
+        out_shape=[
+            jax.ShapeDtypeStruct((total, width), jnp.bfloat16),
+            jax.ShapeDtypeStruct((total, depth - slots), jnp.float32),
+        ],
+        compiler_params=pltpu.CompilerParams(dimension_semantics=("arbitrary",)),
+        name="compact_rows",
+    )(places, counts, gathered)
+
+
+def spread_kernel(places, counts, rows_ref, *out_refs, window):
+    step = pl.program_id(0)
+    total = rows_ref.shape[0]
+    batch, slots = out_refs[0].shape[:2]
+    for side, out_ref in enumerate(out_refs):
+        for lane in range(batch):
+            chip = step * batch + lane
+            start = places[side, chip]
+            base = window_base(start, total, window)
+            row = lax.broadcasted_iota(jnp.int32, (slots, window), 0)
+            column = lax.broadcasted_iota(jnp.int32, (slots, window), 1) + (base - start)
+            chosen = jnp.where((row == column) & (row < counts[side, chip]), 1.0, 0.0)
+            chosen = chosen.astype(jnp.bfloat16)
+            moved = jnp.dot(
+                chosen, rows_ref[pl.ds(base, window), :], preferred_element_type=jnp.float32
+            )
+            out_ref[lane] = moved.astype(jnp.bfloat16)
+
+
+def spread(places, counts, rows, slots):
+    sides, chips = places.shape
+    total, width = rows.shape
+    batch = 2
+    block = pl.BlockSpec((batch, slots, width), lambda i, p, c: (i, 0, 0))
+    return pl.pallas_call(
+        functools.partial(spread_kernel, window=slots + 16),
+        grid_spec=pltpu.PrefetchScalarGridSpec(
+            num_scalar_prefetch=2,
+            grid=(chips // batch,),
+            in_specs=[
+                pl.BlockSpec(
+                    (total, width), lambda i, p, c: (0, 0), pipeline_mode=pl.Buffered(1)
+                )
+            ],
+            out_specs=[block] * sides,
+        ),
+        out_shape=[jax.ShapeDtypeStruct((chips, slots, width), jnp.bfloat16)] * sides,
+        compiler_params=pltpu.CompilerParams(dimension_semantics=("arbitrary",)),
+        name="spread_rows",
+    )(places, counts, rows)
 
 
 def butterfly(value, join, count):
@@ -257,38 +361,47 @@
     label_rows = jnp.stack([shifted // 256, shifted % 256]).astype(jnp.bfloat16)
     label_rows = jnp.pad(label_rows, ((0, 6), (0, width - MAXM)))
     rows_gathered = lax.all_gather(jnp.concatenate([normed_low, label_rows]), AXES, axis=0)
-    all_rows = rows_gathered[:, :MAXM].reshape(count * MAXM, width)
-    label_parts = rows_gathered[:, MAXM : MAXM + 2, :MAXM].astype(jnp.int32)
-    all_labels = (label_parts[:, 0] * 256 + label_parts[:, 1] - 1).reshape(count * MAXM)
+    chips = count // 2
+    label_parts = rows_gathered[:, MAXM : MAXM + 2, :MAXM].astype(jnp.float32)
+    counts = jnp.sum((label_parts[:, 0] + label_parts[:, 1] > 0).astype(jnp.int32), axis=1)
+    by_core = counts.reshape(chips, 2)
+    group = MASK_DEV * chips
+    places = jnp.cumsum(by_core, axis=0) - by_core + jnp.arange(2)[None, :] * group
+    total = 2 * group
+    all_rows, picked_labels = compact(places.reshape(count), counts, rows_gathered, MAXM, total)
+    parts = picked_labels[:, :2].astype(jnp.int32)
+    all_labels = parts[:, 0] * 256 + parts[:, 1] - 1
     slice_index = lax.axis_index(AXES)
     vocab_rows = decoder.shape[0]
     logits = matmul_nt(all_rows, decoder) + to_full(vocab_bias)
     row_peak = jnp.max(logits, axis=1)
     exp_sums = jnp.sum(jnp.exp(logits - row_peak[:, None]), axis=1)
     local_label = all_labels - slice_index * vocab_rows
-    row_valid = all_labels >= 0
-    label_hit = (jnp.arange(vocab_rows)[None, :] == local_label[:, None]) & row_valid[:, None]
+    label_hit = jnp.arange(vocab_rows)[None, :] == local_label[:, None]
     label_sum = jnp.sum(jnp.where(label_hit, logits, 0.0))
-    local_total = (row_peak + jnp.log(exp_sums)).reshape(count, MAXM)
+    local_total = (row_peak + jnp.log(exp_sums)).reshape(-1, 128)
+    lines = local_total.shape[0]
     stats = jnp.concatenate(
-        [local_total, jnp.pad(label_sum[None, None], ((0, 7), (0, MAXM - 1)))], axis=0
+        [local_total, jnp.pad(label_sum[None, None], ((0, 7), (0, 127)))], axis=0
     )
 
     def join(first, second):
         merged = jnp.maximum(first, second) + jnp.log1p(jnp.exp(-jnp.abs(first - second)))
-        is_total = jnp.arange(first.shape[0])[:, None] < count
+        is_total = jnp.arange(first.shape[0])[:, None] < lines
         return jnp.where(is_total, merged, first + second)
 
     stats = butterfly(stats, join, count)
-    log_total = stats[:count].reshape(count * MAXM)
-    row_weight = row_valid.astype(jnp.float32)
-    mean_loss = (jnp.sum(row_weight * log_total) - stats[count, 0]) / (MASK_DEV * count)
+    log_total = stats[:lines].reshape(total)
+    mean_loss = (jnp.sum(log_total) - stats[lines, 0]) / total
     logit_grad = to_low(
-        row_weight[:, None] * (jnp.exp(logits - log_total[:, None]) - label_hit.astype(jnp.float32))
+        jnp.exp(logits - log_total[:, None]) - label_hit.astype(jnp.float32)
     )
     rows_part = to_low(matmul(logit_grad, decoder))
-    normed_grad = to_full(lax.psum_scatter(rows_part, AXES, scatter_dimension=0, tiled=True))
-    decoder_grad = matmul_tn(logit_grad, all_rows)
+    core = lax.axis_index("fsdp")
+    sides = jnp.stack([1 - core, core])
+    away, kept = spread(places.T[sides], by_core.T[sides], rows_part, MAXM)
+    value = first_plane_stage(core_swap(away, kept))
+    normed_grad = level_exchange(second_plane_stage(value))
     vocab_bias_grad = jnp.sum(to_full(logit_grad), axis=0)
     dense_grad, head_gain_grad, head_shift_grad = tail_back(normed_grad)
     dense_grad_low = to_low(dense_grad)
@@ -297,52 +410,120 @@
     picked_grad = to_low(matmul_nt(dense_grad_low, dense_full))
     token_grad = matmul_tn(picker_low, picked_grad)
     output_grad = to_full(cotangent) + token_grad
-    hidden_grad, ffn_terms = ffn_backward(hidden, ffn_params, ffn_saved, output_grad)
-    tokens_grad, attn_terms = attention_backward(tokens, attn_params, attn_saved, hidden_grad)
-
+    pre_act, active, summed2 = ffn_saved
+    up_full, up_bias_full, down_full, _, ffn_gain_full, ffn_shift_full = ffn_params
+    _, norm_back = jax.vjp(layer_norm, summed2, to_full(ffn_gain_full), to_full(ffn_shift_full))
+    summed2_grad, ffn_gain_grad, ffn_shift_grad = norm_back(output_grad)
+    branch2_grad = to_low(summed2_grad)
+    down_bias_grad = jnp.sum(to_full(branch2_grad), axis=0)
+    down_grad = to_low(matmul_tn(active, branch2_grad))
+    first = core_stage([down_grad, to_low(dense_weight_grad)])
+    active_grad = matmul_nt(branch2_grad, down_full)
+    _, gelu_back = jax.vjp(gelu_exact, pre_act)
+    pre_grad = to_low(gelu_back(active_grad)[0])
+    up_bias_grad = jnp.sum(to_full(pre_grad), axis=0)
+    up_grad = to_low(matmul_tn(hidden, pre_grad))
+    hidden_grad = summed2_grad + matmul_nt(pre_grad, up_full)
+    hidden_grad, up_grad, first = tie(hidden_grad, up_grad, first)
+
+    queries, keys_low, values_low, softmax, softmax_low, context, summed1 = attn_saved
+    row_count = tokens.shape[0]
+    shaped = (row_count, HEADS, HEAD_DIM)
+    score_scale = HEAD_DIM ** (-0.5)
+    _, norm_back = jax.vjp(
+        layer_norm, summed1, to_full(attn_params[4]), to_full(attn_params[5])
+    )
+    summed1_grad, attn_gain_grad, attn_shift_grad = norm_back(hidden_grad)
+    branch1_grad = to_low(summed1_grad)
+    out_bias_grad = jnp.sum(to_full(branch1_grad), axis=0)
+    out_grad = to_low(matmul_tn(context, branch1_grad))
+    context_grad = to_low(matmul_nt(branch1_grad, out_full))
+    first = first_plane_stage(first)
+    second = core_stage([*column_blocks(up_grad, width), out_grad])
+    context_grad = context_grad.reshape(shaped)
+    softmax_grad = jnp.einsum(
+        "qhd,khd->hqk", context_grad, values_low, preferred_element_type=jnp.float32
+    )
+    row_dot = jnp.sum(softmax * softmax_grad, axis=-1, keepdims=True)
+    row_dot, second, *first = tie(row_dot, second, *first)
+    score_grad = to_low(softmax * (softmax_grad - row_dot))
+    first = second_plane_stage(first)
+    second = first_plane_stage(second)
+    value_grad = jnp.einsum(
+        "hqk,qhd->khd", softmax_low, context_grad, preferred_element_type=jnp.float32
+    )
+    score_grad, first = tie(score_grad, first)
+    query_grad = (
+        jnp.einsum("hqk,khd->qhd", score_grad, keys_low, preferred_element_type=jnp.float32)
+        * score_scale
+    )
+    key_grad = (
+        jnp.einsum("hqk,qhd->khd", score_grad, queries, preferred_element_type=jnp.float32)
+        * score_scale
+    )
+    mixed = [to_low(part.reshape(row_count, width)) for part in (query_grad, key_grad, value_grad)]
+    bias_grad = jnp.concatenate(
+        [jnp.sum(to_full(mixed[0]), axis=0), jnp.sum(to_full(mixed[2]), axis=0)]
+    )
+    qkv_grads = [to_low(matmul_tn(tokens, part)) for part in mixed]
     small_grads = (
-        *(attn_terms[k] for k in (1, 3, 4, 5)),
-        *(ffn_terms[k] for k in (1, 3, 4, 5)),
+        bias_grad,
+        out_bias_grad,
+        attn_gain_grad,
+        attn_shift_grad,
+        up_bias_grad,
+        down_bias_grad,
+        ffn_gain_grad,
+        ffn_shift_grad,
         dense_bias_grad,
         head_gain_grad,
         head_shift_grad,
     )
-    grad_matrices = [
-        *attn_terms[0],
-        attn_terms[2],
-        *column_blocks(ffn_terms[0], width),
-        ffn_terms[2],
-        dense_weight_grad,
-    ]
-    grads_packed = jnp.concatenate(
-        [to_low(matrix).reshape(count, -1, width) for matrix in grad_matrices]
-        + [to_low(pack_small(small_grads, count, width))],
-        axis=1,
-    )
-    grads = to_full(lax.psum_scatter(grads_packed, AXES, scatter_dimension=0, tiled=True)[0])
-    pieces = []
-    offset = 0
-    for matrix in matrices:
-        pieces.append(grads[offset : offset + matrix.shape[0]])
-        offset += matrix.shape[0]
+    first = level_stage(first) if first.shape[0] > 1 else first
+    third = core_stage([*qkv_grads, to_low(pack_small(small_grads, count, width)).reshape(-1, width)])
+    second = second_plane_stage(second)
+    mixed[0], second, third = tie(mixed[0], second, third)
+    tokens_grad = summed1_grad
+    for part, weight in zip(mixed, qkv_full):
+        tokens_grad = tokens_grad + matmul_nt(part, weight)
+    third = first_plane_stage(third)
+    logit_grad, first = tie(logit_grad, first)
+    decoder_grad = matmul_tn(logit_grad, all_rows)
+    first = level_stages(first)
+    third = second_plane_stage(third)
+    second = level_stages(second)
+    third = level_exchange(third)
+
+    def own_pieces(summed, matrices):
+        ends = []
+        offset = 0
+        for matrix in matrices:
+            share = matrix.shape[0] // count
+            ends.append(summed[offset : offset + share])
+            offset += share
+        return ends
+
+    down_piece, dense_piece = own_pieces(first, [down_grad, dense_weight_grad])
+    *up_pieces, out_piece = own_pieces(second, [*column_blocks(up_grad, width), out_grad])
+    *qkv_pieces, small_grad = own_pieces(third, [*qkv_grads, jnp.zeros((count * 8, 1))])
     small_pieces = []
     start = 0
     for vector in small:
-        small_pieces.append(grads[offset, start : start + vector.shape[0]])
+        small_pieces.append(small_grad[0, start : start + vector.shape[0]])
         start += vector.shape[0]
     return (
         output,
         mean_loss,
         tokens_grad,
-        jnp.concatenate(pieces[:blocks], axis=1),
+        jnp.concatenate(qkv_pieces, axis=1),
         small_pieces[0],
-        pieces[blocks],
+        out_piece,
         *small_pieces[1:4],
-        jnp.concatenate(pieces[blocks + 1 : blocks + 1 + len(up_blocks)], axis=1),
+        jnp.concatenate(up_pieces, axis=1),
         small_pieces[4],
-        pieces[-2],
+        down_piece,
         *small_pieces[5:8],
-        pieces[-1],
+        dense_piece,
         *small_pieces[8:],
         decoder_grad,
         vocab_bias_grad,

time: 764 us -> 637 us (0.83)
  waiting for transfers between devices: 449 us -> 278 us
  matrix products: 167 us -> 134 us
  starting transfers between devices: 6.83 us -> 34.2 us
  Pallas kernels: 0 us -> 17.9 us
  other arithmetic: 57.4 us -> 73.8 us
  local copies, waits for them, and re-layouts: 62 us -> 70.9 us
    reduce_scatter x2 -> x0, waiting for transfers between devices: 260 us -> none  [the longest x1 147 us: per_device(): lax.psum_scatter(grads_packed, AXES, scatter_dimension=0, tiled=True)[0]]
    ppermute x0 -> x24, waiting for transfers between devices: none -> 65.8 us  [the longest x20 59.8 us: halve(): arrived = lax.ppermute(take(value, axis, 1 - bit), 'dp', pairs)]
    all_to_all x0 -> x2, waiting for transfers between devices: none -> 25.7 us  [level_exchange(): lax.all_to_all(value, 'dp', 0, 0, axis_index_groups=groups, tiled=True)]
    convert_element_type x3 -> x25, other arithmetic: 7.5 us -> 29.1 us  [to_low(): return values.astype(jnp.bfloat16)]
    ppermute x0 -> x24, starting transfers between devices: none -> 19.9 us  [the longest x20 19.4 us: halve(): arrived = lax.ppermute(take(value, axis, 1 - bit), 'dp', pairs)]
    pallas_call x0 -> x2, Pallas kernels: none -> 17.9 us  [the longest x1 10.2 us: compact(): pl.pallas_call(functools.partial(compact_kernel, window=slots + 16, slots...]
    dot_general x7, matrix products: 40.5 us -> 24.4 us  [matmul_nt(): lax.dot_general(left_side, right_side, (((1,), (1,)), ((), ())), preferre...]
    dot_general x9, matrix products: 40.5 us -> 28.7 us  [matmul_tn(): lax.dot_general(left_side, right_side, (((0,), (0,)), ((), ())), preferre...]
  transfers between devices with their start and end apart: 9 -> 33, of which waited for: 9 -> 19; matrix products, arithmetic and copies ran while one was open for 3% -> 14% of each run, Pallas kernels for 0% -> 0%
where the time goes in v2:
time: 637 us; the launch traced here: 627 us
  waiting for transfers between devices  278 us (44%)
  matrix products  134 us (21%)
  other arithmetic  73.8 us (12%)
  local copies, waits for them, and re-layouts  70.9 us (11%)
  starting transfers between devices  34.2 us (5%)
  between operations  18.8 us (3%)
  Pallas kernels  17.9 us (3%)
    all_gather x1, waiting for transfers between devices, per_device(): gathered = lax.all_gather(packed, AXES, axis=0)  109 us
    all_gather x1, waiting for transfers between devices, per_device(): lax.all_gather(jnp.concatenate([normed_low, label_rows]), AXES, axis=0)  69.4 us
    ppermute x20, waiting for transfers between devices, halve(): arrived = lax.ppermute(take(value, axis, 1 - bit), 'dp', pairs)  59.8 us
    dot_general x9, matrix products, matmul(): return jnp.dot(left_side, right_side, preferred_element_type=jnp.float32)  46.7 us
    convert_element_type x25, other arithmetic, to_low(): return values.astype(jnp.bfloat16)  29.1 us
    dot_general x9, matrix products, matmul_tn(): lax.dot_general(left_side, right_side, (((0,), (0,)), ((), ())), preferre...  28.7 us
    all_to_all x2, waiting for transfers between devices, level_exchange(): lax.all_to_all(value, 'dp', 0, 0, axis_index_groups=groups, tiled=True)  25.7 us
    dot_general x7, matrix products, matmul_nt(): lax.dot_general(left_side, right_side, (((1,), (1,)), ((), ())), preferre...  24.4 us
  transfers between devices with their start and end apart: 33, of which 19 were waited for; matrix products, arithmetic and copies ran while one was open for 14% of the time, Pallas kernels for 0%

profile of v2, /device:TPU:0, one launch (start us, length us, event | category | flops | bytes accessed | tf_op | source)
XLA Modules:
  0.0 627.3 jit_solution(2014890342798785796)
XLA Ops:
  20.9 109.0 %all-gather.5.cloned.1.call-done = bf16[10240,768]{1,0:T(8,128)(2,1)} async-done(((bf16[320,768]{1,0:T(8,128)(2,1)}), bf16[10240,768]{1,0:T(8,128)(2,1)}) %all-gather.5.cloned.1.call-update) | async-done | bytes 15728656 | tf_op jit(solution)/shard_map/all_gather | solution.py:324
  132.7 7.8 %fusion.85 = (bf16[32,24,768]{2,1,0:T(8,128)(2,1)}, bf16[32,24,768]{2,1,0:T(8,128)(2,1)}, bf16[32,24,768]{2,1,0:T(8,128)(2,1)}, bf16[32,24,768]{2,1,0:T(8,128)(2...) fusion(bf16[32,320,768]{2,1,0:T(8,128)(2,1)} %bitcast.369), kind=kLoop, calls=%fused_computation.336 | loop fusion | bytes 21233664 | tf_op jit(solution)/shard_map/slice | solution.py:329
  157.0 10.9 %fusion.92 = (f32[12,512]{1,0:T(8,128)}, f32[12,512,512]{1,2,0:T(8,128)}) fusion(pred[512,512]{0,1:T(8,128)(4,1)S(1)} %broadcast_compare_fusion, bf16[512,12,64]{0,2,1:T(8,128)(2,1)} %bitcast.431, bf16[512,12,64]{0,2,1:T(8,128)(2,1)S(1)} %bitcast.408), kind=kOutput, calls=%fused_computation.343 | convolution fusion | flops 415236608 | bytes 14442496 | tf_op jit(solution)/shard_map/sub | solution.py:74
  167.9 6.1 fusion.21
  176.7 23.2 %multiply_convert_fusion.1 = (bf16[512,3072]{1,0:T(8,128)(2,1)S(1)}, f32[512,3072]{1,0:T(8,128)}, f32[512,3072]{1,0:T(8,128)}) fusion(f32[3072]{0:T(1024)S(1)} %copy-done.49, bf16[768,768]{1,0:T(8,128)(2,1)} %bitcast.421, bf16[768,768]{1,0:T(8,128)(2,1)} %bitcast.423, bf16[768,768]{1,0:T(8,128)(2,1)} %bitcast.425, bf16[768,768]{1,0:T(8,128)(2,1)} %bitcast.427, ...), kind=kOutput, calls=%fused_computation.18 | convolution fusion | flops 2540568576 | bytes 22042624 | tf_op jit(solution)/shard_map/dot_general | solution.py:43
  211.8 69.4 %all-gather.7.cloned.1.call-done = bf16[4352,768]{1,0:T(8,128)(2,1)} async-done(((bf16[136,768]{1,0:T(8,128)(2,1)}), bf16[4352,768]{1,0:T(8,128)(2,1)}) %all-gather.7.cloned.1.call-update) | async-done | bytes 6684688 | tf_op jit(solution)/shard_map/all_gather | solution.py:363
  283.5 10.2 %compact_rows.1 = (bf16[2048,768]{1,0:T(8,128)(2,1)}, f32[2048,8]{1,0:T(8,128)}) custom-call(s32[32]{0:T(128)} %subtract_add_fusion.places, s32[32]{0:T(128)} %copy-done.50, bf16[32,136,768]{2,1,0:T(8,128)(2,1)} %bitcast.381), custom_call_target="tpu_custom_call" | custom-call | tf_op jit(solution)/shard_map/compact_rows/pallas_call | solution.py:203
  301.1 5.5 exponential_reduce_fusion
  325.9 11.7 %convert_reduce_fusion = (f32[1568]{0:T(1024)}, bf16[2048,1568]{0,1:T(8,128)(2,1)}) fusion(s32[2048]{0:T(1024)S(1)} %fusion.31, f32[2048]{0:T(1024)S(1)} %get-tuple-element.165, f32[2048,1568]{0,1:T(8,128)} %copy-done.2, f32[1568]{0:T(1024)S(1)} %convert_element_type.636), kind=kLoop, calls=%fused_computation.3 | loop fusion | flops 25688544 | bytes 19296512 | tf_op jit(solution)/shard_map/reduce_sum | solution.py:405
  337.6 10.4 %convolution_convert_fusion.2.rows_ref = bf16[2048,768]{1,0:T(8,128)(2,1)} fusion(bf16[2048,1568]{0,1:T(8,128)(2,1)} %get-tuple-element.56, bf16[1568,768]{1,0:T(8,128)(2,1)S(1)} %copy-done), kind=kOutput, calls=%fused_computation.42 | convolution fusion | flops 4934074368 | bytes 11976704 | tf_op jit(solution)/shard_map/dot_general | solution.py:43
  348.0 7.8 %spread_rows.1 = (bf16[16,128,768]{2,1,0:T(8,128)(2,1)}, bf16[16,128,768]{2,1,0:T(8,128)(2,1)}) custom-call(s32[2,16]{1,0:T(2,128)} %gather_fusion, s32[2,16]{1,0:T(2,128)} %gather_fusion.1, bf16[2048,768]{1,0:T(8,128)(2,1)} %convolution_convert_fusion.2.rows_ref), custom_call_target="tpu_custom_call" | custom-call | tf_op jit(solution)/shard_map/spread_rows/pallas_call | solution.py:247
  355.7 6.0 collective-permute-done.5
  373.8 14.4 %collective-permute-done.8 = bf16[4,2,128,384]{3,2,1,0:T(8,128)(2,1)} collective-permute-done((bf16[4,2,128,384]{3,2,1,0:T(8,128)(2,1)}, bf16[4,2,128,384]{3,2,1,0:T(8,128)(2,1)}, u32[]{:S(2)}, u32[]{:S(2)}) %collective-permute-start.8) | collective-permute-done | bytes 786464 | tf_op jit(solution)/shard_map/ppermute | solution.py:112
  395.4 5.7 collective-permute-done.9
  411.2 15.6 %all-to-all-done = bf16[4,128,768]{2,1,0:T(8,128)(2,1)S(1)} async-done(((bf16[4,128,768]{2,1,0:T(8,128)(2,1)}), bf16[4,128,768]{2,1,0:T(8,128)(2,1)S(1)}, u32[]{:S(2)}, u32[]{:S(2)}) %all-to-all-start) | async-done | bytes 786464 | tf_op jit(solution)/shard_map/all_to_all | solution.py:159
  444.3 8.1 %fusion.77 = (bf16[3072]{0:T(1024)(128)(2,1)S(1)}, bf16[512,3072]{1,0:T(8,128)(2,1)}) fusion(f32[512,3072]{1,0:T(8,128)S(1)} %bitcast.456, f32[512,3072]{1,0:T(8,128)} %get-tuple-element.173, f32[3072]{0:T(1024)S(1)} %copy-done.49, bf16[512,768]{1,0:T(8,128)(2,1)S(1)} %get-tuple-element.74, bf16[3072,768]{1,0:T(8,128)(2,1)S(1)} %bitcast.395), kind=kOutput, calls=%fused_computation.330 | convolution fusion | flops 2441081856 | bytes 21252096 | tf_op jit(solution)/shard_map/dot_general | solution.py:53
  453.4 6.7 %convolution_convert_fusion.1 = bf16[768,3072]{1,0:T(8,128)(2,1)} fusion(bf16[512,3072]{1,0:T(8,128)(2,1)} %get-tuple-element.76, f32[512,768]{1,0:T(8,128)S(1)} %copy-done.7, f32[768]{0:T(1024)S(1)} %copy-done.52, f32[768]{0:T(1024)S(1)} %copy-done.47, f32[512]{0:T(512)S(1)} %fusion.65, f32[512]{0:T(512)S(1)} %broadcast_multiply_fusion.1), kind=kOutput, calls=%fused_computation.39 | convolution fusion | flops 2420244480 | bytes 9447424 | tf_op jit(solution)/shard_map/dot_general | solution.py:47
  474.7 7.0 %bitcast_reduce_fusion = (bf16[12,64]{1,0:T(8,128)(2,1)S(1)}, bf16[12,64,512]{2,1,0:T(8,128)(2,1)S(1)}) fusion(bf16[512,12,64]{0,2,1:T(8,128)(2,1)S(1)} %bitcast.429, f32[12,512,512]{1,2,0:T(8,128)} %get-tuple-element.170, f32[12,512]{1,0:T(8,128)S(1)} %copy-done.48), kind=kOutput, calls=%fused_computation.117 | convolution fusion | flops 409730304 | bytes 14181888 | tf_op jit(solution)/shard_map/hqk,qhd->khd/dot_general | solution.py:452
  492.6 6.0 multiply_reduce_fusion
  522.8 6.8 %multiply_convert_fusion = bf16[12,512,512]{1,2,0:T(8,128)(2,1)S(1)} fusion(f32[12,512,512]{1,2,0:T(8,128)} %get-tuple-element.181, f32[12,512]{1,0:T(8,128)S(1)} %get-tuple-element.180, f32[12,512,512]{1,2,0:T(8,128)S(1)} %bitcast.376, f32[12,512]{1,0:T(8,128)S(1)} %copy-done.48), kind=kLoop, calls=%fused_computation.8 | loop fusion | flops 12582912 | bytes 31506432 | tf_op jit(solution)/shard_map/convert_element_type | solution.py:21
  549.3 12.1 %collective-permute-done.27 = bf16[2,120,768]{2,1,0:T(8,128)(2,1)S(1)} collective-permute-done((bf16[2,120,768]{2,1,0:T(8,128)(2,1)S(1)}, bf16[2,120,768]{2,1,0:T(8,128)(2,1)S(1)}, u32[]{:S(2)}, u32[]{:S(2)}) %collective-permute-start.27) | collective-permute-done | bytes 368672 | tf_op jit(solution)/shard_map/ppermute | solution.py:112
  561.6 7.0 %fusion.98 = f32[1568,768]{1,0:T(8,128)} fusion(bf16[2048,1568]{0,1:T(8,128)(2,1)S(1)} %bitcast.383, bf16[2048,768]{1,0:T(8,128)(2,1)S(1)} %copy-done.58), kind=kOutput, calls=%fused_computation.349 | convolution fusion | flops 4932501504 | bytes 14385152 | tf_op jit(solution)/shard_map/dot_general | solution.py:47
  578.6 13.7 %collective-permute-done.25 = bf16[2,120,768]{2,1,0:T(8,128)(2,1)S(1)} collective-permute-done((bf16[2,120,768]{2,1,0:T(8,128)(2,1)S(1)}, bf16[2,120,768]{2,1,0:T(8,128)(2,1)S(1)}, u32[]{:S(2)}, u32[]{:S(2)}) %collective-permute-start.25) | collective-permute-done | bytes 368672 | tf_op jit(solution)/shard_map/ppermute | solution.py:112
  606.2 10.2 %all-to-all-done.1 = bf16[4,80,768]{2,1,0:T(8,128)(2,1)S(1)} async-done(((bf16[4,80,768]{2,1,0:T(8,128)(2,1)}), bf16[4,80,768]{2,1,0:T(8,128)(2,1)S(1)}, u32[]{:S(2)}, u32[]{:S(2)}) %all-to-all-start.1) | async-done | bytes 491552 | tf_op jit(solution)/shard_map/all_to_all | solution.py:159
  (460 shorter events, 217.4 us)
Async XLA Ops:
  7.2 122.7 %all-gather.5.cloned.1.call-start = ((), (), s32[]{:S(2)}) async-start(), calls=%async_computation.2 | async-start | bytes 16220160 | tf_op jit(solution)/shard_map/all_gather | solution.py:324
  17.0 264.2 %all-gather.7.cloned.1.call-start = ((), (), s32[]{:S(2)}) async-start(), calls=%async_computation.3 | async-start | bytes 6893568 | tf_op jit(solution)/shard_map/all_gather | solution.py:363
  368.3 19.9 %collective-permute-start.8 = (bf16[4,2,128,384]{3,2,1,0:T(8,128)(2,1)}, bf16[4,2,128,384]{3,2,1,0:T(8,128)(2,1)}, u32[]{:S(2)}, u32[]{:S(2)}) collective-permute-start(bf16[4,2,128,384]{3,2,1,0:T(8,128)(2,1)} %dynamic-slice_bitcast_fusion.2), channel_id=1, source_target_pairs={{0,4},{2,6},{4,0},{6,2},{8,12},{10,14},{12,8},{14,10},{16,20},{18,... | collective-permute-start | bytes 2359304 | tf_op jit(solution)/shard_map/ppermute | solution.py:112
  373.2 20.7 %collective-permute-start.6 = (bf16[4,2,128,384]{3,2,0,1:T(8,128)(2,1)}, bf16[4,2,128,384]{3,2,0,1:T(8,128)(2,1)}, u32[]{:S(2)}, u32[]{:S(2)}) collective-permute-start(bf16[4,2,128,384]{3,2,0,1:T(8,128)(2,1)} %bitcast.363), channel_id=1, source_target_pairs={{0,2},{2,0},{4,6},{6,4},{8,10},{10,8},{12,14},{14,12},{16,18},{18,... | collective-permute-start | bytes 2359304 | tf_op jit(solution)/shard_map/ppermute | solution.py:112
  389.6 11.6 %collective-permute-start.9 = (bf16[4,128,384]{2,1,0:T(8,128)(2,1)S(1)}, bf16[4,128,384]{2,1,0:T(8,128)(2,1)S(1)}, u32[]{:S(2)}, u32[]{:S(2)}) collective-permute-start(bf16[4,128,384]{2,1,0:T(8,128)(2,1)S(1)} %dynamic-slice_bitcast_fusion.14), channel_id=1, source_target_pairs={{0,2},{2,0},{4,6},{6,4},{8,10},{10,8},{12,14},{14,12},{16,18},{18,... | collective-permute-start | bytes 1179656 | tf_op jit(solution)/shard_map/ppermute | solution.py:112
  395.3 8.9 %collective-permute-start.7 = (bf16[4,128,384]{2,1,0:T(8,128)(2,1)S(1)}, bf16[4,128,384]{2,1,0:T(8,128)(2,1)S(1)}, u32[]{:S(2)}, u32[]{:S(2)}) collective-permute-start(bf16[4,128,384]{2,1,0:T(8,128)(2,1)S(1)} %dynamic-slice_bitcast_fusion.15), channel_id=1, source_target_pairs={{0,4},{2,6},{4,0},{6,2},{8,12},{10,14},{12,8},{14,10},{16,20},{18,... | collective-permute-start | bytes 1179656 | tf_op jit(solution)/shard_map/ppermute | solution.py:112
  405.4 21.4 %all-to-all-start = ((bf16[4,128,768]{2,1,0:T(8,128)(2,1)}), bf16[4,128,768]{2,1,0:T(8,128)(2,1)S(1)}, u32[]{:S(2)}, u32[]{:S(2)}) async-start(bf16[4,128,768]{2,1,0:T(8,128)(2,1)} %pad_maximum_fusion.5), calls=%async_computation | async-start | bytes 1572864 | tf_op jit(solution)/shard_map/all_to_all | solution.py:159
  444.3 18.5 %collective-permute-start.10 = (bf16[16,120,768]{2,1,0:T(8,128)(2,1)}, bf16[16,120,768]{2,1,0:T(8,128)(2,1)}, u32[]{:S(2)}, u32[]{:S(2)}) collective-permute-start(bf16[16,120,768]{2,1,0:T(8,128)(2,1)} %pad_maximum_fusion.1), channel_id=1, source_target_pairs={{0,1},{1,0},{2,3},{3,2},{4,5},{5,4},{6,7},{7,6},{8,9},{9,8},{10,11... | collective-permute-start | bytes 8847368 | tf_op jit(solution)/shard_map/ppermute | solution.py:131
  487.2 25.9 %collective-permute-start.11 = (bf16[16,120,768]{2,1,0:T(8,128)(2,1)}, bf16[16,120,768]{2,1,0:T(8,128)(2,1)}, u32[]{:S(2)}, u32[]{:S(2)}) collective-permute-start(bf16[16,120,768]{2,1,0:T(8,128)(2,1)} %get-tuple-element.133), channel_id=1, source_target_pairs={{0,1},{1,0},{2,3},{3,2},{4,5},{5,4},{6,7},{7,6},{8,9},{9,8},{10,11... | collective-permute-start | bytes 8847368 | tf_op jit(solution)/shard_map/ppermute | solution.py:131
  490.4 21.4 %collective-permute-start.12 = (bf16[4,2,120,384]{3,2,0,1:T(8,128)(2,1)}, bf16[4,2,120,384]{3,2,0,1:T(8,128)(2,1)}, u32[]{:S(2)}, u32[]{:S(2)}) collective-permute-start(bf16[4,2,120,384]{3,2,0,1:T(8,128)(2,1)} %bitcast.365), channel_id=1, source_target_pairs={{0,2},{2,0},{4,6},{6,4},{8,10},{10,8},{12,14},{14,12},{16,18},{18,... | collective-permute-start | bytes 2211848 | tf_op jit(solution)/shard_map/ppermute | solution.py:112
  491.7 18.8 %collective-permute-start.13 = (bf16[4,2,120,384]{3,2,1,0:T(8,128)(2,1)S(1)}, bf16[4,2,120,384]{3,2,1,0:T(8,128)(2,1)}, u32[]{:S(2)}, u32[]{:S(2)}) collective-permute-start(bf16[4,2,120,384]{3,2,1,0:T(8,128)(2,1)S(1)} %dynamic-slice_bitcast_fusion.4), channel_id=1, source_target_pairs={{0,4},{2,6},{4,0},{6,2},{8,12},{10,14},{12,8},{14,10},{16,20},{18,... | collective-permute-start | bytes 2211848 | tf_op jit(solution)/shard_map/ppermute | solution.py:112
  516.1 13.6 %collective-permute-start.15 = (bf16[4,120,384]{2,1,0:T(8,128)(2,1)S(1)}, bf16[4,120,384]{2,1,0:T(8,128)(2,1)S(1)}, u32[]{:S(2)}, u32[]{:S(2)}) collective-permute-start(bf16[4,120,384]{2,1,0:T(8,128)(2,1)S(1)} %dynamic-slice_bitcast_fusion.20), channel_id=1, source_target_pairs={{0,2},{2,0},{4,6},{6,4},{8,10},{10,8},{12,14},{14,12},{16,18},{18,... | collective-permute-start | bytes 1105928 | tf_op jit(solution)/shard_map/ppermute | solution.py:112
  517.0 12.8 %collective-permute-start.14 = (bf16[4,120,384]{2,1,0:T(8,128)(2,1)S(1)}, bf16[4,120,384]{2,1,0:T(8,128)(2,1)S(1)}, u32[]{:S(2)}, u32[]{:S(2)}) collective-permute-start(bf16[4,120,384]{2,1,0:T(8,128)(2,1)S(1)} %dynamic-slice_bitcast_fusion.21), channel_id=1, source_target_pairs={{0,4},{2,6},{4,0},{6,2},{8,12},{10,14},{12,8},{14,10},{16,20},{18,... | collective-permute-start | bytes 1105928 | tf_op jit(solution)/shard_map/ppermute | solution.py:112
  519.5 24.2 %collective-permute-start.18 = (bf16[4,2,120,384]{3,2,1,0:T(8,128)(2,1)}, bf16[4,2,120,384]{3,2,1,0:T(8,128)(2,1)}, u32[]{:S(2)}, u32[]{:S(2)}) collective-permute-start(bf16[4,2,120,384]{3,2,1,0:T(8,128)(2,1)} %dynamic-slice_bitcast_fusion.3), channel_id=1, source_target_pairs={{0,4},{2,6},{4,0},{6,2},{8,12},{10,14},{12,8},{14,10},{16,20},{18,... | collective-permute-start | bytes 2211848 | tf_op jit(solution)/shard_map/ppermute | solution.py:112
  521.6 25.2 %collective-permute-start.16 = (bf16[4,2,120,384]{3,2,0,1:T(8,128)(2,1)}, bf16[4,2,120,384]{3,2,0,1:T(8,128)(2,1)}, u32[]{:S(2)}, u32[]{:S(2)}) collective-permute-start(bf16[4,2,120,384]{3,2,0,1:T(8,128)(2,1)} %bitcast.364), channel_id=1, source_target_pairs={{0,2},{2,0},{4,6},{6,4},{8,10},{10,8},{12,14},{14,12},{16,18},{18,... | collective-permute-start | bytes 2211848 | tf_op jit(solution)/shard_map/ppermute | solution.py:112
  542.5 27.8 %collective-permute-start.20 = (bf16[16,80,768]{2,1,0:T(8,128)(2,1)S(1)}, bf16[16,80,768]{2,1,0:T(8,128)(2,1)S(1)}, u32[]{:S(2)}, u32[]{:S(2)}) collective-permute-start(bf16[16,80,768]{2,1,0:T(8,128)(2,1)S(1)} %pad_maximum_fusion.2), channel_id=1, source_target_pairs={{0,1},{1,0},{2,3},{3,2},{4,5},{5,4},{6,7},{7,6},{8,9},{9,8},{10,11... | collective-permute-start | bytes 5898248 | tf_op jit(solution)/shard_map/ppermute | solution.py:131
  542.7 18.6 %collective-permute-start.27 = (bf16[2,120,768]{2,1,0:T(8,128)(2,1)S(1)}, bf16[2,120,768]{2,1,0:T(8,128)(2,1)S(1)}, u32[]{:S(2)}, u32[]{:S(2)}) collective-permute-start(bf16[2,120,768]{2,1,0:T(8,128)(2,1)S(1)} %dynamic-slice_bitcast_fusion.16), channel_id=1, source_target_pairs={{0,16},{2,18},{4,20},{6,22},{8,24},{10,26},{12,28},{14,30},{16,0},... | collective-permute-start | bytes 1105928 | tf_op jit(solution)/shard_map/ppermute | solution.py:112
  545.8 24.2 %collective-permute-start.19 = (bf16[4,120,384]{2,1,0:T(8,128)(2,1)S(1)}, bf16[4,120,384]{2,1,0:T(8,128)(2,1)S(1)}, u32[]{:S(2)}, u32[]{:S(2)}) collective-permute-start(bf16[4,120,384]{2,1,0:T(8,128)(2,1)S(1)} %dynamic-slice_bitcast_fusion.18), channel_id=1, source_target_pairs={{0,2},{2,0},{4,6},{6,4},{8,10},{10,8},{12,14},{14,12},{16,18},{18,... | collective-permute-start | bytes 1105928 | tf_op jit(solution)/shard_map/ppermute | solution.py:112
  548.1 22.0 %collective-permute-start.17 = (bf16[4,120,384]{2,1,0:T(8,128)(2,1)S(1)}, bf16[4,120,384]{2,1,0:T(8,128)(2,1)S(1)}, u32[]{:S(2)}, u32[]{:S(2)}) collective-permute-start(bf16[4,120,384]{2,1,0:T(8,128)(2,1)S(1)} %dynamic-slice_bitcast_fusion.19), channel_id=1, source_target_pairs={{0,4},{2,6},{4,0},{6,2},{8,12},{10,14},{12,8},{14,10},{16,20},{18,... | collective-permute-start | bytes 1105928 | tf_op jit(solution)/shard_map/ppermute | solution.py:112
  571.2 21.2 %collective-permute-start.23 = (bf16[4,2,80,384]{3,2,1,0:T(8,128)(2,1)S(1)}, bf16[4,2,80,384]{3,2,1,0:T(8,128)(2,1)S(1)}, u32[]{:S(2)}, u32[]{:S(2)}) collective-permute-start(bf16[4,2,80,384]{3,2,1,0:T(8,128)(2,1)S(1)} %dynamic-slice_bitcast_fusion.13), channel_id=1, source_target_pairs={{0,4},{2,6},{4,0},{6,2},{8,12},{10,14},{12,8},{14,10},{16,20},{18,... | collective-permute-start | bytes 1474568 | tf_op jit(solution)/shard_map/ppermute | solution.py:112
  572.2 21.4 %collective-permute-start.21 = (bf16[4,2,80,384]{3,2,0,1:T(8,128)(2,1)S(1)}, bf16[4,2,80,384]{3,2,0,1:T(8,128)(2,1)S(1)}, u32[]{:S(2)}, u32[]{:S(2)}) collective-permute-start(bf16[4,2,80,384]{3,2,0,1:T(8,128)(2,1)S(1)} %bitcast.435), channel_id=1, source_target_pairs={{0,2},{2,0},{4,6},{6,4},{8,10},{10,8},{12,14},{14,12},{16,18},{18,... | collective-permute-start | bytes 1474568 | tf_op jit(solution)/shard_map/ppermute | solution.py:112
  573.4 18.9 %collective-permute-start.25 = (bf16[2,120,768]{2,1,0:T(8,128)(2,1)S(1)}, bf16[2,120,768]{2,1,0:T(8,128)(2,1)S(1)}, u32[]{:S(2)}, u32[]{:S(2)}) collective-permute-start(bf16[2,120,768]{2,1,0:T(8,128)(2,1)S(1)} %dynamic-slice_bitcast_fusion.17), channel_id=1, source_target_pairs={{0,16},{2,18},{4,20},{6,22},{8,24},{10,26},{12,28},{14,30},{16,0},... | collective-permute-start | bytes 1105928 | tf_op jit(solution)/shard_map/ppermute | solution.py:112
  595.7 9.1 %collective-permute-start.26 = (bf16[1,120,768]{2,1,0:T(8,128)(2,1)}, bf16[1,120,768]{2,1,0:T(8,128)(2,1)S(1)}, u32[]{:S(2)}, u32[]{:S(2)}) collective-permute-start(bf16[1,120,768]{2,1,0:T(8,128)(2,1)} %constant_dynamic-slice_fusion.1), channel_id=1, source_target_pairs={{0,8},{2,10},{4,12},{6,14},{8,0},{10,2},{12,4},{14,6},{16,24},{18,... | collective-permute-start | bytes 552968 | tf_op jit(solution)/shard_map/ppermute | solution.py:112
  601.1 15.3 %all-to-all-start.1 = ((bf16[4,80,768]{2,1,0:T(8,128)(2,1)}), bf16[4,80,768]{2,1,0:T(8,128)(2,1)S(1)}, u32[]{:S(2)}, u32[]{:S(2)}) async-start(bf16[4,80,768]{2,1,0:T(8,128)(2,1)} %pad_maximum_fusion.8), calls=%async_computation.1 | async-start | bytes 983040 | tf_op jit(solution)/shard_map/all_to_all | solution.py:159
  (95 other events, 879.1 us)
Sparse Core Ops, SparseCore 0:
  17.1 112.7 all-gather.4
  211.8 69.3 all-gather.6

commit v3 on v1

v3 whole, which is shorter than its diff:
```python
import functools

import jax
import jax.numpy as jnp
from jax import lax
from jax.experimental import pallas as pl
from jax.experimental.pallas import tpu as pltpu
from jax.sharding import PartitionSpec as P

HEADS = 12
HEAD_DIM = 64
MASK_DEV = 64
MAXM = 128

EPSILON = 1e-05
NEGATIVE = -1e30
AXES = ("dp", "fsdp")


def to_low(values):
    return values.astype(jnp.bfloat16)


def to_full(values):
    return values.astype(jnp.float32)


def layer_norm(values, gain_vector, shift_vector):
    center = values - jnp.mean(values, axis=-1, keepdims=True)
    spread = jnp.mean(center * center, axis=-1, keepdims=True)
    return center * lax.rsqrt(spread + EPSILON) * gain_vector + shift_vector


def gelu_exact(values):
    return jax.nn.gelu(values, approximate=False)


def head_tail(dense_out, gain_vector, shift_vector):
    return layer_norm(gelu_exact(dense_out), gain_vector, shift_vector)


def matmul(left_side, right_side):
    return jnp.dot(left_side, right_side, preferred_element_type=jnp.float32)


def matmul_tn(left_side, right_side):
    return lax.dot_general(
        left_side, right_side, (((0,), (0,)), ((), ())), preferred_element_type=jnp.float32
    )


def matmul_nt(left_side, right_side):
    return lax.dot_general(
        left_side, right_side, (((1,), (1,)), ((), ())), preferred_element_type=jnp.float32
    )


def column_blocks(matrix, width):
    return [matrix[:, k : k + width] for k in range(0, matrix.shape[1], width)]


def gelu_parts(values):
    size = jnp.abs(values) * 0.7071067811865476
    ratio = 1.0 / (1.0 + 0.3275911 * size)
    bell = jnp.exp(-0.5 * values * values)
    series = 1.421413741 + ratio * (-1.453152027 + ratio * 1.061405429)
    series = ratio * (0.254829592 + ratio * (-0.284496736 + ratio * series))
    tail = 0.5 * series * bell
    below = jnp.where(values < 0, tail, 1.0 - tail)
    return values * below, below + values * bell * 0.3989422804014327


def flat_rows(value):
    return value.reshape(-1, value.shape[-1])


def whole(array):
    return pl.BlockSpec(array.shape, lambda *_: (0,) * array.ndim)


class Weights:
    def __init__(self, arrays, shares):
        self.arrays = arrays
        self.starts = [sum(shares[:k]) for k in range(len(shares))]
        self.shares = shares

    def natural(self, index, core):
        span = slice(self.starts[index], self.starts[index] + self.shares[index])
        pieces = [array[:, span] for array in self.arrays]
        if len(pieces) == 2:
            pieces = [jnp.stack(in_order(*pieces, core), axis=1)]
        return flat_rows(pieces[0].reshape(-1, *pieces[0].shape[-2:]))

    def operands(self, index, core, columns, column_map, parts=1, part_map=lambda *_: 0):
        share, start = self.shares[index], self.starts[index]
        if share % 8 or start % share:
            array = self.natural(index, core)
            rows = array.shape[0] // parts
            spec = pl.BlockSpec((rows, columns), lambda *i: (part_map(*i), column_map(*i)))
            return [array], [spec]
        place = start // share
        specs = [
            pl.BlockSpec(
                (array.shape[0] // parts, share, columns),
                lambda *i: (part_map(*i), place, column_map(*i)),
            )
            for array in self.arrays
        ]
        return list(self.arrays), specs


def up_operands_of(weights, steps):
    share = weights.shares[0]
    width = weights.arrays[0].shape[-1]
    if share % 8:
        array = jnp.concatenate([weights.natural(k, None) for k in range(steps)], axis=1)
        return [array], [pl.BlockSpec((array.shape[0], width), lambda s, *_: (0, s))]
    array = weights.arrays[0]
    return [array], [pl.BlockSpec((array.shape[0], share, width), lambda s, *_: (0, s, 0))]


def in_order(mine, other, core):
    return jnp.where(core == 0, mine, other), jnp.where(core == 0, other, mine)


def read_weight(refs, core):
    if len(refs) == 1:
        return flat_rows(refs[0][...])
    return flat_rows(jnp.stack(in_order(refs[0][...], refs[1][...], core), axis=1))


def pack_kernel(*refs, layout):
    *sources, out_ref = refs
    for source, (column, row, rows, columns) in zip(sources, layout):
        for k in range(column):
            out_ref[row[k] : row[k] + rows, :] = source[:, k * columns : (k + 1) * columns]


def pack_rows(pieces):
    width = pieces[0][0].shape[1] // len(pieces[0][1])
    total = max(row + m.shape[0] for m, rows in pieces for row in rows)
    if any(row % 8 for _, rows in pieces for row in rows):
        placed = sorted(
            (row, m[:, k * width : (k + 1) * width])
            for m, rows in pieces
            for k, row in enumerate(rows)
        )
        return jnp.concatenate([block for _, block in placed], axis=0)
    matrices = [m for m, _ in pieces]
    layout = [(len(rows), tuple(rows), m.shape[0], width) for m, rows in pieces]
    return pl.pallas_call(
        functools.partial(pack_kernel, layout=layout),
        grid=(1,),
        in_specs=[whole(m) for m in matrices],
        out_specs=pl.BlockSpec((total, width), lambda i: (0, 0)),
        out_shape=jax.ShapeDtypeStruct((total, width), matrices[0].dtype),
        name="pack_rows",
    )(*matrices)


def pack_later_kernel(flags_ref, targets_ref, *refs, layout, label_place):
    *sources, out_ref = refs
    pack_kernel(*sources, out_ref, layout=layout)
    count = flags_ref.shape[1]
    flags = jnp.broadcast_to(flags_ref[...], (8, count))
    row = lax.broadcasted_iota(jnp.int32, (count, count), 0)
    column = lax.broadcasted_iota(jnp.int32, (count, count), 1)
    until = to_low(jnp.where(row <= column, 1.0, 0.0))
    rank = matmul(to_low(flags.astype(jnp.float32)), until)[:1] - 1.0
    slot = lax.broadcasted_iota(jnp.int32, (MAXM, count), 0).astype(jnp.float32)
    picker = to_low(jnp.where((slot == rank) & (flags_ref[...] > 0), 1.0, 0.0))
    shifted = targets_ref[...] + 1
    high = lax.shift_right_logical(shifted, 8)
    level = lax.broadcasted_iota(jnp.int32, (8, count), 0)
    halves = jnp.where(level == 0, high, jnp.where(level == 1, shifted - high * 256, 0))
    labels = matmul_nt(to_low(halves.astype(jnp.float32)), picker)
    empty = jnp.zeros((8, out_ref.shape[1] - MAXM), jnp.float32)
    out_ref[label_place : label_place + 8, :] = to_low(jnp.concatenate([labels, empty], axis=1))


def pack_later(pieces, mask_flags, targets):
    width = pieces[0][0].shape[1] // len(pieces[0][1])
    label_place = max(row + m.shape[0] for m, rows in pieces for row in rows)
    if any(row % 8 for _, rows in pieces for row in rows) or label_place % 8:
        rank = jnp.cumsum(mask_flags) - 1
        picker = (jnp.arange(MAXM)[:, None] == rank[None, :]) & (mask_flags > 0)[None, :]
        shifted = jnp.sum(jnp.where(picker, targets[None, :] + 1, 0), axis=1)
        labels = jnp.stack([shifted // 256, shifted % 256]).astype(jnp.bfloat16)
        labels = jnp.pad(labels, ((0, 6), (0, width - MAXM)))
        return pack_rows([*pieces, (labels, [label_place])])
    matrices = [m for m, _ in pieces]
    layout = [(len(rows), tuple(rows), m.shape[0], width) for m, rows in pieces]
    operands = [mask_flags[None], targets[None], *matrices]
    return pl.pallas_call(
        functools.partial(pack_later_kernel, layout=layout, label_place=label_place),
        grid=(1,),
        in_specs=[whole(operand) for operand in operands],
        out_specs=pl.BlockSpec((label_place + 8, width), lambda i: (0, 0)),
        out_shape=jax.ShapeDtypeStruct((label_place + 8, width), matrices[0].dtype),
        name="pack_later",
    )(*operands)


def place_kernel(index, line_ref, out_ref, *, plan):
    rows, width = out_ref.shape
    device = index[0]
    line = jnp.broadcast_to(line_ref[...], (8, width))
    lane = lax.broadcasted_iota(jnp.int32, (rows, width), 1)
    level = lax.broadcasted_iota(jnp.int32, (rows, width), 0)
    out = jnp.zeros((rows, width), jnp.float32)
    for first_row, start, share in plan:
        spot = device * share
        row, place = first_row + spot // width, spot % width
        moved = pltpu.roll(line, lax.rem(place - start + width, width), 1)
        here = (level == row) & (lane >= place) & (lane < place + share)
        out = jnp.where(here, jnp.broadcast_to(moved[:1], (rows, width)), out)
    out_ref[...] = out.astype(out_ref.dtype)


def place_shares(device, vectors, first_rows, rows, width):
    plan = []
    line = 0.0
    start = 0
    for vector, first_row in zip(vectors, first_rows):
        end = start + vector.shape[0]
        plan.append((first_row, start, vector.shape[0]))
        line = line + jnp.pad(to_full(vector), (start, width - end))
        start = end
    line = line[None, :]
    return pl.pallas_call(
        functools.partial(place_kernel, plan=plan),
        grid_spec=pltpu.PrefetchScalarGridSpec(
            num_scalar_prefetch=1,
            grid=(1,),
            in_specs=[whole(line)],
            out_specs=pl.BlockSpec((rows, width), lambda i, d: (0, 0)),
        ),
        out_shape=jax.ShapeDtypeStruct((rows, width), jnp.bfloat16),
        name="place_shares",
    )(device.reshape(1), line)


def double(value, stride, axis):
    chips = lax.axis_size("dp")
    bit = (lax.axis_index("dp") // stride) % 2
    arrived = lax.ppermute(value, "dp", [(chip, chip ^ stride) for chip in range(chips)])
    low, high = in_order(value, arrived, bit)
    return jnp.stack([low, high], axis=axis)


def gather_pair(value, split):
    chips = lax.axis_size("dp")
    stride = 4
    value = value[None]
    while stride < chips:
        value = double(value, stride, 0)
        value = value.reshape(-1, *value.shape[2:])
        stride *= 2
    upper, lower = value[:, :split], value[:, split:]
    upper, lower = double(upper, 1, 1), double(lower, 2, 1)
    upper, lower = double(upper, 2, 1), double(lower, 1, 2)
    upper, lower = (part.reshape(chips, *part.shape[-2:]) for part in (upper, lower))
    swap = [(0, 1), (1, 0)]
    return (upper, lax.ppermute(upper, "fsdp", swap)), (lower, lax.ppermute(lower, "fsdp", swap))


def attention_kernel(core, *refs, sizes):
    ends = [0]
    for size in sizes:
        ends.append(ends[-1] + size)
    weights = [refs[ends[k] : ends[k + 1]] for k in range(len(sizes))]
    (tokens_ref, bias_ref, vector_ref, down_ref, across_ref) = refs[ends[-1] : ends[-1] + 5]
    (q_ref, k_ref, v_ref, context_ref, total_ref, summed_ref, hidden_ref) = refs[ends[-1] + 5 : -2]
    mask_ref, all_ref = refs[-2:]
    step = pl.program_id(0)

    @pl.when(step == 0)
    def _():
        mask_ref[...] = jnp.where(down_ref[...] == across_ref[...], 0.0, NEGATIVE)

    tokens = tokens_ref[...]
    queries = to_low(matmul(tokens, read_weight(weights[0], core[0])) + bias_ref[0:1, :])
    keys = to_low(matmul(tokens, read_weight(weights[1], core[0])))
    values = to_low(matmul(tokens, read_weight(weights[2], core[0])) + bias_ref[1:2, :])
    q_ref[...], k_ref[...], v_ref[...] = queries, keys, values
    heads = queries.shape[1] // HEAD_DIM
    pair_width = 2 * HEAD_DIM
    lane = lax.broadcasted_iota(jnp.int32, (1, pair_width), 1)
    for pair in range(heads // 2):
        span = slice(pair_width * pair, pair_width * (pair + 1))
        scaled = to_full(queries[:, span]) * HEAD_DIM ** (-0.5)
        sides = []
        for side in range(2):
            mine = to_low(jnp.where((lane < HEAD_DIM) == (side == 0), scaled, 0.0))
            scores = matmul_nt(keys[:, span], mine) + mask_ref[...]
            peak = jnp.max(scores, axis=0, keepdims=True)
            exponent = jnp.exp(scores - peak)
            total = jnp.sum(exponent, axis=0, keepdims=True)
            total_ref[pl.ds(step * heads + 2 * pair + side, 1), :] = peak + jnp.log(total)
            softmax_low = to_low(exponent * (1.0 / total))
            mixed = matmul_tn(values[:, span], softmax_low)
            sides.append(mixed[HEAD_DIM * side : HEAD_DIM * (side + 1)])
        context = to_low(jnp.concatenate(sides, axis=0).T)
        context_ref[:, span] = context
        all_ref[step * (heads // 2) + pair] = context

    @pl.when(step == pl.num_programs(0) - 1)
    def _():
        pairs = all_ref.shape[0]
        context = jnp.concatenate([all_ref[k] for k in range(pairs)], axis=1)
        product = matmul(context, read_weight(weights[3], core[0]))
        summed = to_full(tokens_ref[...]) + product + vector_ref[2:3, :]
        summed_ref[...] = summed
        hidden_ref[...] = to_low(layer_norm(summed, vector_ref[3:4, :], vector_ref[4:5, :]))


def attention_forward(core, tokens, segments, weights, vectors):
    rows, width = tokens.shape
    columns = 256
    arrays, specs, sizes = [], [], []
    for k, (group, index) in enumerate(weights):
        size, place = (columns, lambda s, c: s) if k < 3 else (width, lambda s, c: 0)
        some, their = group.operands(index, core, size, place)
        arrays, specs, sizes = arrays + some, specs + their, sizes + [len(some)]
    down, across = segments[:, None], segments[None, :]
    block = pl.BlockSpec((rows, columns), lambda s, c: (0, s))
    head_rows = 16
    return pl.pallas_call(
        functools.partial(attention_kernel, sizes=sizes),
        grid_spec=pltpu.PrefetchScalarGridSpec(
            num_scalar_prefetch=1,
            grid=(width // columns,),
            in_specs=[
                *specs,
                whole(tokens),
                pl.BlockSpec((8, columns), lambda s, c: (0, s)),
                whole(vectors),
                whole(down),
                whole(across),
            ],
            out_specs=[
                block,
                block,
                block,
                block,
                pl.BlockSpec((head_rows, rows), lambda s, c: (0, 0)),
                whole(tokens),
                whole(tokens),
            ],
            scratch_shapes=[
                pltpu.VMEM((rows, rows), jnp.float32),
                pltpu.VMEM((width // (2 * HEAD_DIM), rows, 2 * HEAD_DIM), jnp.bfloat16),
            ],
        ),
        out_shape=[
            *[jax.ShapeDtypeStruct((rows, width), jnp.bfloat16)] * 4,
            jax.ShapeDtypeStruct((head_rows, rows), jnp.float32),
            jax.ShapeDtypeStruct((rows, width), jnp.float32),
            jax.ShapeDtypeStruct((rows, width), jnp.bfloat16),
        ],
        compiler_params=pltpu.CompilerParams(dimension_semantics=("arbitrary",)),
        name="attention_forward",
    )(core.reshape(1), *arrays, tokens, vectors, vectors, down, across)


def ffn_kernel(*refs, sizes):
    up_refs, down_refs = refs[: sizes[0]], refs[sizes[0] : sum(sizes)]
    hidden_ref, bias_ref, vector_ref = refs[sum(sizes) : sum(sizes) + 3]
    active_ref, slope_ref, summed_ref, output_ref, total_ref = refs[sum(sizes) + 3 :]
    step = pl.program_id(0)
    up, down = read_weight(up_refs, None), read_weight(down_refs, None)
    pre_act = matmul(hidden_ref[...], up) + bias_ref[pl.ds(step, 1), :]
    active, slope = gelu_parts(pre_act)
    active = to_low(active)
    active_ref[...] = active
    slope_ref[...] = slope
    part = matmul(active, down)

    @pl.when(step == 0)
    def _():
        total_ref[...] = part

    @pl.when(step > 0)
    def _():
        total_ref[...] += part

    @pl.when(step == pl.num_programs(0) - 1)
    def _():
        summed = to_full(hidden_ref[...]) + total_ref[...] + vector_ref[5:6, :]
        summed_ref[...] = summed
        output_ref[...] = to_low(layer_norm(summed, vector_ref[6:7, :], vector_ref[7:8, :]))


def ffn_forward(hidden, weights, up_bias, vectors):
    rows, width = hidden.shape
    steps = len(weights.shares) - 2
    first, first_specs = up_operands_of(weights, steps)
    second, second_specs = weights.operands(steps, None, width, lambda s: 0, steps, lambda s: s)
    block = pl.BlockSpec((rows, width), lambda s: (0, s))
    return pl.pallas_call(
        functools.partial(ffn_kernel, sizes=[len(first), len(second)]),
        grid=(steps,),
        in_specs=[*first_specs, *second_specs, whole(hidden), whole(up_bias), whole(vectors)],
        out_specs=[block, block, whole(hidden), whole(hidden)],
        out_shape=[
            jax.ShapeDtypeStruct((rows, steps * width), jnp.bfloat16),
            jax.ShapeDtypeStruct((rows, steps * width), jnp.float32),
            jax.ShapeDtypeStruct((rows, width), jnp.float32),
            jax.ShapeDtypeStruct((rows, width), jnp.bfloat16),
        ],
        scratch_shapes=[pltpu.VMEM((rows, width), jnp.float32)],
        compiler_params=pltpu.CompilerParams(dimension_semantics=("arbitrary",)),
        name="ffn_forward",
    )(*first, *second, hidden, up_bias, vectors)


def head_kernel(*refs, size):
    weight_refs = refs[:size]
    picker_ref, output_ref, vector_ref, own_ref, dense_ref, normed_ref = refs[size:]
    own = to_low(matmul(picker_ref[...], output_ref[...]))
    own_ref[...] = own
    dense = matmul(own, read_weight(weight_refs, None)) + vector_ref[4:5, :]
    dense_ref[...] = dense
    active = gelu_parts(dense)[0]
    normed_ref[...] = to_low(layer_norm(active, vector_ref[5:6, :], vector_ref[6:7, :]))


def head_forward(picker, output, group, index, vectors):
    slots, width = picker.shape[0], output.shape[1]
    arrays, specs = group.operands(index, None, width, lambda s: 0)
    operands = [picker, output, vectors]
    out_shape = [
        jax.ShapeDtypeStruct((slots, width), kind)
        for kind in (jnp.bfloat16, jnp.float32, jnp.bfloat16)
    ]
    return pl.pallas_call(
        functools.partial(head_kernel, size=len(arrays)),
        grid=(1,),
        in_specs=[*specs, *[whole(operand) for operand in operands]],
        out_specs=[whole(shape) for shape in out_shape],
        out_shape=out_shape,
        name="head_forward",
    )(*arrays, *operands)


def norm_backward(summed, gain_row, grad):
    center = summed - jnp.mean(summed, axis=-1, keepdims=True)
    scale = lax.rsqrt(jnp.mean(center * center, axis=-1, keepdims=True) + EPSILON)
    unit = center * scale
    inner = grad * gain_row
    mean = jnp.mean(inner, axis=-1, keepdims=True)
    along = jnp.mean(inner * unit, axis=-1, keepdims=True)
    gain_grad = jnp.sum(grad * unit, axis=0, keepdims=True)
    shift_grad = jnp.sum(grad, axis=0, keepdims=True)
    return scale * (inner - mean - unit * along), gain_grad, shift_grad


def feed_back_kernel(place, *refs, sizes, share, down_share):
    up_refs, down_refs = refs[: sizes[0]], refs[sizes[0] : sum(sizes)]
    (cotangent_ref, picker_ref, picked_ref, summed_ref, vector_ref, own_ref, dense_ref) = refs[
        sum(sizes) : sum(sizes) + 7
    ]
    hidden_ref, active_ref, slope_ref, total_ref, sums_ref, *outs = refs[sum(sizes) + 7 : -2]
    low_ref, turned_ref = refs[-2:]
    step = pl.program_id(0)
    width = vector_ref.shape[1]

    @pl.when(step == 0)
    def _():
        grad = to_full(cotangent_ref[...]) + matmul_tn(picker_ref[...], picked_ref[...])
        summed_grad, gain_grad, shift_grad = norm_backward(
            summed_ref[...], vector_ref[6:7, :], grad
        )
        total_ref[...] = summed_grad
        low = to_low(summed_grad)
        low_ref[...] = low
        turned_ref[...] = hidden_ref[...].T
        sums_ref[...] = jnp.zeros_like(sums_ref)
        sums_ref[0:1, :] = jnp.sum(to_full(low), axis=0, keepdims=True)
        sums_ref[1:2, :] = gain_grad
        sums_ref[2:3, :] = shift_grad
        dense_grad = to_low(matmul_tn(own_ref[...], dense_ref[...]))
        if down_share:
            store_blocks(outs, dense_grad, place, share, slice(2 * down_share, None))
        else:
            outs[2][...] = dense_grad

    low = low_ref[...]
    up, down = read_weight(up_refs, None), read_weight(down_refs, None)
    down_grad = to_low(matmul_tn(active_ref[...], low))
    pre_grad = to_low(matmul_nt(low, down) * slope_ref[...])
    total_ref[...] += matmul_nt(pre_grad, up)
    sums_ref[pl.ds(3 + step, 1), :] = jnp.sum(to_full(pre_grad), axis=0, keepdims=True)
    up_grad = to_low(matmul(turned_ref[...], pre_grad))
    if down_share:
        chips = width // (2 * down_share)
        rows = slice(down_share, 2 * down_share)
        store_blocks(outs, down_grad, place, down_share, rows, step * chips)
        rows = pl.ds(pl.multiple_of(step * share, share), share)
        store_blocks(outs, up_grad, place, share, rows)
    else:
        outs[0][...] = up_grad
        outs[1][...] = down_grad


def feed_backward(place, count, cotangent, picker, picked_grad, summed, vectors, own, dense, hidden, active, slope, weights):
    rows, width = cotangent.shape
    steps = active.shape[1] // width
    share, down_share, chips = width // count, active.shape[1] // count, count // 2
    aligned = share % 8 == 0
    first, first_specs = up_operands_of(weights, steps)
    second, second_specs = weights.operands(steps, None, width, lambda s, c: 0, steps, lambda s, c: s)
    operands = [cotangent, picker, picked_grad, summed, vectors, own, dense, hidden]
    block = pl.BlockSpec((rows, width), lambda s, c: (0, s))
    low = jnp.bfloat16
    if aligned:
        shape = jax.ShapeDtypeStruct((chips, 2 * down_share + share, width // 2), low)
        out_shape, out_specs = [shape] * 4, [whole(shape)] * 4
    else:
        out_shape = [
            jax.ShapeDtypeStruct((width, steps * width), low),
            jax.ShapeDtypeStruct((steps * width, width), low),
            jax.ShapeDtypeStruct((width, width), low),
        ]
        out_specs = [
            pl.BlockSpec((width, width), lambda s, c: (0, s)),
            pl.BlockSpec((width, width), lambda s, c: (s, 0)),
            whole(out_shape[2]),
        ]
    common = [
        jax.ShapeDtypeStruct((rows, width), jnp.float32),
        jax.ShapeDtypeStruct((8, width), jnp.float32),
    ]
    kernel = functools.partial(
        feed_back_kernel,
        sizes=[len(first), len(second)],
        share=share,
        down_share=down_share if aligned else 0,
    )
    hidden_grad, sums, *outs = pl.pallas_call(
        kernel,
        grid_spec=pltpu.PrefetchScalarGridSpec(
            num_scalar_prefetch=1,
            grid=(steps,),
            in_specs=[
                *first_specs,
                *second_specs,
                *[whole(operand) for operand in operands],
                block,
                block,
            ],
            out_specs=[*[whole(shape) for shape in common], *out_specs],
            scratch_shapes=[pltpu.VMEM((rows, width), low), pltpu.VMEM((width, rows), low)],
        ),
        out_shape=[*common, *out_shape],
        compiler_params=pltpu.CompilerParams(dimension_semantics=("arbitrary",)),
        name="feed_backward",
    )(place, *first, *second, *operands, active, slope)
    if not aligned:
        away, kept = arranged([*column_blocks(outs[0], width), *outs[1:]], place)
    else:
        away, kept = outs[:2], outs[2:]
    return hidden_grad, sums, away, kept


def out_back_kernel(core, *refs, size):
    weight_refs = refs[:size]
    grad_ref, summed_ref, vector_ref, total_ref, low_ref, back_ref, sums_ref = refs[size:]
    width = vector_ref.shape[1]
    summed_grad, gain_grad, shift_grad = norm_backward(
        summed_ref[...], vector_ref[3:4, :], grad_ref[...]
    )
    total_ref[...] = summed_grad
    low = to_low(summed_grad)
    low_ref[...] = low
    bias_grad = jnp.sum(to_full(low), axis=0, keepdims=True)
    zero = jnp.zeros((5, width), jnp.float32)
    sums_ref[...] = jnp.concatenate([bias_grad, gain_grad, shift_grad, zero], axis=0)
    back_ref[...] = to_low(matmul_nt(low, read_weight(weight_refs, core[0])))


def out_backward(core, hidden_grad, summed, vectors, group, index):
    rows, width = hidden_grad.shape
    arrays, specs = group.operands(index, core, width, lambda s, c: 0)
    operands = [hidden_grad, summed, vectors]
    out_shape = [
        jax.ShapeDtypeStruct((rows, width), jnp.float32),
        jax.ShapeDtypeStruct((rows, width), jnp.bfloat16),
        jax.ShapeDtypeStruct((rows, width), jnp.bfloat16),
        jax.ShapeDtypeStruct((8, width), jnp.float32),
    ]
    return pl.pallas_call(
        functools.partial(out_back_kernel, size=len(arrays)),
        grid_spec=pltpu.PrefetchScalarGridSpec(
            num_scalar_prefetch=1,
            grid=(1,),
            in_specs=[*specs, *[whole(operand) for operand in operands]],
            out_specs=[whole(shape) for shape in out_shape],
        ),
        out_shape=out_shape,
        name="out_backward",
    )(core.reshape(1), *arrays, *operands)


def attention_back_kernel(*refs, first_head):
    (grad_ref, q_ref, k_ref, v_ref, total_ref, down_ref, across_ref) = refs[:7]
    dq_ref, dk_ref, dv_ref, sums_ref, mask_ref = refs[7:]
    step = pl.program_id(0)

    @pl.when(step == 0)
    def _():
        mask_ref[...] = jnp.where(down_ref[...] == across_ref[...], 0.0, NEGATIVE)

    pair_width = 2 * HEAD_DIM
    scale = HEAD_DIM ** (-0.5)
    lane = lax.broadcasted_iota(jnp.int32, (1, pair_width), 1)
    columns = q_ref.shape[1]
    heads = columns // HEAD_DIM
    for pair in range(heads // 2):
        span = slice(pair_width * pair, pair_width * (pair + 1))
        queries, keys, values = q_ref[:, span], k_ref[:, span], v_ref[:, span]
        grads = grad_ref[:, span]
        scaled = to_full(queries) * scale
        sides = []
        for side in range(2):
            here = (lane < HEAD_DIM) == (side == 0)
            mine = to_low(jnp.where(here, scaled, 0.0))
            my_grads = jnp.where(here, grads, jnp.zeros_like(grads))
            head = first_head + step * heads + 2 * pair + side
            scores = matmul_nt(keys, mine) + mask_ref[...]
            softmax = jnp.exp(scores - total_ref[pl.ds(head, 1), :])
            softmax_grad = matmul_nt(values, my_grads)
            inner = jnp.sum(softmax * softmax_grad, axis=0, keepdims=True)
            score_grad = to_low(softmax * (softmax_grad - inner))
            query_grad = matmul_tn(keys, score_grad)[HEAD_DIM * side : HEAD_DIM * (side + 1)]
            sides.append((query_grad, matmul(score_grad, mine), matmul(to_low(softmax), my_grads)))
        query_grad = to_low(jnp.concatenate([sides[0][0], sides[1][0]], axis=0).T * scale)
        value_grad = to_low(sides[0][2] + sides[1][2])
        dq_ref[:, span] = query_grad
        dk_ref[:, span] = to_low(sides[0][1] + sides[1][1])
        dv_ref[:, span] = value_grad
        sums_ref[0:1, span] = jnp.sum(to_full(query_grad), axis=0, keepdims=True)
        sums_ref[1:2, span] = jnp.sum(to_full(value_grad), axis=0, keepdims=True)


def attention_backward(context_grad, queries, keys, values, score_total, segments, start, columns):
    rows = context_grad.shape[0]
    size = 2 * HEAD_DIM
    down, across = segments[:, None], segments[None, :]
    block = pl.BlockSpec((rows, size), lambda s: (0, start // size + s))
    out_block = pl.BlockSpec((rows, size), lambda s: (0, s))
    return pl.pallas_call(
        functools.partial(attention_back_kernel, first_head=start // HEAD_DIM),
        grid=(columns // size,),
        in_specs=[*[block] * 4, whole(score_total), whole(down), whole(across)],
        out_specs=[*[out_block] * 3, pl.BlockSpec((8, size), lambda s: (0, s))],
        out_shape=[
            *[jax.ShapeDtypeStruct((rows, columns), jnp.bfloat16)] * 3,
            jax.ShapeDtypeStruct((8, columns), jnp.float32),
        ],
        scratch_shapes=[pltpu.VMEM((rows, rows), jnp.float32)],
        compiler_params=pltpu.CompilerParams(dimension_semantics=("arbitrary",)),
        name="attention_backward",
    )(context_grad, queries, keys, values, score_total, down, across)


def joined_sums(bias_sums, out_sums, feed_sums, head_sums, steps):
    return jnp.concatenate(
        [
            jnp.concatenate([part[:2] for part in bias_sums], axis=1),
            out_sums[:3],
            feed_sums[: 3 + steps],
            head_sums[: 8 - steps],
        ],
        axis=0,
    )


def last_grads_kernel(place, *refs, parts, share, steps):
    tokens_ref, context_ref, branch_ref, out_sums_ref, feed_sums_ref, head_sums_ref, *rest = refs
    mixed_refs, rest = rest[: 3 * parts], rest[3 * parts :]
    bias_refs, outs = rest[:parts], rest[parts:]
    turned = tokens_ref[...].T
    for which in range(3):
        for part in range(parts):
            mixed = mixed_refs[3 * part + which][...]
            columns = mixed.shape[1]
            grad = to_low(matmul(turned, mixed))
            if share:
                rows = slice(share * which, share * (which + 1))
                store_blocks(outs, grad, place, share, rows, column=columns * part)
            else:
                outs[which][:, columns * part : columns * (part + 1)] = grad
    grad = to_low(matmul_tn(context_ref[...], branch_ref[...]))
    if share:
        store_blocks(outs, grad, place, share, slice(3 * share, 4 * share))
        small = to_low(
            joined_sums(
                [ref[...] for ref in bias_refs],
                out_sums_ref[...],
                feed_sums_ref[...],
                head_sums_ref[...],
                steps,
            )
        )
        half = small.shape[1] // 2
        for index, out_ref in enumerate(outs):
            part = small[:, half * (index % 2) : half * (index % 2 + 1)]
            out_ref[:, 4 * share :, :] = jnp.broadcast_to(
                part[None], (out_ref.shape[0], *part.shape)
            )
    else:
        outs[3][...] = grad


def last_grads(place, count, tokens, context, branch_grad, sums, steps, mixed):
    width = tokens.shape[1]
    share, chips = width // count, count // 2
    aligned = share % 8 == 0
    parts = len(mixed)
    biases = [part[3] for part in mixed]
    mixed = [part[:3] for part in mixed]
    operands = [tokens, context, branch_grad, *sums, *[m for part in mixed for m in part], *biases]
    small = joined_sums(biases, *sums, steps)
    if aligned:
        rows = 4 * share + small.shape[0]
        out_shape = [jax.ShapeDtypeStruct((chips, rows, width // 2), jnp.bfloat16)] * 4
    else:
        out_shape = [jax.ShapeDtypeStruct((width, width), jnp.bfloat16)] * 4
    outs = pl.pallas_call(
        functools.partial(
            last_grads_kernel, parts=parts, share=share if aligned else 0, steps=steps
        ),
        grid_spec=pltpu.PrefetchScalarGridSpec(
            num_scalar_prefetch=1,
            grid=(1,),
            in_specs=[whole(operand) for operand in operands],
            out_specs=[whole(shape) for shape in out_shape],
        ),
        out_shape=out_shape,
        name="last_grads",
    )(place, *operands)
    if not aligned:
        both = jnp.broadcast_to(to_low(small)[None], (count, *small.shape))
        return arranged([*outs, both.reshape(-1, width)], place)
    return outs[:2], outs[2:]


def tokens_back_kernel(core, *refs, sizes, parts):
    ends = [sum(sizes[:k]) for k in range(4)]
    weights = [refs[ends[k] : ends[k + 1]] for k in range(3)]
    summed_ref, *mixed_refs, out_ref = refs[ends[3] :]
    total = summed_ref[...]
    for which in range(3):
        weight = read_weight(weights[which], core[0])
        for part in range(parts):
            mixed = mixed_refs[3 * part + which][...]
            columns = mixed.shape[1]
            total += matmul_nt(mixed, weight[:, columns * part : columns * (part + 1)])
    out_ref[...] = total


def tokens_backward(core, summed_grad, mixed, weights):
    width = summed_grad.shape[1]
    arrays, specs, sizes = [], [], []
    for group, index in weights:
        some, their = group.operands(index, core, width, lambda s, c: 0)
        arrays, specs, sizes = arrays + some, specs + their, sizes + [len(some)]
    operands = [summed_grad, *[matrix for part in mixed for matrix in part]]
    return pl.pallas_call(
        functools.partial(tokens_back_kernel, sizes=sizes, parts=len(mixed)),
        grid_spec=pltpu.PrefetchScalarGridSpec(
            num_scalar_prefetch=1,
            grid=(1,),
            in_specs=[*specs, *[whole(operand) for operand in operands]],
            out_specs=whole(summed_grad),
        ),
        out_shape=jax.ShapeDtypeStruct(summed_grad.shape, jnp.float32),
        name="tokens_backward",
    )(core.reshape(1), *arrays, *operands)


def take_kernel(index, whole_ref, *out_refs, plan):
    width = whole_ref.shape[1]
    for out_ref, (first_row, share) in zip(out_refs, plan):
        spot = index[0] * share
        row, place = first_row + spot // width, spot % width
        line = jnp.broadcast_to(whole_ref[pl.ds(row, 1), :], (8, width))
        moved = pltpu.roll(line, lax.rem(width - place, width), 1)
        out_ref[...] = moved[:1, :share]


def take_shares(device, values, first_rows, shares):
    shapes = [jax.ShapeDtypeStruct((1, share), jnp.float32) for share in shares]
    lines = pl.pallas_call(
        functools.partial(take_kernel, plan=list(zip(first_rows, shares))),
        grid_spec=pltpu.PrefetchScalarGridSpec(
            num_scalar_prefetch=1,
            grid=(1,),
            in_specs=[whole(values)],
            out_specs=[whole(shape) for shape in shapes],
        ),
        out_shape=shapes,
        name="take_shares",
    )(device.reshape(1), values)
    return [line[0] for line in lines]


def take(value, axis, index):
    return lax.dynamic_index_in_dim(value, index, axis, keepdims=False)


def add_low(first, second):
    return to_low(to_full(first) + to_full(second))


def halve(value, axis, stride):
    chips = lax.axis_size("dp")
    bit = (lax.axis_index("dp") // stride) % 2
    pairs = [(chip, chip ^ stride) for chip in range(chips)]
    arrived = lax.ppermute(take(value, axis, 1 - bit), "dp", pairs)
    return add_low(take(value, axis, bit), arrived)


def core_swap(away):
    return lax.ppermute(away, "fsdp", [(0, 1), (1, 0)])


def along(sent, stride):
    chips = lax.axis_size("dp")
    return lax.ppermute(sent, "dp", [(chip, chip ^ stride) for chip in range(chips)])


def total_of(addends):
    total = to_full(addends[0])
    for addend in addends[1:]:
        total = total + to_full(addend)
    return total


def my_place():
    chip = lax.axis_index("dp")
    return jnp.stack([lax.axis_index("fsdp"), chip % 2, (chip // 2) % 2, chip // 4])


def chip_at(index, place, levels, first_axis):
    outer, level = index // levels, index % levels
    bits = (outer // 2, outer % 2) if first_axis == 0 else (outer % 2, outer // 2)
    return ((place[3] ^ level) * 2 + (place[2] ^ bits[1])) * 2 + (place[1] ^ bits[0])


def index_of(chip, place, levels, first_axis):
    bits = ((chip % 2) ^ place[1], ((chip // 2) % 2) ^ place[2])
    outer = 2 * bits[first_axis] + bits[1 - first_axis]
    return outer * levels + ((chip // 4) ^ place[3])


class ChipSum:
    def __init__(self, away, kept):
        self.sides = [[part] for part in kept]
        self.strides = [[1, 2], [2, 1]]
        self.arrived = [core_swap(part) for part in away]

    def add(self, arrived):
        for side, part in zip(self.sides, arrived):
            side.append(part)

    def sends(self):
        sent = [to_low(total_of([a[a.shape[0] // 2 :] for a in side])) for side in self.sides]
        self.sides = [[a[: a.shape[0] // 2] for a in side] for side in self.sides]
        return sent

    def start(self, sent):
        self.arrived = [along(part, strides.pop(0)) for part, strides in zip(sent, self.strides)]

    def level_block(self, level):
        return jnp.concatenate(
            [total_of([a[level] for a in side]) for side in self.sides], axis=-1
        )

    def level_sends(self):
        while self.sides[0][0].shape[0] > 4:
            stride = 4 * (self.sides[0][0].shape[0] // 2)
            sent = self.sends()
            self.add([along(part, stride) for part in sent])
        levels = self.sides[0][0].shape[0]
        return [to_low(self.level_block(level)) for level in range(1, levels)]

    def start_levels(self, sent):
        self.arrived = [along(part, 4 * (level + 1)) for level, part in enumerate(sent)]

    def result(self, arrived):
        return total_of([self.level_block(0), *arrived])


def arranged(matrices, place):
    chips = lax.axis_size("dp")
    value = jnp.concatenate(
        [matrix.reshape(chips, 2, -1, matrix.shape[-1]) for matrix in matrices], axis=2
    )
    half = value.shape[-1] // 2
    sides = []
    for core in (1 - place[0], place[0]):
        mine = take(value, 1, core)
        sides.append(
            [
                jnp.take(
                    mine[..., axis * half : (axis + 1) * half],
                    chip_at(jnp.arange(chips), place, chips // 4, axis),
                    axis=0,
                )
                for axis in range(2)
            ]
        )
    return sides


def store_blocks(outs, value, place, share, rows, first_chip=0, column=0):
    columns = value.shape[-1]
    split = value.reshape(-1, 2, share, columns)
    kept, away = in_order(split[:, 0], split[:, 1], place[0])
    levels = outs[0].shape[0] // 4
    width = outs[0].shape[-1]
    for chip in range(split.shape[0]):
        for which, half in enumerate((away, kept)):
            for axis in range(2):
                low, high = max(column, axis * width), min(column + columns, (axis + 1) * width)
                if low >= high:
                    continue
                spot = index_of(first_chip + chip, place, levels, axis)
                outs[2 * which + axis][
                    pl.ds(spot, 1), rows, low - axis * width : high - axis * width
                ] = half[chip : chip + 1, :, low - column : high - column]


def tie(value, *others):
    return lax.optimization_barrier((value, *others))


def window_base(start, total, window):
    return pl.multiple_of(jnp.minimum((start // 16) * 16, total - window), 16)


def compact_kernel(place, places, counts, mine_ref, other_ref, out_ref, *, window):
    step = pl.program_id(0)

    @pl.when(step == 0)
    def _():
        out_ref[...] = jnp.zeros_like(out_ref)

    _, batch, slots, half = mine_ref.shape
    levels = pl.num_programs(0) * batch // 4
    total = out_ref.shape[0]
    for which, ref in enumerate((mine_ref, other_ref)):
        core = place[0] if which == 0 else 1 - place[0]
        for axis in range(2):
            for lane in range(batch):
                source = 2 * chip_at(step * batch + lane, place, levels, axis) + core
                start = places[source]
                base = window_base(start, total, window)
                row = lax.broadcasted_iota(jnp.int32, (window, slots), 0) + (base - start)
                column = lax.broadcasted_iota(jnp.int32, (window, slots), 1)
                chosen = jnp.where((row == column) & (column < counts[source]), 1.0, 0.0)
                moved = matmul(to_low(chosen), ref[axis, lane])
                out_ref[pl.ds(base, window), half * axis : half * (axis + 1)] += to_low(moved)


def compact(place, places, counts, mine, other, total):
    _, chips, slots, half = mine.shape
    batch = 4
    block = pl.BlockSpec((2, batch, slots, half), lambda i, *_: (0, i, 0, 0))
    return pl.pallas_call(
        functools.partial(compact_kernel, window=slots + 16),
        grid_spec=pltpu.PrefetchScalarGridSpec(
            num_scalar_prefetch=3,
            grid=(chips // batch,),
            in_specs=[block, block],
            out_specs=pl.BlockSpec((total, 2 * half), lambda i, *_: (0, 0)),
        ),
        out_shape=jax.ShapeDtypeStruct((total, 2 * half), jnp.bfloat16),
        compiler_params=pltpu.CompilerParams(dimension_semantics=("arbitrary",)),
        name="compact_rows",
    )(place, places, counts, mine, other)


def compact_labels_kernel(places, counts, lines_ref, out_ref):
    out_ref[...] = jnp.zeros_like(out_ref)
    sources, slots = lines_ref.shape
    total = out_ref.shape[1]
    wide = 2 * slots
    lane = lax.broadcasted_iota(jnp.int32, (8, wide), 1)

    def place_one(source, carry):
        start = places[source]
        base = pl.multiple_of(jnp.minimum(start // slots * slots, total - wide), slots)
        shift = start - base
        line = jnp.broadcast_to(to_full(lines_ref[pl.ds(source, 1), :]), (8, slots))
        line = jnp.concatenate([line, jnp.zeros_like(line)], axis=1)
        moved = pltpu.roll(line, lax.rem(shift, wide), 1)
        here = (lane >= shift) & (lane < shift + counts[source])
        span = pl.ds(base, wide)
        out_ref[:, span] = jnp.where(here, moved, out_ref[:, span])
        return carry

    lax.fori_loop(0, sources, place_one, 0)


def compact_labels(places, counts, lines, total):
    out = pl.pallas_call(
        compact_labels_kernel,
        grid_spec=pltpu.PrefetchScalarGridSpec(
            num_scalar_prefetch=2,
            grid=(1,),
            in_specs=[whole(lines)],
            out_specs=pl.BlockSpec((8, total), lambda *_: (0, 0)),
        ),
        out_shape=jax.ShapeDtypeStruct((8, total), jnp.float32),
        name="compact_labels",
    )(places, counts, lines)
    return out[0].astype(jnp.int32)


def gather_blocks(value, beside, given):
    chips = lax.axis_size("dp")
    levels = chips // 4
    half = value.shape[-1] // 2
    if levels <= 4:
        others = jnp.stack([along(value, 4 * level) for level in range(1, levels)])
    else:
        others = value[None]
        while others.shape[0] < levels:
            others = jnp.concatenate([others, along(others, 4 * others.shape[0])])
        others = others[1:]
    own = [value[:, :half], value[:, half:]]
    strides = [(1, 2), (2, 1)]
    near = [along(part, first) for part, (first, _) in zip(own, strides)]
    far_sent = [jnp.stack([part, got]) for part, got in zip(own, near)]
    others = tie(others, *far_sent)[0]
    far = [along(sent, second) for sent, (_, second) in zip(far_sent, strides)]
    rest = [others[..., :half], others[..., half:]]
    near_rest = [along(part, first) for part, (first, _) in zip(rest, strides)]
    given, *near_rest = tie(given, *near_rest)
    far_rest = [
        along(jnp.concatenate([part, got]), second)
        for part, got, (_, second) in zip(rest, near_rest, strides)
    ]
    result, *far_rest = tie(beside(given), *far_rest)
    count = levels - 1
    mine = jnp.stack(
        [
            jnp.concatenate(
                [
                    own[k][None],
                    rest[k],
                    far[k][:1],
                    far_rest[k][:count],
                    near[k][None],
                    near_rest[k],
                    far[k][1:],
                    far_rest[k][count:],
                ]
            )
            for k in range(2)
        ]
    )
    return mine, core_swap(mine), result


def spread_kernel(place, places, counts, rows_ref, *out_refs, window):
    step = pl.program_id(0)
    total = rows_ref.shape[0]
    batch, slots, half = out_refs[0].shape
    levels = pl.num_programs(0) * batch // 4
    for which in range(2):
        core = 1 - place[0] if which == 0 else place[0]
        for axis in range(2):
            for lane in range(batch):
                chip = chip_at(step * batch + lane, place, levels, axis)
                source = 2 * chip + core
                start = places[source]
                base = window_base(start, total, window)
                row = lax.broadcasted_iota(jnp.int32, (slots, window), 0)
                column = lax.broadcasted_iota(jnp.int32, (slots, window), 1) + (base - start)
                chosen = jnp.where((row == column) & (row < counts[source]), 1.0, 0.0)
                moved = matmul(
                    to_low(chosen), rows_ref[pl.ds(base, window), half * axis : half * (axis + 1)]
                )
                out_refs[2 * which + axis][lane] = to_low(moved)


def spread(place, places, counts, rows, slots):
    chips = places.shape[0] // 2
    total, width = rows.shape
    batch = 2
    block = pl.BlockSpec((batch, slots, width // 2), lambda i, *_: (i, 0, 0))
    shape = jax.ShapeDtypeStruct((chips, slots, width // 2), jnp.bfloat16)
    outs = pl.pallas_call(
        functools.partial(spread_kernel, window=slots + 16),
        grid_spec=pltpu.PrefetchScalarGridSpec(
            num_scalar_prefetch=3,
            grid=(chips // batch,),
            in_specs=[
                pl.BlockSpec((total, width), lambda i, *_: (0, 0), pipeline_mode=pl.Buffered(1))
            ],
            out_specs=[block] * 4,
        ),
        out_shape=[shape] * 4,
        compiler_params=pltpu.CompilerParams(dimension_semantics=("arbitrary",)),
        name="spread_rows",
    )(place, places, counts, rows)
    return outs[:2], outs[2:]


def per_device(
    tokens,
    segments,
    mask_flags,
    targets,
    cotangent,
    qkv_weight,
    attn_bias,
    out_weight,
    out_bias,
    attn_gain,
    attn_shift,
    up_weight,
    up_bias,
    down_weight,
    down_bias,
    ffn_gain,
    ffn_shift,
    dense_weight,
    dense_bias,
    head_gain,
    head_shift,
    decoder,
    vocab_bias,
):
    count = lax.axis_size(AXES)
    width = tokens.shape[1]
    core = lax.axis_index("fsdp")
    device = lax.axis_index(AXES)
    here = my_place()
    blocks = qkv_weight.shape[1] // width
    steps = up_weight.shape[1] // width
    share, up_share, down_share = out_weight.shape[0], up_weight.shape[0], down_weight.shape[0]
    label_place = up_share * steps + down_share + share
    later_packed = pack_later(
        [
            (up_weight, [up_share * k for k in range(steps)]),
            (down_weight, [up_share * steps]),
            (dense_weight, [up_share * steps + down_share]),
        ],
        mask_flags,
        targets,
    )
    later_gathered = lax.all_gather(later_packed, AXES, axis=0)
    later = Weights([later_gathered], [*[up_share] * steps, down_share, share])
    small = (
        attn_bias,
        out_bias,
        attn_gain,
        attn_shift,
        down_bias,
        ffn_gain,
        ffn_shift,
        up_bias,
        dense_bias,
        head_gain,
        head_shift,
    )
    small_rows = (0, 2, 3, 4, 5, 6, 7, 8, 12, 13, 14)
    placed = place_shares(device, small, small_rows, 16, width)
    half = 2 * share + 8
    first_packed = pack_rows(
        [
            (qkv_weight, [0, share, half]),
            (placed[:8], [2 * share]),
            (out_weight, [half + share]),
            (placed[8:], [half + 2 * share]),
        ]
    )
    upper, lower = gather_pair(first_packed, half)
    first_group, second_group = (Weights(list(pair), [share, share, 8]) for pair in (upper, lower))
    vectors, more_vectors = (
        sum(jnp.sum(to_full(array[:, 2 * share :]), axis=0) for array in pair)
        for pair in (upper, lower)
    )
    queries, keys_low, values_low, context, score_total, summed1, hidden = attention_forward(
        core,
        tokens,
        segments,
        [(first_group, 0), (first_group, 1), (second_group, 0), (second_group, 1)],
        vectors,
    )
    active, slope, summed2, output = ffn_forward(hidden, later, more_vectors[:4], vectors)
    head_gain_full, head_shift_full = more_vectors[5], more_vectors[6]
    mask_rank = jnp.cumsum(mask_flags) - 1
    slot_place = jnp.where(mask_flags > 0, mask_rank, -1)
    picker_low = (jnp.arange(MAXM)[:, None] == slot_place[None, :]).astype(jnp.bfloat16)
    own_rows, dense, normed_low = head_forward(picker_low, output, later, steps + 1, more_vectors)
    _, tail_back = jax.vjp(head_tail, dense, head_gain_full, head_shift_full)
    chips = count // 2
    group = MASK_DEV * chips
    total = 2 * group
    gathered_late, normed_low = tie(later_gathered, normed_low)
    label_parts = gathered_late[:, label_place : label_place + 2, :MAXM].astype(jnp.int32)
    label_lines = label_parts[:, 0] * 256 + label_parts[:, 1] - 1
    counts = jnp.sum((label_lines >= 0).astype(jnp.int32), axis=1)
    by_core = counts.reshape(chips, 2)
    earlier = jnp.arange(chips)[:, None] < jnp.arange(chips)[None, :]
    places = jnp.sum(jnp.where(earlier[:, :, None], by_core[:, None, :], 0), axis=0)
    places = (places + jnp.arange(2)[None, :] * group).reshape(count)
    all_labels = compact_labels(places, counts, label_lines, total)
    slice_index = lax.axis_index(AXES)
    vocab_rows = decoder.shape[0]
    local_label = all_labels - slice_index * vocab_rows
    label_hit = jnp.arange(vocab_rows)[None, :] == local_label[:, None]

    def pull_labels(chosen):
        hit = jnp.arange(vocab_rows)[None, :] == chosen[:, None]
        return to_low(matmul(hit.astype(jnp.bfloat16), decoder))

    mine, other, label_pull = gather_blocks(normed_low, pull_labels, local_label)
    all_rows = compact(here, places, counts, mine, other, total)
    logits = matmul_nt(all_rows, decoder) + to_full(vocab_bias)
    row_peak = jnp.max(logits, axis=1)
    exp_sums = jnp.sum(jnp.exp(logits - row_peak[:, None]), axis=1)
    label_sum = jnp.sum(jnp.where(label_hit, logits, 0.0))
    local_total = (row_peak + jnp.log(exp_sums)).reshape(-1, 128)
    lines = local_total.shape[0]
    merged = jnp.concatenate(
        [local_total, jnp.pad(label_sum[None, None], ((0, 7), (0, 127)))], axis=0
    )
    is_total = jnp.arange(lines + 8)[:, None] < lines
    pull = None
    stride = 1
    while stride < count:
        arrived = lax.ppermute(merged, AXES, [(place, place ^ stride) for place in range(count)])
        if pull is None:
            pull = matmul(to_low(jnp.exp(logits - row_peak[:, None])), decoder)
            arrived, pull = tie(arrived, pull)
        both = jnp.maximum(merged, arrived) + jnp.log1p(jnp.exp(-jnp.abs(merged - arrived)))
        merged = jnp.where(is_total, both, merged + arrived)
        stride *= 2
    log_total = merged[:lines].reshape(total)
    mean_loss = (jnp.sum(log_total) - merged[lines, 0]) / total
    rows_part = to_low(pull * jnp.exp(row_peak - log_total)[:, None] - to_full(label_pull))
    rows_sum = ChipSum(*spread(here, places, counts, rows_part, MAXM))
    rows_sum.add(rows_sum.arrived)
    rows_sum.start(rows_sum.sends())
    logit_grad = to_low(jnp.exp(logits - log_total[:, None]) - label_hit.astype(jnp.float32))
    vocab_bias_grad = jnp.sum(to_full(logit_grad), axis=0)
    logit_grad, vocab_bias_grad, *arrived = tie(logit_grad, vocab_bias_grad, *rows_sum.arrived)
    rows_sum.add(arrived)
    rows_sum.start(rows_sum.sends())
    decoder_grad = matmul_tn(logit_grad, all_rows)
    decoder_grad, *arrived = tie(decoder_grad, *rows_sum.arrived)
    rows_sum.add(arrived)
    rows_sum.start_levels(rows_sum.level_sends())
    normed_grad = rows_sum.result(rows_sum.arrived)
    dense_grad, head_gain_grad, head_shift_grad = tail_back(normed_grad)
    dense_grad_low = to_low(dense_grad)
    dense_bias_grad = jnp.sum(to_full(dense_grad_low), axis=0)
    dense_full = Weights([gathered_late], later.shares).natural(steps + 1, None)
    picked_grad = to_low(matmul_nt(dense_grad_low, dense_full))
    hidden_grad, feed_sums, *feed_grads = feed_backward(
        here,
        count,
        cotangent,
        picker_low,
        picked_grad,
        summed2,
        vectors,
        own_rows,
        dense_grad_low,
        hidden,
        active,
        slope,
        later,
    )
    first = ChipSum(*feed_grads)
    summed1_grad, branch1_grad, context_grad, out_sums = out_backward(
        core, hidden_grad, summed1, vectors, second_group, 1
    )
    context_grad, *arrived = tie(context_grad, *first.arrived)
    first.add(arrived)
    context_grad, *sent = tie(context_grad, *first.sends())
    first.start(sent)
    saved = (queries, keys_low, values_low, score_total, segments)
    middle = width // 2
    mixed = [list(attention_backward(context_grad, *saved, 0, middle))]
    mixed[0][0], context_grad = tie(mixed[0][0], context_grad)
    mixed.append(list(attention_backward(context_grad, *saved, middle, width - middle)))
    head_sums = jnp.stack(
        [dense_bias_grad, head_gain_grad, head_shift_grad, *[jnp.zeros((width,))] * 5]
    )
    away, kept = last_grads(
        here, count, tokens, context, branch1_grad, (out_sums, feed_sums, head_sums), steps, mixed
    )
    mixed = [part[:3] for part in mixed]
    second = ChipSum(away, kept)
    mixed[0][0], _, *arrived = tie(mixed[0][0], away[0], *first.arrived)
    first.add(arrived)
    mixed[0][0], *sent = tie(mixed[0][0], *first.sends())
    first.start(sent)
    mixed[0][0], *arrived = tie(mixed[0][0], *second.arrived)
    second.add(arrived)
    mixed[0][0], *sent = tie(mixed[0][0], *second.sends())
    second.start(sent)
    tokens_grad = tokens_backward(
        core, summed1_grad, mixed, [(first_group, 0), (first_group, 1), (second_group, 0)]
    )
    first.add(first.arrived)
    first.start_levels(first.level_sends())
    second.add(second.arrived)
    second.start(second.sends())
    second.add(second.arrived)
    second.start_levels(second.level_sends())
    first, second = first.result(first.arrived), second.result(second.arrived)
    up_pieces = [first[share * k : share * (k + 1)] for k in range(steps)]
    down_piece = first[up_share * steps : up_share * steps + down_share]
    dense_piece = first[up_share * steps + down_share :]
    qkv_pieces = [second[share * k : share * (k + 1)] for k in range(blocks)]
    out_piece = second[share * blocks : share * (blocks + 1)]
    small_pieces = take_shares(
        device, second[share * (blocks + 1) :], small_rows, [vector.shape[0] for vector in small]
    )
    return (
        output,
        mean_loss,
        tokens_grad,
        jnp.concatenate(qkv_pieces, axis=1),
        small_pieces[0],
        out_piece,
        *small_pieces[1:4],
        jnp.concatenate(up_pieces, axis=1),
        small_pieces[7],
        down_piece,
        *small_pieces[4:7],
        dense_piece,
        *small_pieces[8:],
        decoder_grad,
        vocab_bias_grad,
    )


def solution(mesh):
    matrix_spec = P(AXES, None)
    vector_spec = P(AXES)
    m, v = matrix_spec, vector_spec
    return jax.shard_map(
        per_device,
        mesh=mesh,
        in_specs=(m, v, v, v, m, m, v, m, v, v, v, m, v, m, v, v, v, m, v, v, v, m, v),
        out_specs=(m, P(), m, m, v, m, v, v, v, m, v, m, v, v, v, m, v, v, v, m, v),
        check_vma=False,
    )
```

time: 764 us -> 476 us (0.62)
  waiting for transfers between devices: 449 us -> 154 us
  matrix products: 167 us -> 32 us
  Pallas kernels: 0 us -> 119 us
  starting transfers between devices: 6.83 us -> 55.9 us
  local copies, waits for them, and re-layouts: 62 us -> 19.8 us
  other arithmetic: 57.4 us -> 72.9 us
    reduce_scatter x2 -> x0, waiting for transfers between devices: 260 us -> none  [the longest x1 147 us: per_device(): lax.psum_scatter(grads_packed, AXES, scatter_dimension=0, tiled=True)[0]]
    all_gather x2 -> x1, waiting for transfers between devices: 178 us -> 3.2 us  [per_device(): later_gathered = lax.all_gather(later_packed, AXES, axis=0)]
    ppermute x5 -> x52, waiting for transfers between devices: 10.7 us -> 151 us  [the longest x32 69.2 us: along(): lax.ppermute(sent, 'dp', [(chip, chip ^ stride) for chip in range(chips)])]
    pallas_call x0 -> x16, Pallas kernels: none -> 119 us  [the longest x1 21.4 us: feed_backward(): pl.pallas_call(kernel, grid_spec=pltpu.PrefetchScalarGridSpec(num_scalar_...]
    ppermute x5 -> x52, starting transfers between devices: 6.66 us -> 55.8 us  [the longest x32 38.4 us: along(): lax.ppermute(sent, 'dp', [(chip, chip ^ stride) for chip in range(chips)])]
    dot_general x9 -> x2, matrix products: 49 us -> 14.9 us  [matmul(): return jnp.dot(left_side, right_side, preferred_element_type=jnp.float32)]
    dot_general x7 -> x2, matrix products: 40.5 us -> 8.44 us  [matmul_nt(): lax.dot_general(left_side, right_side, (((1,), (1,)), ((), ())), preferre...]
    dot_general x9 -> x1, matrix products: 40.5 us -> 8.63 us  [matmul_tn(): lax.dot_general(left_side, right_side, (((0,), (0,)), ((), ())), preferre...]
  transfers between devices with their start and end apart: 9 -> 53, of which waited for: 9 -> 28; matrix products, arithmetic and copies ran while one was open for 3% -> 18% of each run, Pallas kernels for 0% -> 13%
where the time goes in v3:
time: 476 us; the launch traced here: 471 us
  waiting for transfers between devices  154 us (32%)
  Pallas kernels  119 us (25%)
  other arithmetic  72.9 us (15%)
  starting transfers between devices  55.9 us (12%)
  matrix products  32 us (7%)
  local copies, waits for them, and re-layouts  19.8 us (4%)
  between operations  17.5 us (4%)
    ppermute x32, waiting for transfers between devices, along(): lax.ppermute(sent, 'dp', [(chip, chip ^ stride) for chip in range(chips)])  69.2 us
    ppermute x6, waiting for transfers between devices, double(): lax.ppermute(value, 'dp', [(chip, chip ^ stride) for chip in range(chips)])  62 us
    ppermute x32, starting transfers between devices, along(): lax.ppermute(sent, 'dp', [(chip, chip ^ stride) for chip in range(chips)])  38.4 us
    convert_element_type x13, other arithmetic, to_low(): return values.astype(jnp.bfloat16)  26.8 us
    pallas_call x1, Pallas kernels, feed_backward(): pl.pallas_call(kernel, grid_spec=pltpu.PrefetchScalarGridSpec(num_scalar_...  21.4 us
    pallas_call x2, Pallas kernels, attention_backward(): pl.pallas_call(functools.partial(attention_back_kernel, first_head=start...  16.6 us
    pallas_call x1, Pallas kernels, ffn_forward(): pl.pallas_call(functools.partial(ffn_kernel, sizes=[len(first), len(secon...  15.4 us
    dot_general x2, matrix products, matmul(): return jnp.dot(left_side, right_side, preferred_element_type=jnp.float32)  14.9 us
  transfers between devices with their start and end apart: 53, of which 28 were waited for; matrix products, arithmetic and copies ran while one was open for 18% of the time, Pallas kernels for 13%

profile of v3, /device:TPU:0, one launch (start us, length us, event | category | flops | bytes accessed | tf_op | source)
XLA Modules:
  0.0 471.4 jit_solution(17414384375821900961)
XLA Ops:
  26.9 22.0 %collective-permute-done.1 = bf16[2,112,768]{2,1,0:T(8,128)(2,1)S(1)} collective-permute-done((bf16[2,112,768]{2,1,0:T(8,128)(2,1)S(1)}, bf16[2,112,768]{2,1,0:T(8,128)(2,1)S(1)}, u32[]{:S(2)}, u32[]{:S(2)}) %collective-permute-start.1) | collective-permute-done | bytes 344096 | tf_op jit(solution)/shard_map/ppermute | solution.py:246
  52.8 10.8 %collective-permute-done.5 = bf16[4,56,768]{2,1,0:T(8,128)(2,1)S(1)} collective-permute-done((bf16[4,56,768]{2,1,0:T(8,128)(2,1)}, bf16[4,56,768]{2,1,0:T(8,128)(2,1)S(1)}, u32[]{:S(2)}, u32[]{:S(2)}) %collective-permute-start.5) | collective-permute-done | bytes 344096 | tf_op jit(solution)/shard_map/ppermute | solution.py:246
  72.0 19.6 %collective-permute-done.6 = bf16[4,2,56,768]{3,2,1,0:T(8,128)(2,1)S(1)} collective-permute-done((bf16[4,2,56,768]{3,2,1,0:T(8,128)(2,1)S(1)}, bf16[4,2,56,768]{3,2,1,0:T(8,128)(2,1)S(1)}, u32[]{:S(2)}, u32[]{:S(2)}) %collective-permute-start.6) | collective-permute-done | bytes 688160 | tf_op jit(solution)/shard_map/ppermute | solution.py:246
  102.1 14.4 %attention_forward.1 = (bf16[512,768]{1,0:T(8,128)(2,1)}, bf16[512,768]{1,0:T(8,128)(2,1)}, bf16[512,768]{1,0:T(8,128)(2,1)}, bf16[512,768]{1,0:T(8,128)(2,1)}, ...) custom-call(s32[1]{0:T(128)} %bitcast.3.core, bf16[16,56,768]{2,1,0:T(8,128)(2,1)} %bitcast.16.refs_0_.refs_2_, ...), custom_call_target="tpu_custom_call" | custom-call | tf_op jit(solution)/shard_map/attention_forward/pallas_call | solution.py:328
  119.8 15.4 %ffn_forward.1 = (bf16[512,3072]{1,0:T(8,128)(2,1)}, f32[512,3072]{1,0:T(8,128)}, f32[512,768]{1,0:T(8,128)}, bf16[512,768]{1,0:T(8,128)(2,1)}) custom-call(bf16[32,224,768]{2,1,0:T(8,128)(2,1)} %bitcast.146, bf16[32,224,768]{2,1,0:T(8,128)(2,1)} %bitcast.147, bf16[512,768]{1,0:T(8,128)(2,1)} %get-tuple-element.110.refs_2_.refs_9_, ...), custom_call_target="tpu_custom_call" | custom-call | tf_op jit(solution)/shard_map/ffn_forward/pallas_call | solution.py:400
  164.7 6.8 %collective-permute-done.14 = bf16[3,128,384]{2,1,0:T(8,128)(2,1)S(1)} collective-permute-done((bf16[3,128,384]{2,1,0:T(8,128)(2,1)S(1)}, bf16[3,128,384]{2,1,0:T(8,128)(2,1)S(1)}, u32[]{:S(2)}, u32[]{:S(2)}) %collective-permute-start.14) | collective-permute-done | bytes 294944 | tf_op jit(solution)/shard_map/ppermute | solution.py:831
  173.9 7.8 %fusion.8 = bf16[2048,768]{1,0:T(8,128)(2,1)} fusion(bf16[1568,768]{1,0:T(8,128)(2,1)S(1)} %copy-done, s32[2048]{0:T(1024)S(1)} %bitcast.166), kind=kOutput, calls=%fused_computation.15 | convolution fusion | flops 4937285632 | bytes 5562368 | tf_op jit(solution)/shard_map/dot_general | solution.py:43
  189.4 5.2 %collective-permute-done.19.other_ref = bf16[2,16,128,384]{3,2,1,0:T(8,128)(2,1)} collective-permute-done((bf16[2,16,128,384]{3,2,1,0:T(8,128)(2,1)S(1)}, bf16[2,16,128,384]{3,2,1,0:T(8,128)(2,1)}, u32[]{:S(2)}, u32[]{:S(2)}) %collective-permute-start.19) | collective-permute-done | bytes 3145760 | tf_op jit(solution)/shard_map/ppermute | solution.py:826
  194.6 7.8 %compact_rows.1 = bf16[2048,768]{1,0:T(8,128)(2,1)} custom-call(s32[4]{0:T(128)} %pad_add_fusion.place, s32[32]{0:T(128)} %add.600.places, s32[32]{0:T(128)} %copy-done.22, bf16[2,16,128,384]{3,2,1,0:T(8,128)(2,1)} %copy-done.3, bf16[2,16,128,384]{3,2,1,0:T(8,128)(2,1)} %collective-permute-done.19.other_ref), custom_call_target="tpu_custom_call" | custom-call | tf_op jit(solution)/shard_map/compact_rows/pallas_call | solution.py:972
  202.4 7.2 %add_reduce_fusion = (f32[2048]{0:T(1024)S(1)}, f32[2048,1568]{0,1:T(8,128)S(1)}) fusion(f32[1568]{0:T(1024)S(1)} %convert_element_type.653, bf16[2048,768]{1,0:T(8,128)(2,1)} %compact_rows.1, bf16[1568,768]{1,0:T(8,128)(2,1)S(1)} %copy-done), kind=kOutput, calls=%fused_computation.9 | convolution fusion | flops 4938921984 | bytes 18413696 | tf_op jit(solution)/shard_map/dot_general | solution.py:53
  209.6 5.6 %fusion.2 = (f32[2048]{0:T(1024)S(1)}, f32[]{:T(128)}) fusion(f32[2048,1568]{0,1:T(8,128)S(1)} %get-tuple-element.280, f32[2048]{0:T(1024)S(1)} %get-tuple-element.279, f32[1568]{0:T(1024)S(1)} %convert_element_type.653, s32[2048]{0:T(1024)S(1)} %bitcast.167), kind=kLoop, calls=%fused_computation.8 | loop fusion | flops 19265536 | bytes 12875908 | tf_op jit(solution)/shard_map/reduce_sum | solution.py:1228
  216.1 7.1 %fusion.4 = f32[2048,768]{1,0:T(8,128)S(1)} fusion(bf16[1568,768]{1,0:T(8,128)(2,1)S(1)} %copy-done, f32[2048,1568]{0,1:T(8,128)S(1)} %get-tuple-element.280, f32[2048]{0:T(1024)S(1)} %get-tuple-element.279, f32[1568]{0:T(1024)S(1)} %convert_element_type.653), kind=kOutput, calls=%fused_computation.11 | convolution fusion | flops 4942135296 | bytes 21559424 | tf_op jit(solution)/shard_map/dot_general | solution.py:43
  244.5 8.0 %spread_rows.1 = (bf16[16,128,384]{2,1,0:T(8,128)(2,1)}, bf16[16,128,384]{2,1,0:T(8,128)(2,1)}, bf16[16,128,384]{2,1,0:T(8,128)(2,1)}, bf16[16,128,384]{2,1,0:T(8,128)(2,1)}) custom-call(s32[4]{0:T(128)} %pad_add_fusion.place, s32[32]{0:T(128)} %add.600.places, s32[32]{0:T(128)} %copy-done.22, bf16[2048,768]{1,0:T(8,128)(2,1)} %subtract_convert_fusion.1.rows_ref), custom_call_target="tpu_custom_call" | custom-call | tf_op jit(solution)/shard_map/spread_rows/pallas_call | solution.py:1097
  261.5 11.6 %convert_reduce_fusion = (f32[1568]{0:T(1024)}, bf16[2048,1568]{0,1:T(8,128)(2,1)}) fusion(s32[2048]{0:T(1024)S(1)} %bitcast.168, f32[2048]{0:T(1024)S(1)} %get-tuple-element.275, f32[2048,1568]{0,1:T(8,128)} %copy-done.2, f32[1568]{0:T(1024)S(1)} %convert_element_type.653), kind=kLoop, calls=%fused_computation.2 | loop fusion | flops 25688544 | bytes 19296512 | tf_op jit(solution)/shard_map/reduce_sum | solution.py:1253
  285.8 8.6 %fusion.51 = f32[1568,768]{1,0:T(8,128)} fusion(bf16[2048,1568]{0,1:T(8,128)(2,1)} %get-tuple-element.130, bf16[2048,768]{1,0:T(8,128)(2,1)S(1)} %copy-done.4), kind=kOutput, calls=%fused_computation.200 | convolution fusion | flops 4932501504 | bytes 14385152 | tf_op jit(solution)/shard_map/dot_general | solution.py:47
  307.2 8.1 %collective-permute-done.32 = bf16[128,768]{1,0:T(8,128)(2,1)S(1)} collective-permute-done((bf16[128,768]{1,0:T(8,128)(2,1)S(1)}, bf16[128,768]{1,0:T(8,128)(2,1)S(1)}, u32[]{:S(2)}, u32[]{:S(2)}) %collective-permute-start.32) | collective-permute-done | bytes 196640 | tf_op jit(solution)/shard_map/ppermute | solution.py:831
  317.5 21.4 %feed_backward.1 = (f32[512,768]{1,0:T(8,128)}, f32[8,768]{1,0:T(8,128)}, bf16[16,216,384]{2,1,0:T(8,128)(2,1)}, bf16[16,216,384]{2,1,0:T(8,128)(2,1)}, bf16[16,...) custom-call(s32[4]{0:T(128)} %pad_add_fusion.place, bf16[32,224,768]{2,1,0:T(8,128)(2,1)} %bitcast.151, ...), custom_call_target="tpu_custom_call" | custom-call | tf_op jit(solution)/shard_map/feed_backward/pallas_call | solution.py:540
  339.4 5.3 %out_backward.1 = (f32[512,768]{1,0:T(8,128)}, bf16[512,768]{1,0:T(8,128)(2,1)}, bf16[512,768]{1,0:T(8,128)(2,1)}, f32[8,768]{1,0:T(8,128)}) custom-call(s32[1]{0:T(128)} %bitcast.3.core, bf16[16,56,768]{2,1,0:T(8,128)(2,1)} %bitcast.23.refs_4_.refs_6_.refs_0_, bf16[16,56,768]{2,1,0:T(8,128)(2,1)} %collective-permute-done.7.refs_5_.refs_7_.refs_1_, ...), custom_call_target="tpu_custom_call" | custom-call | tf_op jit(solution)/shard_map/out_backward/pallas_call | solution.py:592
  355.8 8.2 %attention_backward.2 = (bf16[512,384]{1,0:T(8,128)(2,1)}, bf16[512,384]{1,0:T(8,128)(2,1)}, bf16[512,384]{1,0:T(8,128)(2,1)}, f32[8,384]{1,0:T(8,128)}) custom-call(bf16[512,768]{1,0:T(8,128)(2,1)} %get-tuple-element.162.refs_0_, bf16[512,768]{1,0:T(8,128)(2,1)} %get-tuple-element.150.refs_1_, bf16[512,768]{1,0:T(8,128)(2,1)} %get-tuple-element.151.refs_2_, ...), custom_call_target="tpu_custom_call" | custom-call | tf_op jit(solution)/shard_map/attention_backward/pallas_call | solution.py:652
  364.0 8.4 %attention_backward.3 = (bf16[512,384]{1,0:T(8,128)(2,1)}, bf16[512,384]{1,0:T(8,128)(2,1)}, bf16[512,384]{1,0:T(8,128)(2,1)}, f32[8,384]{1,0:T(8,128)}) custom-call(bf16[512,768]{1,0:T(8,128)(2,1)} %get-tuple-element.162.refs_0_, bf16[512,768]{1,0:T(8,128)(2,1)} %get-tuple-element.150.refs_1_, bf16[512,768]{1,0:T(8,128)(2,1)} %get-tuple-element.151.refs_2_, ...), custom_call_target="tpu_custom_call" | custom-call | tf_op jit(solution)/shard_map/attention_backward/pallas_call | solution.py:652
  372.4 8.8 %last_grads.1 = (bf16[16,112,384]{2,1,0:T(8,128)(2,1)}, bf16[16,112,384]{2,1,0:T(8,128)(2,1)}, bf16[16,112,384]{2,1,0:T(8,128)(2,1)}, bf16[16,112,384]{2,1,0:T(8,128)(2,1)}) custom-call(s32[4]{0:T(128)} %pad_add_fusion.place, bf16[512,768]{1,0:T(8,128)(2,1)} %refs_0_.5, bf16[512,768]{1,0:T(8,128)(2,1)} %get-tuple-element.156.refs_1_, ...), custom_call_target="tpu_custom_call" | custom-call | tf_op jit(solution)/shard_map/last_grads/pallas_call | solution.py:730
  402.0 6.9 %tokens_backward.1 = f32[512,768]{1,0:T(8,128)} custom-call(s32[1]{0:T(128)} %bitcast.3.core, bf16[16,56,768]{2,1,0:T(8,128)(2,1)} %bitcast.16.refs_0_.refs_2_, bf16[16,56,768]{2,1,0:T(8,128)(2,1)} %collective-permute-done.4.refs_1_.refs_3_, bf16[16,56,768]{2,1,0:T(8,128)(2,1)} %bitcast.16.refs_0_.refs_2_, ...), custom_call_target="tpu_custom_call" | custom-call | tf_op jit(solution)/shard_map/tokens_backward/pallas_call | solution.py:770
  419.0 6.2 %collective-permute-done.42 = bf16[8,112,384]{2,1,0:T(8,128)(2,1)} collective-permute-done((bf16[8,112,384]{2,1,0:T(8,128)(2,1)}, bf16[8,112,384]{2,1,0:T(8,128)(2,1)}, u32[]{:S(2)}, u32[]{:S(2)}) %collective-permute-start.42) | collective-permute-done | bytes 688160 | tf_op jit(solution)/shard_map/ppermute | solution.py:831
  429.2 12.1 %collective-permute-done.50 = bf16[216,768]{1,0:T(8,128)(2,1)S(1)} collective-permute-done((bf16[216,768]{1,0:T(8,128)(2,1)S(1)}, bf16[216,768]{1,0:T(8,128)(2,1)S(1)}, u32[]{:S(2)}, u32[]{:S(2)}) %collective-permute-start.50) | collective-permute-done | bytes 331808 | tf_op jit(solution)/shard_map/ppermute | solution.py:831
  (280 shorter events, 210.6 us)
Async XLA Ops:
  7.2 112.6 %all-gather.3.cloned.1.call-start = ((), (), s32[]{:S(2)}) async-start(), calls=%async_computation | async-start | bytes 11354112 | tf_op jit(solution)/shard_map/all_gather | solution.py:1157
  24.0 24.8 %collective-permute-start.1 = (bf16[2,112,768]{2,1,0:T(8,128)(2,1)S(1)}, bf16[2,112,768]{2,1,0:T(8,128)(2,1)S(1)}, u32[]{:S(2)}, u32[]{:S(2)}) collective-permute-start(bf16[2,112,768]{2,1,0:T(8,128)(2,1)S(1)} %maximum_bitcast_fusion), channel_id=1, source_target_pairs={{0,16},{2,18},{4,20},{6,22},{8,24},{10,26},{12,28},{14,30},{16,0},... | collective-permute-start | bytes 1032200 | tf_op jit(solution)/shard_map/ppermute | solution.py:246
  51.3 17.3 %collective-permute-start.2 = (bf16[4,56,768]{2,1,0:T(8,128)(2,1)}, bf16[4,56,768]{2,1,0:T(8,128)(2,1)}, u32[]{:S(2)}, u32[]{:S(2)}) collective-permute-start(bf16[4,56,768]{2,1,0:T(8,128)(2,1)} %get-tuple-element.249), channel_id=1, source_target_pairs={{0,2},{2,0},{4,6},{6,4},{8,10},{10,8},{12,14},{14,12},{16,18},{18,... | collective-permute-start | bytes 1032200 | tf_op jit(solution)/shard_map/ppermute | solution.py:246
  69.8 21.8 %collective-permute-start.6 = (bf16[4,2,56,768]{3,2,1,0:T(8,128)(2,1)S(1)}, bf16[4,2,56,768]{3,2,1,0:T(8,128)(2,1)S(1)}, u32[]{:S(2)}, u32[]{:S(2)}) collective-permute-start(bf16[4,2,56,768]{3,2,1,0:T(8,128)(2,1)S(1)} %pad_maximum_fusion.5), channel_id=1, source_target_pairs={{0,2},{2,0},{4,6},{6,4},{8,10},{10,8},{12,14},{14,12},{16,18},{18,... | collective-permute-start | bytes 2064392 | tf_op jit(solution)/shard_map/ppermute | solution.py:246
  70.3 22.6 %collective-permute-start.3 = (bf16[4,2,56,768]{3,2,0,1:T(8,128)(2,1)S(1)}, bf16[4,2,56,768]{3,2,0,1:T(8,128)(2,1)S(1)}, u32[]{:S(2)}, u32[]{:S(2)}) collective-permute-start(bf16[4,2,56,768]{3,2,0,1:T(8,128)(2,1)S(1)} %pad_maximum_fusion.4), channel_id=1, source_target_pairs={{0,4},{2,6},{4,0},{6,2},{8,12},{10,14},{12,8},{14,10},{16,20},{18,... | collective-permute-start | bytes 2064392 | tf_op jit(solution)/shard_map/ppermute | solution.py:246
  139.9 16.8 %collective-permute-start.10 = (bf16[128,768]{1,0:T(8,128)(2,1)}, bf16[128,768]{1,0:T(8,128)(2,1)S(1)}, u32[]{:S(2)}, u32[]{:S(2)}) collective-permute-start(bf16[128,768]{1,0:T(8,128)(2,1)} %get-tuple-element.114), channel_id=1, source_target_pairs={{0,24},{2,26},{4,28},{6,30},{8,16},{10,18},{12,20},{14,22},{16,8},... | collective-permute-start | bytes 589832 | tf_op jit(solution)/shard_map/ppermute | solution.py:831
  142.2 19.4 %collective-permute-start.9 = (bf16[128,768]{1,0:T(8,128)(2,1)}, bf16[128,768]{1,0:T(8,128)(2,1)S(1)}, u32[]{:S(2)}, u32[]{:S(2)}) collective-permute-start(bf16[128,768]{1,0:T(8,128)(2,1)} %get-tuple-element.114), channel_id=1, source_target_pairs={{0,16},{2,18},{4,20},{6,22},{8,24},{10,26},{12,28},{14,30},{16,0},... | collective-permute-start | bytes 589832 | tf_op jit(solution)/shard_map/ppermute | solution.py:831
  144.0 17.6 %collective-permute-start.8 = (bf16[128,768]{1,0:T(8,128)(2,1)}, bf16[128,768]{1,0:T(8,128)(2,1)S(1)}, u32[]{:S(2)}, u32[]{:S(2)}) collective-permute-start(bf16[128,768]{1,0:T(8,128)(2,1)} %get-tuple-element.114), channel_id=1, source_target_pairs={{0,8},{2,10},{4,12},{6,14},{8,0},{10,2},{12,4},{14,6},{16,24},{18,... | collective-permute-start | bytes 589832 | tf_op jit(solution)/shard_map/ppermute | solution.py:831
  171.6 14.5 %collective-permute-start.16 = (bf16[6,128,384]{2,1,0:T(8,128)(2,1)S(1)}, bf16[6,128,384]{2,1,0:T(8,128)(2,1)S(1)}, u32[]{:S(2)}, u32[]{:S(2)}) collective-permute-start(bf16[6,128,384]{2,1,0:T(8,128)(2,1)S(1)} %pad_maximum_fusion.7), channel_id=1, source_target_pairs={{0,4},{2,6},{4,0},{6,2},{8,12},{10,14},{12,8},{14,10},{16,20},{18,... | collective-permute-start | bytes 1769480 | tf_op jit(solution)/shard_map/ppermute | solution.py:831
  257.0 19.7 %collective-permute-start.26 = (bf16[8,128,384]{2,1,0:T(8,128)(2,1)S(1)}, bf16[8,128,384]{2,1,0:T(8,128)(2,1)}, u32[]{:S(2)}, u32[]{:S(2)}) collective-permute-start(bf16[8,128,384]{2,1,0:T(8,128)(2,1)S(1)} %add_convert_fusion.3), channel_id=1, source_target_pairs={{0,2},{2,0},{4,6},{6,4},{8,10},{10,8},{12,14},{14,12},{16,18},{18,... | collective-permute-start | bytes 2359304 | tf_op jit(solution)/shard_map/ppermute | solution.py:831
  259.8 19.8 %collective-permute-start.28 = (bf16[8,128,384]{2,1,0:T(8,128)(2,1)}, bf16[8,128,384]{2,1,0:T(8,128)(2,1)}, u32[]{:S(2)}, u32[]{:S(2)}) collective-permute-start(bf16[8,128,384]{2,1,0:T(8,128)(2,1)} %add_convert_fusion.2), channel_id=1, source_target_pairs={{0,4},{2,6},{4,0},{6,2},{8,12},{10,14},{12,8},{14,10},{16,20},{18,... | collective-permute-start | bytes 2359304 | tf_op jit(solution)/shard_map/ppermute | solution.py:831
  299.9 15.4 %collective-permute-start.32 = (bf16[128,768]{1,0:T(8,128)(2,1)S(1)}, bf16[128,768]{1,0:T(8,128)(2,1)S(1)}, u32[]{:S(2)}, u32[]{:S(2)}) collective-permute-start(bf16[128,768]{1,0:T(8,128)(2,1)S(1)} %pad_maximum_fusion.17), channel_id=1, source_target_pairs={{0,16},{2,18},{4,20},{6,22},{8,24},{10,26},{12,28},{14,30},{16,0},... | collective-permute-start | bytes 589832 | tf_op jit(solution)/shard_map/ppermute | solution.py:831
  300.0 15.3 %collective-permute-start.31 = (bf16[128,768]{1,0:T(8,128)(2,1)S(1)}, bf16[128,768]{1,0:T(8,128)(2,1)S(1)}, u32[]{:S(2)}, u32[]{:S(2)}) collective-permute-start(bf16[128,768]{1,0:T(8,128)(2,1)S(1)} %pad_maximum_fusion.16), channel_id=1, source_target_pairs={{0,8},{2,10},{4,12},{6,14},{8,0},{10,2},{12,4},{14,6},{16,24},{18,... | collective-permute-start | bytes 589832 | tf_op jit(solution)/shard_map/ppermute | solution.py:831
  354.0 31.4 %collective-permute-start.36 = (bf16[8,216,384]{2,1,0:T(8,128)(2,1)}, bf16[8,216,384]{2,1,0:T(8,128)(2,1)S(1)}, u32[]{:S(2)}, u32[]{:S(2)}) collective-permute-start(bf16[8,216,384]{2,1,0:T(8,128)(2,1)} %add_convert_fusion.1), channel_id=1, source_target_pairs={{0,2},{2,0},{4,6},{6,4},{8,10},{10,8},{12,14},{14,12},{16,18},{18,... | collective-permute-start | bytes 3981320 | tf_op jit(solution)/shard_map/ppermute | solution.py:831
  354.9 31.2 %collective-permute-start.37 = (bf16[8,216,384]{2,1,0:T(8,128)(2,1)}, bf16[8,216,384]{2,1,0:T(8,128)(2,1)}, u32[]{:S(2)}, u32[]{:S(2)}) collective-permute-start(bf16[8,216,384]{2,1,0:T(8,128)(2,1)} %add_convert_fusion), channel_id=1, source_target_pairs={{0,4},{2,6},{4,0},{6,2},{8,12},{10,14},{12,8},{14,10},{16,20},{18,... | collective-permute-start | bytes 3981320 | tf_op jit(solution)/shard_map/ppermute | solution.py:831
  391.5 18.1 %collective-permute-start.48 = (bf16[4,216,384]{2,1,0:T(8,128)(2,1)}, bf16[4,216,384]{2,1,0:T(8,128)(2,1)S(1)}, u32[]{:S(2)}, u32[]{:S(2)}) collective-permute-start(bf16[4,216,384]{2,1,0:T(8,128)(2,1)} %add_convert_fusion.6), channel_id=1, source_target_pairs={{0,2},{2,0},{4,6},{6,4},{8,10},{10,8},{12,14},{14,12},{16,18},{18,... | collective-permute-start | bytes 1990664 | tf_op jit(solution)/shard_map/ppermute | solution.py:831
  394.2 18.2 %collective-permute-start.47 = (bf16[4,216,384]{2,1,0:T(8,128)(2,1)}, bf16[4,216,384]{2,1,0:T(8,128)(2,1)}, u32[]{:S(2)}, u32[]{:S(2)}) collective-permute-start(bf16[4,216,384]{2,1,0:T(8,128)(2,1)} %add_convert_fusion.7), channel_id=1, source_target_pairs={{0,4},{2,6},{4,0},{6,2},{8,12},{10,14},{12,8},{14,10},{16,20},{18,... | collective-permute-start | bytes 1990664 | tf_op jit(solution)/shard_map/ppermute | solution.py:831
  399.1 26.2 %collective-permute-start.42 = (bf16[8,112,384]{2,1,0:T(8,128)(2,1)}, bf16[8,112,384]{2,1,0:T(8,128)(2,1)}, u32[]{:S(2)}, u32[]{:S(2)}) collective-permute-start(bf16[8,112,384]{2,1,0:T(8,128)(2,1)} %add_convert_fusion.4), channel_id=1, source_target_pairs={{0,4},{2,6},{4,0},{6,2},{8,12},{10,14},{12,8},{14,10},{16,20},{18,... | collective-permute-start | bytes 2064392 | tf_op jit(solution)/shard_map/ppermute | solution.py:831
  400.8 26.9 %collective-permute-start.40 = (bf16[8,112,384]{2,1,0:T(8,128)(2,1)}, bf16[8,112,384]{2,1,0:T(8,128)(2,1)S(1)}, u32[]{:S(2)}, u32[]{:S(2)}) collective-permute-start(bf16[8,112,384]{2,1,0:T(8,128)(2,1)} %add_convert_fusion.5), channel_id=1, source_target_pairs={{0,2},{2,0},{4,6},{6,4},{8,10},{10,8},{12,14},{14,12},{16,18},{18,... | collective-permute-start | bytes 2064392 | tf_op jit(solution)/shard_map/ppermute | solution.py:831
  414.4 14.8 %collective-permute-start.51 = (bf16[216,768]{1,0:T(8,128)(2,1)S(1)}, bf16[216,768]{1,0:T(8,128)(2,1)S(1)}, u32[]{:S(2)}, u32[]{:S(2)}) collective-permute-start(bf16[216,768]{1,0:T(8,128)(2,1)S(1)} %pad_maximum_fusion.11), channel_id=1, source_target_pairs={{0,24},{2,26},{4,28},{6,30},{8,16},{10,18},{12,20},{14,22},{16,8},... | collective-permute-start | bytes 995336 | tf_op jit(solution)/shard_map/ppermute | solution.py:831
  416.8 24.5 %collective-permute-start.50 = (bf16[216,768]{1,0:T(8,128)(2,1)S(1)}, bf16[216,768]{1,0:T(8,128)(2,1)S(1)}, u32[]{:S(2)}, u32[]{:S(2)}) collective-permute-start(bf16[216,768]{1,0:T(8,128)(2,1)S(1)} %pad_maximum_fusion.10), channel_id=1, source_target_pairs={{0,16},{2,18},{4,20},{6,22},{8,24},{10,26},{12,28},{14,30},{16,0},... | collective-permute-start | bytes 995336 | tf_op jit(solution)/shard_map/ppermute | solution.py:831
  416.9 24.4 %collective-permute-start.49 = (bf16[216,768]{1,0:T(8,128)(2,1)S(1)}, bf16[216,768]{1,0:T(8,128)(2,1)S(1)}, u32[]{:S(2)}, u32[]{:S(2)}) collective-permute-start(bf16[216,768]{1,0:T(8,128)(2,1)S(1)} %pad_maximum_fusion.9), channel_id=1, source_target_pairs={{0,8},{2,10},{4,12},{6,14},{8,0},{10,2},{12,4},{14,6},{16,24},{18,... | collective-permute-start | bytes 995336 | tf_op jit(solution)/shard_map/ppermute | solution.py:831
  426.5 16.4 %collective-permute-start.43 = (bf16[4,112,384]{2,1,0:T(8,128)(2,1)S(1)}, bf16[4,112,384]{2,1,0:T(8,128)(2,1)S(1)}, u32[]{:S(2)}, u32[]{:S(2)}) collective-permute-start(bf16[4,112,384]{2,1,0:T(8,128)(2,1)S(1)} %add_convert_fusion.10), channel_id=1, source_target_pairs={{0,2},{2,0},{4,6},{6,4},{8,10},{10,8},{12,14},{14,12},{16,18},{18,... | collective-permute-start | bytes 1032200 | tf_op jit(solution)/shard_map/ppermute | solution.py:831
  428.8 15.4 %collective-permute-start.41 = (bf16[4,112,384]{2,1,0:T(8,128)(2,1)S(1)}, bf16[4,112,384]{2,1,0:T(8,128)(2,1)S(1)}, u32[]{:S(2)}, u32[]{:S(2)}) collective-permute-start(bf16[4,112,384]{2,1,0:T(8,128)(2,1)S(1)} %add_convert_fusion.11), channel_id=1, source_target_pairs={{0,4},{2,6},{4,0},{6,2},{8,12},{10,14},{12,8},{14,10},{16,20},{18,... | collective-permute-start | bytes 1032200 | tf_op jit(solution)/shard_map/ppermute | solution.py:831
  (53 other events, 533.1 us)
Sparse Core Ops, SparseCore 0:
  11.5 108.2 all-gather.2

commit v4 on v3

--- a/solution.py
+++ b/solution.py
@@ -941,21 +941,22 @@
     return pl.multiple_of(jnp.minimum((start // 16) * 16, total - window), 16)
 
 
-def compact_kernel(place, places, counts, mine_ref, other_ref, out_ref, *, window):
+def compact_kernel(place, places, counts, indices, mine_ref, other_ref, *refs, window, levels):
     step = pl.program_id(0)
+    *before, out_ref = refs
 
     @pl.when(step == 0)
     def _():
-        out_ref[...] = jnp.zeros_like(out_ref)
+        out_ref[...] = before[0][...] if before else jnp.zeros_like(out_ref)
 
     _, batch, slots, half = mine_ref.shape
-    levels = pl.num_programs(0) * batch // 4
     total = out_ref.shape[0]
     for which, ref in enumerate((mine_ref, other_ref)):
         core = place[0] if which == 0 else 1 - place[0]
         for axis in range(2):
             for lane in range(batch):
-                source = 2 * chip_at(step * batch + lane, place, levels, axis) + core
+                index = indices[step * batch + lane]
+                source = 2 * chip_at(index, place, levels, axis) + core
                 start = places[source]
                 base = window_base(start, total, window)
                 row = lax.broadcasted_iota(jnp.int32, (window, slots), 0) + (base - start)
@@ -965,22 +966,23 @@
                 out_ref[pl.ds(base, window), half * axis : half * (axis + 1)] += to_low(moved)
 
 
-def compact(place, places, counts, mine, other, total):
-    _, chips, slots, half = mine.shape
-    batch = 4
+def compact(place, places, counts, mine, other, indices, total, before=()):
+    _, blocks, slots, half = mine.shape
+    levels = lax.axis_size("dp") // 4
+    batch = blocks // 2 if blocks <= 16 else 2
     block = pl.BlockSpec((2, batch, slots, half), lambda i, *_: (0, i, 0, 0))
     return pl.pallas_call(
-        functools.partial(compact_kernel, window=slots + 16),
+        functools.partial(compact_kernel, window=slots + 16, levels=levels),
         grid_spec=pltpu.PrefetchScalarGridSpec(
-            num_scalar_prefetch=3,
-            grid=(chips // batch,),
-            in_specs=[block, block],
+            num_scalar_prefetch=4,
+            grid=(blocks // batch,),
+            in_specs=[block, block, *[whole(rows) for rows in before]],
             out_specs=pl.BlockSpec((total, 2 * half), lambda i, *_: (0, 0)),
         ),
         out_shape=jax.ShapeDtypeStruct((total, 2 * half), jnp.bfloat16),
         compiler_params=pltpu.CompilerParams(dimension_semantics=("arbitrary",)),
         name="compact_rows",
-    )(place, places, counts, mine, other)
+    )(place, places, counts, jnp.array(indices, jnp.int32), mine, other, *before)
 
 
 def compact_labels_kernel(places, counts, lines_ref, out_ref):
@@ -1018,6 +1020,12 @@
         name="compact_labels",
     )(places, counts, lines)
     return out[0].astype(jnp.int32)
+
+
+def block_order():
+    levels = lax.axis_size("dp") // 4
+    near = [*range(levels), *range(2 * levels, 3 * levels), levels, 3 * levels]
+    return near, [k for k in range(4 * levels) if k not in near]
 
 
 def gather_blocks(value, beside, given):
@@ -1044,26 +1052,16 @@
         along(jnp.concatenate([part, got]), second)
         for part, got, (_, second) in zip(rest, near_rest, strides)
     ]
-    result, *far_rest = tie(beside(given), *far_rest)
-    count = levels - 1
-    mine = jnp.stack(
+    early = jnp.stack(
         [
-            jnp.concatenate(
-                [
-                    own[k][None],
-                    rest[k],
-                    far[k][:1],
-                    far_rest[k][:count],
-                    near[k][None],
-                    near_rest[k],
-                    far[k][1:],
-                    far_rest[k][count:],
-                ]
-            )
+            jnp.concatenate([own[k][None], rest[k], near[k][None], near_rest[k], far[k]])
             for k in range(2)
         ]
     )
-    return mine, core_swap(mine), result
+    results = beside(early, core_swap(early), given)
+    tied = tie(*far_rest, *results)
+    late = jnp.stack(tied[:2])
+    return late, core_swap(late), tied[2:]
 
 
 def spread_kernel(place, places, counts, rows_ref, *out_refs, window):
@@ -1217,12 +1215,17 @@
     local_label = all_labels - slice_index * vocab_rows
     label_hit = jnp.arange(vocab_rows)[None, :] == local_label[:, None]
 
-    def pull_labels(chosen):
+    early_order, late_order = block_order()
+
+    def beside_last(mine, other, chosen):
         hit = jnp.arange(vocab_rows)[None, :] == chosen[:, None]
-        return to_low(matmul(hit.astype(jnp.bfloat16), decoder))
-
-    mine, other, label_pull = gather_blocks(normed_low, pull_labels, local_label)
-    all_rows = compact(here, places, counts, mine, other, total)
+        pulled = to_low(matmul(hit.astype(jnp.bfloat16), decoder))
+        return compact(here, places, counts, mine, other, early_order, total), pulled
+
+    mine, other, (early_rows, label_pull) = gather_blocks(normed_low, beside_last, local_label)
+    late = (here, places, counts, mine, other, late_order, total)
+    small_total = total <= 4096
+    all_rows = compact(*late, (early_rows,)) if small_total else early_rows + compact(*late)
     logits = matmul_nt(all_rows, decoder) + to_full(vocab_bias)
     row_peak = jnp.max(logits, axis=1)
     exp_sums = jnp.sum(jnp.exp(logits - row_peak[:, None]), axis=1)
@@ -1233,19 +1236,33 @@
         [local_total, jnp.pad(label_sum[None, None], ((0, 7), (0, 127)))], axis=0
     )
     is_total = jnp.arange(lines + 8)[:, None] < lines
-    pull = None
-    stride = 1
-    while stride < count:
-        arrived = lax.ppermute(merged, AXES, [(place, place ^ stride) for place in range(count)])
-        if pull is None:
-            pull = matmul(to_low(jnp.exp(logits - row_peak[:, None])), decoder)
-            arrived, pull = tie(arrived, pull)
-        both = jnp.maximum(merged, arrived) + jnp.log1p(jnp.exp(-jnp.abs(merged - arrived)))
-        merged = jnp.where(is_total, both, merged + arrived)
-        stride *= 2
+    middle = total // 2
+    pulls = []
+    rounds = [[1], [2, 4, 6]]
+    rounds += [[8, 16, 24]] if count == 32 else [[8 << k] for k in range((count // 8).bit_length() - 1)]
+    for distances in rounds:
+        arrived = [
+            lax.ppermute(merged, AXES, [(place, place ^ far) for place in range(count)])
+            for far in distances
+        ]
+        if len(pulls) < 2:
+            rows = slice(middle * len(pulls), middle * (len(pulls) + 1))
+            pull = matmul(to_low(jnp.exp(logits[rows] - row_peak[rows, None])), decoder)
+            *arrived, pull = tie(*arrived, pull)
+            pulls.append(pull)
+        every = [merged, *arrived]
+        peak = functools.reduce(jnp.maximum, every)
+        both = peak + jnp.log(sum(jnp.exp(part - peak) for part in every))
+        merged = jnp.where(is_total, both, sum(every))
     log_total = merged[:lines].reshape(total)
     mean_loss = (jnp.sum(log_total) - merged[lines, 0]) / total
-    rows_part = to_low(pull * jnp.exp(row_peak - log_total)[:, None] - to_full(label_pull))
+    scale = jnp.exp(row_peak - log_total)[:, None]
+    rows_part = jnp.concatenate(
+        [
+            to_low(pull * scale[rows] - to_full(label_pull[rows]))
+            for pull, rows in zip(pulls, (slice(0, middle), slice(middle, total)))
+        ]
+    )
     rows_sum = ChipSum(*spread(here, places, counts, rows_part, MAXM))
     rows_sum.add(rows_sum.arrived)
     rows_sum.start(rows_sum.sends())

time: 476 us -> 464 us (0.975)
  waiting for transfers between devices: 154 us -> 136 us
  starting transfers between devices: 55.9 us -> 62.1 us
    ppermute x5 -> x7, waiting for transfers between devices: 11.5 us -> 1.77 us  [per_device(): lax.ppermute(merged, AXES, [(place, place ^ far) for place in range(count)])]
    convert_element_type x13 -> x12, other arithmetic: 26.8 us -> 20.1 us  [to_low(): return values.astype(jnp.bfloat16)]
    ppermute x32, waiting for transfers between devices: 69.2 us -> 63.1 us  [along(): lax.ppermute(sent, 'dp', [(chip, chip ^ stride) for chip in range(chips)])]
    pallas_call x1 -> x2, Pallas kernels: 7.82 us -> 12.2 us  [compact(): pl.pallas_call(functools.partial(compact_kernel, window=slots + 16, level...]
    dot_general x2 -> x3, matrix products: 14.9 us -> 14.5 us  [matmul(): return jnp.dot(left_side, right_side, preferred_element_type=jnp.float32)]
  transfers between devices with their start and end apart: 53 -> 56, of which waited for: 28 -> 27; matrix products, arithmetic and copies ran while one was open for 18% -> 18% of each run, Pallas kernels for 13% -> 14%
where the time goes in v4:
time: 464 us; the launch traced here: 460 us
  waiting for transfers between devices  136 us (29%)
  Pallas kernels  123 us (27%)
  other arithmetic  70.7 us (15%)
  starting transfers between devices  62.1 us (13%)
  matrix products  31.6 us (7%)
  local copies, waits for them, and re-layouts  17.8 us (4%)
  between operations  17.5 us (4%)
    ppermute x32, waiting for transfers between devices, along(): lax.ppermute(sent, 'dp', [(chip, chip ^ stride) for chip in range(chips)])  63.1 us
    ppermute x6, waiting for transfers between devices, double(): lax.ppermute(value, 'dp', [(chip, chip ^ stride) for chip in range(chips)])  62 us
    ppermute x32, starting transfers between devices, along(): lax.ppermute(sent, 'dp', [(chip, chip ^ stride) for chip in range(chips)])  40.8 us
    pallas_call x1, Pallas kernels, feed_backward(): pl.pallas_call(kernel, grid_spec=pltpu.PrefetchScalarGridSpec(num_scalar_...  21.4 us
    convert_element_type x12, other arithmetic, to_low(): return values.astype(jnp.bfloat16)  20.1 us
    pallas_call x2, Pallas kernels, attention_backward(): pl.pallas_call(functools.partial(attention_back_kernel, first_head=start...  16.6 us
    pallas_call x1, Pallas kernels, ffn_forward(): pl.pallas_call(functools.partial(ffn_kernel, sizes=[len(first), len(secon...  15.4 us
    dot_general x3, matrix products, matmul(): return jnp.dot(left_side, right_side, preferred_element_type=jnp.float32)  14.5 us
  transfers between devices with their start and end apart: 56, of which 27 were waited for; matrix products, arithmetic and copies ran while one was open for 18% of the time, Pallas kernels for 14%

profile of v4, /device:TPU:0, one launch (start us, length us, event | category | flops | bytes accessed | tf_op | source)
XLA Modules:
  0.0 459.5 jit_solution(5166677428816475019)
XLA Ops:
  26.9 22.0 %collective-permute-done.1 = bf16[2,112,768]{2,1,0:T(8,128)(2,1)S(1)} collective-permute-done((bf16[2,112,768]{2,1,0:T(8,128)(2,1)S(1)}, bf16[2,112,768]{2,1,0:T(8,128)(2,1)S(1)}, u32[]{:S(2)}, u32[]{:S(2)}) %collective-permute-start.1) | collective-permute-done | bytes 344096 | tf_op jit(solution)/shard_map/ppermute | solution.py:246
  52.8 10.8 %collective-permute-done.5 = bf16[4,56,768]{2,1,0:T(8,128)(2,1)S(1)} collective-permute-done((bf16[4,56,768]{2,1,0:T(8,128)(2,1)}, bf16[4,56,768]{2,1,0:T(8,128)(2,1)S(1)}, u32[]{:S(2)}, u32[]{:S(2)}) %collective-permute-start.5) | collective-permute-done | bytes 344096 | tf_op jit(solution)/shard_map/ppermute | solution.py:246
  72.0 19.6 %collective-permute-done.6 = bf16[4,2,56,768]{3,2,1,0:T(8,128)(2,1)S(1)} collective-permute-done((bf16[4,2,56,768]{3,2,1,0:T(8,128)(2,1)S(1)}, bf16[4,2,56,768]{3,2,1,0:T(8,128)(2,1)S(1)}, u32[]{:S(2)}, u32[]{:S(2)}) %collective-permute-start.6) | collective-permute-done | bytes 688160 | tf_op jit(solution)/shard_map/ppermute | solution.py:246
  102.1 14.4 %attention_forward.1 = (bf16[512,768]{1,0:T(8,128)(2,1)}, bf16[512,768]{1,0:T(8,128)(2,1)}, bf16[512,768]{1,0:T(8,128)(2,1)}, bf16[512,768]{1,0:T(8,128)(2,1)}, ...) custom-call(s32[1]{0:T(128)} %bitcast.3.core, bf16[16,56,768]{2,1,0:T(8,128)(2,1)} %bitcast.16.refs_0_.refs_2_, ...), custom_call_target="tpu_custom_call" | custom-call | tf_op jit(solution)/shard_map/attention_forward/pallas_call | solution.py:328
  119.8 15.4 %ffn_forward.1 = (bf16[512,3072]{1,0:T(8,128)(2,1)}, f32[512,3072]{1,0:T(8,128)}, f32[512,768]{1,0:T(8,128)}, bf16[512,768]{1,0:T(8,128)(2,1)}) custom-call(bf16[32,224,768]{2,1,0:T(8,128)(2,1)} %bitcast.149, bf16[32,224,768]{2,1,0:T(8,128)(2,1)} %bitcast.150, bf16[512,768]{1,0:T(8,128)(2,1)} %get-tuple-element.115.refs_2_.refs_9_, ...), custom_call_target="tpu_custom_call" | custom-call | tf_op jit(solution)/shard_map/ffn_forward/pallas_call | solution.py:400
  156.4 6.1 %collective-permute-done.9 = bf16[128,768]{1,0:T(8,128)(2,1)S(1)} collective-permute-done((bf16[128,768]{1,0:T(8,128)(2,1)}, bf16[128,768]{1,0:T(8,128)(2,1)S(1)}, u32[]{:S(2)}, u32[]{:S(2)}) %collective-permute-start.9) | collective-permute-done | bytes 196640 | tf_op jit(solution)/shard_map/ppermute | solution.py:831
  176.2 7.8 %fusion.6 = bf16[2048,768]{1,0:T(8,128)(2,1)} fusion(bf16[1568,768]{1,0:T(8,128)(2,1)S(1)} %copy-done, s32[2048]{0:T(1024)S(1)} %bitcast.169), kind=kOutput, calls=%fused_computation.15 | convolution fusion | flops 4937285632 | bytes 5562368 | tf_op jit(solution)/shard_map/dot_general | solution.py:43
  184.0 6.1 %compact_rows.2.refs_0_ = bf16[2048,768]{1,0:T(8,128)(2,1)} custom-call(s32[4]{0:T(128)} %pad_add_fusion.place, s32[32]{0:T(128)} %add.621.places, s32[32]{0:T(128)} %copy-done.19, s32[10]{0:T(128)} %constant.197.clone.indices, bf16[2,10,128,384]{3,2,1,0:T(8,128)(2,1)} %copy-done.3, bf16[2,10,128,384]{3,2,1,0:T(8,128)(2,1)} %collective-permute-done.19.other_ref), custom_call_target="tpu_custom_call" | custom-call | tf_op jit(solution)/shard_map/compact_rows/pallas_call | solution.py:974
  196.8 6.1 %compact_rows.3 = bf16[2048,768]{1,0:T(8,128)(2,1)} custom-call(s32[4]{0:T(128)} %pad_add_fusion.place, s32[32]{0:T(128)} %add.621.places, s32[32]{0:T(128)} %copy-done.19, s32[6]{0:T(128)} %constant.198.clone.indices, bf16[2,6,128,384]{3,2,1,0:T(8,128)(2,1)} %copy-done.4, bf16[2,6,128,384]{3,2,1,0:T(8,128)(2,1)} %collective-permute-done.20.other_ref, ...), custom_call_target="tpu_custom_call" | custom-call | tf_op jit(solution)/shard_map/compact_rows/pallas_call | solution.py:974
  202.9 7.3 %fusion.58 = (f32[2048]{0:T(1024)S(1)}, f32[2048,1568]{0,1:T(8,128)S(1)}) fusion(f32[1568]{0:T(1024)S(1)} %convert_element_type.662, bf16[2048,768]{1,0:T(8,128)(2,1)} %compact_rows.3, bf16[1568,768]{1,0:T(8,128)(2,1)S(1)} %copy-done), kind=kOutput, calls=%fused_computation.204 | convolution fusion | flops 4938921984 | bytes 18413696 | tf_op jit(solution)/shard_map/dot_general | solution.py:53
  236.1 8.1 %spread_rows.1 = (bf16[16,128,384]{2,1,0:T(8,128)(2,1)}, bf16[16,128,384]{2,1,0:T(8,128)(2,1)}, bf16[16,128,384]{2,1,0:T(8,128)(2,1)}, bf16[16,128,384]{2,1,0:T(8,128)(2,1)}) custom-call(s32[4]{0:T(128)} %pad_add_fusion.place, s32[32]{0:T(128)} %add.621.places, s32[32]{0:T(128)} %copy-done.19, bf16[2048,768]{1,0:T(8,128)(2,1)} %pad_maximum_fusion.rows_ref), custom_call_target="tpu_custom_call" | custom-call | tf_op jit(solution)/shard_map/spread_rows/pallas_call | solution.py:1095
  252.7 12.2 %convert_reduce_fusion = (f32[1568]{0:T(1024)}, bf16[2048,1568]{0,1:T(8,128)(2,1)}) fusion(s32[2048]{0:T(1024)S(1)} %bitcast.171, f32[2048,1568]{0,1:T(8,128)} %copy-done.2, f32[2048]{0:T(1024)S(1)} %get-tuple-element.287), kind=kLoop, calls=%fused_computation.2 | loop fusion | flops 22477280 | bytes 19290240 | tf_op jit(solution)/shard_map/reduce_sum | solution.py:1270
  276.0 8.6 %fusion.59 = f32[1568,768]{1,0:T(8,128)} fusion(bf16[2048,1568]{0,1:T(8,128)(2,1)} %get-tuple-element.140, bf16[2048,768]{1,0:T(8,128)(2,1)S(1)} %copy-done.5), kind=kOutput, calls=%fused_computation.205 | convolution fusion | flops 4932501504 | bytes 14385152 | tf_op jit(solution)/shard_map/dot_general | solution.py:47
  292.4 5.1 %collective-permute-done.36 = bf16[128,768]{1,0:T(8,128)(2,1)S(1)} collective-permute-done((bf16[128,768]{1,0:T(8,128)(2,1)S(1)}, bf16[128,768]{1,0:T(8,128)(2,1)S(1)}, u32[]{:S(2)}, u32[]{:S(2)}) %collective-permute-start.36) | collective-permute-done | bytes 196640 | tf_op jit(solution)/shard_map/ppermute | solution.py:831
  297.5 9.4 %collective-permute-done.35 = bf16[128,768]{1,0:T(8,128)(2,1)S(1)} collective-permute-done((bf16[128,768]{1,0:T(8,128)(2,1)S(1)}, bf16[128,768]{1,0:T(8,128)(2,1)S(1)}, u32[]{:S(2)}, u32[]{:S(2)}) %collective-permute-start.35) | collective-permute-done | bytes 196640 | tf_op jit(solution)/shard_map/ppermute | solution.py:831
  309.0 21.4 %feed_backward.1 = (f32[512,768]{1,0:T(8,128)}, f32[8,768]{1,0:T(8,128)}, bf16[16,216,384]{2,1,0:T(8,128)(2,1)}, bf16[16,216,384]{2,1,0:T(8,128)(2,1)}, bf16[16,...) custom-call(s32[4]{0:T(128)} %pad_add_fusion.place, bf16[32,224,768]{2,1,0:T(8,128)(2,1)} %bitcast.154, ...), custom_call_target="tpu_custom_call" | custom-call | tf_op jit(solution)/shard_map/feed_backward/pallas_call | solution.py:540
  331.0 5.2 %out_backward.1 = (f32[512,768]{1,0:T(8,128)}, bf16[512,768]{1,0:T(8,128)(2,1)}, bf16[512,768]{1,0:T(8,128)(2,1)}, f32[8,768]{1,0:T(8,128)}) custom-call(s32[1]{0:T(128)} %bitcast.3.core, bf16[16,56,768]{2,1,0:T(8,128)(2,1)} %bitcast.23.refs_4_.refs_6_.refs_0_, bf16[16,56,768]{2,1,0:T(8,128)(2,1)} %collective-permute-done.7.refs_5_.refs_7_.refs_1_, ...), custom_call_target="tpu_custom_call" | custom-call | tf_op jit(solution)/shard_map/out_backward/pallas_call | solution.py:592
  347.3 8.2 %attention_backward.2 = (bf16[512,384]{1,0:T(8,128)(2,1)}, bf16[512,384]{1,0:T(8,128)(2,1)}, bf16[512,384]{1,0:T(8,128)(2,1)}, f32[8,384]{1,0:T(8,128)}) custom-call(bf16[512,768]{1,0:T(8,128)(2,1)} %get-tuple-element.172.refs_0_, bf16[512,768]{1,0:T(8,128)(2,1)} %get-tuple-element.160.refs_1_, bf16[512,768]{1,0:T(8,128)(2,1)} %get-tuple-element.161.refs_2_, ...), custom_call_target="tpu_custom_call" | custom-call | tf_op jit(solution)/shard_map/attention_backward/pallas_call | solution.py:652
  355.4 8.4 %attention_backward.3 = (bf16[512,384]{1,0:T(8,128)(2,1)}, bf16[512,384]{1,0:T(8,128)(2,1)}, bf16[512,384]{1,0:T(8,128)(2,1)}, f32[8,384]{1,0:T(8,128)}) custom-call(bf16[512,768]{1,0:T(8,128)(2,1)} %get-tuple-element.172.refs_0_, bf16[512,768]{1,0:T(8,128)(2,1)} %get-tuple-element.160.refs_1_, bf16[512,768]{1,0:T(8,128)(2,1)} %get-tuple-element.161.refs_2_, ...), custom_call_target="tpu_custom_call" | custom-call | tf_op jit(solution)/shard_map/attention_backward/pallas_call | solution.py:652
  363.9 8.9 %last_grads.1 = (bf16[16,112,384]{2,1,0:T(8,128)(2,1)}, bf16[16,112,384]{2,1,0:T(8,128)(2,1)}, bf16[16,112,384]{2,1,0:T(8,128)(2,1)}, bf16[16,112,384]{2,1,0:T(8,128)(2,1)}) custom-call(s32[4]{0:T(128)} %pad_add_fusion.place, bf16[512,768]{1,0:T(8,128)(2,1)} %refs_0_.5, bf16[512,768]{1,0:T(8,128)(2,1)} %get-tuple-element.166.refs_1_, ...), custom_call_target="tpu_custom_call" | custom-call | tf_op jit(solution)/shard_map/last_grads/pallas_call | solution.py:730
  391.2 6.9 %tokens_backward.1 = f32[512,768]{1,0:T(8,128)} custom-call(s32[1]{0:T(128)} %bitcast.3.core, bf16[16,56,768]{2,1,0:T(8,128)(2,1)} %bitcast.16.refs_0_.refs_2_, bf16[16,56,768]{2,1,0:T(8,128)(2,1)} %collective-permute-done.4.refs_1_.refs_3_, bf16[16,56,768]{2,1,0:T(8,128)(2,1)} %bitcast.16.refs_0_.refs_2_, ...), custom_call_target="tpu_custom_call" | custom-call | tf_op jit(solution)/shard_map/tokens_backward/pallas_call | solution.py:770
  408.4 5.6 %collective-permute-done.45 = bf16[8,112,384]{2,1,0:T(8,128)(2,1)} collective-permute-done((bf16[8,112,384]{2,1,0:T(8,128)(2,1)}, bf16[8,112,384]{2,1,0:T(8,128)(2,1)}, u32[]{:S(2)}, u32[]{:S(2)}) %collective-permute-start.45) | collective-permute-done | bytes 688160 | tf_op jit(solution)/shard_map/ppermute | solution.py:831
  418.9 10.8 %collective-permute-done.53 = bf16[216,768]{1,0:T(8,128)(2,1)S(1)} collective-permute-done((bf16[216,768]{1,0:T(8,128)(2,1)S(1)}, bf16[216,768]{1,0:T(8,128)(2,1)S(1)}, u32[]{:S(2)}, u32[]{:S(2)}) %collective-permute-start.53) | collective-permute-done | bytes 331808 | tf_op jit(solution)/shard_map/ppermute | solution.py:831
  442.4 5.3 %collective-permute-done.48 = bf16[112,768]{1,0:T(8,128)(2,1)S(1)} collective-permute-done((bf16[112,768]{1,0:T(8,128)(2,1)S(1)}, bf16[112,768]{1,0:T(8,128)(2,1)S(1)}, u32[]{:S(2)}, u32[]{:S(2)}) %collective-permute-start.48) | collective-permute-done | bytes 172064 | tf_op jit(solution)/shard_map/ppermute | solution.py:831
  (278 shorter events, 202.4 us)
Async XLA Ops:
  7.2 112.6 %all-gather.3.cloned.1.call-start = ((), (), s32[]{:S(2)}) async-start(), calls=%async_computation | async-start | bytes 11354112 | tf_op jit(solution)/shard_map/all_gather | solution.py:1155
  24.0 24.8 %collective-permute-start.1 = (bf16[2,112,768]{2,1,0:T(8,128)(2,1)S(1)}, bf16[2,112,768]{2,1,0:T(8,128)(2,1)S(1)}, u32[]{:S(2)}, u32[]{:S(2)}) collective-permute-start(bf16[2,112,768]{2,1,0:T(8,128)(2,1)S(1)} %maximum_bitcast_fusion), channel_id=1, source_target_pairs={{0,16},{2,18},{4,20},{6,22},{8,24},{10,26},{12,28},{14,30},{16,0},... | collective-permute-start | bytes 1032200 | tf_op jit(solution)/shard_map/ppermute | solution.py:246
  51.3 17.3 %collective-permute-start.2 = (bf16[4,56,768]{2,1,0:T(8,128)(2,1)}, bf16[4,56,768]{2,1,0:T(8,128)(2,1)}, u32[]{:S(2)}, u32[]{:S(2)}) collective-permute-start(bf16[4,56,768]{2,1,0:T(8,128)(2,1)} %get-tuple-element.261), channel_id=1, source_target_pairs={{0,2},{2,0},{4,6},{6,4},{8,10},{10,8},{12,14},{14,12},{16,18},{18,... | collective-permute-start | bytes 1032200 | tf_op jit(solution)/shard_map/ppermute | solution.py:246
  69.8 21.8 %collective-permute-start.6 = (bf16[4,2,56,768]{3,2,1,0:T(8,128)(2,1)S(1)}, bf16[4,2,56,768]{3,2,1,0:T(8,128)(2,1)S(1)}, u32[]{:S(2)}, u32[]{:S(2)}) collective-permute-start(bf16[4,2,56,768]{3,2,1,0:T(8,128)(2,1)S(1)} %pad_maximum_fusion.7), channel_id=1, source_target_pairs={{0,2},{2,0},{4,6},{6,4},{8,10},{10,8},{12,14},{14,12},{16,18},{18,... | collective-permute-start | bytes 2064392 | tf_op jit(solution)/shard_map/ppermute | solution.py:246
  70.3 22.6 %collective-permute-start.3 = (bf16[4,2,56,768]{3,2,0,1:T(8,128)(2,1)S(1)}, bf16[4,2,56,768]{3,2,0,1:T(8,128)(2,1)S(1)}, u32[]{:S(2)}, u32[]{:S(2)}) collective-permute-start(bf16[4,2,56,768]{3,2,0,1:T(8,128)(2,1)S(1)} %pad_maximum_fusion.6), channel_id=1, source_target_pairs={{0,4},{2,6},{4,0},{6,2},{8,12},{10,14},{12,8},{14,10},{16,20},{18,... | collective-permute-start | bytes 2064392 | tf_op jit(solution)/shard_map/ppermute | solution.py:246
  138.3 18.1 %collective-permute-start.10 = (bf16[128,768]{1,0:T(8,128)(2,1)}, bf16[128,768]{1,0:T(8,128)(2,1)S(1)}, u32[]{:S(2)}, u32[]{:S(2)}) collective-permute-start(bf16[128,768]{1,0:T(8,128)(2,1)} %get-tuple-element.119), channel_id=1, source_target_pairs={{0,24},{2,26},{4,28},{6,30},{8,16},{10,18},{12,20},{14,22},{16,8},... | collective-permute-start | bytes 589832 | tf_op jit(solution)/shard_map/ppermute | solution.py:831
  153.5 18.3 %collective-permute-start.18 = (bf16[2,128,384]{2,1,0:T(8,128)(2,1)S(1)}, bf16[2,128,384]{2,1,0:T(8,128)(2,1)S(1)}, u32[]{:S(2)}, u32[]{:S(2)}) collective-permute-start(bf16[2,128,384]{2,1,0:T(8,128)(2,1)S(1)} %pad_maximum_fusion.17), channel_id=1, source_target_pairs={{0,2},{2,0},{4,6},{6,4},{8,10},{10,8},{12,14},{14,12},{16,18},{18,... | collective-permute-start | bytes 589832 | tf_op jit(solution)/shard_map/ppermute | solution.py:831
  155.3 16.6 %collective-permute-start.17 = (bf16[2,128,384]{2,1,0:T(8,128)(2,1)S(1)}, bf16[2,128,384]{2,1,0:T(8,128)(2,1)S(1)}, u32[]{:S(2)}, u32[]{:S(2)}) collective-permute-start(bf16[2,128,384]{2,1,0:T(8,128)(2,1)S(1)} %pad_maximum_fusion.16), channel_id=1, source_target_pairs={{0,4},{2,6},{4,0},{6,2},{8,12},{10,14},{12,8},{14,10},{16,20},{18,... | collective-permute-start | bytes 589832 | tf_op jit(solution)/shard_map/ppermute | solution.py:831
  173.1 17.0 %collective-permute-start.15 = (bf16[6,128,384]{2,1,0:T(8,128)(2,1)S(1)}, bf16[6,128,384]{2,1,0:T(8,128)(2,1)}, u32[]{:S(2)}, u32[]{:S(2)}) collective-permute-start(bf16[6,128,384]{2,1,0:T(8,128)(2,1)S(1)} %pad_maximum_fusion.9), channel_id=1, source_target_pairs={{0,4},{2,6},{4,0},{6,2},{8,12},{10,14},{12,8},{14,10},{16,20},{18,... | collective-permute-start | bytes 1769480 | tf_op jit(solution)/shard_map/ppermute | solution.py:831
  175.8 15.6 %collective-permute-start.16 = (bf16[6,128,384]{2,1,0:T(8,128)(2,1)}, bf16[6,128,384]{2,1,0:T(8,128)(2,1)}, u32[]{:S(2)}, u32[]{:S(2)}) collective-permute-start(bf16[6,128,384]{2,1,0:T(8,128)(2,1)} %pad_maximum_fusion.10), channel_id=1, source_target_pairs={{0,2},{2,0},{4,6},{6,4},{8,10},{10,8},{12,14},{14,12},{16,18},{18,... | collective-permute-start | bytes 1769480 | tf_op jit(solution)/shard_map/ppermute | solution.py:831
  249.7 19.6 %collective-permute-start.29 = (bf16[8,128,384]{2,1,0:T(8,128)(2,1)S(1)}, bf16[8,128,384]{2,1,0:T(8,128)(2,1)}, u32[]{:S(2)}, u32[]{:S(2)}) collective-permute-start(bf16[8,128,384]{2,1,0:T(8,128)(2,1)S(1)} %add_convert_fusion.3), channel_id=1, source_target_pairs={{0,2},{2,0},{4,6},{6,4},{8,10},{10,8},{12,14},{14,12},{16,18},{18,... | collective-permute-start | bytes 2359304 | tf_op jit(solution)/shard_map/ppermute | solution.py:831
  251.7 19.3 %collective-permute-start.31 = (bf16[8,128,384]{2,1,0:T(8,128)(2,1)S(1)}, bf16[8,128,384]{2,1,0:T(8,128)(2,1)}, u32[]{:S(2)}, u32[]{:S(2)}) collective-permute-start(bf16[8,128,384]{2,1,0:T(8,128)(2,1)S(1)} %add_convert_fusion.2), channel_id=1, source_target_pairs={{0,4},{2,6},{4,0},{6,2},{8,12},{10,14},{12,8},{14,10},{16,20},{18,... | collective-permute-start | bytes 2359304 | tf_op jit(solution)/shard_map/ppermute | solution.py:831
  290.0 16.9 %collective-permute-start.35 = (bf16[128,768]{1,0:T(8,128)(2,1)S(1)}, bf16[128,768]{1,0:T(8,128)(2,1)S(1)}, u32[]{:S(2)}, u32[]{:S(2)}) collective-permute-start(bf16[128,768]{1,0:T(8,128)(2,1)S(1)} %pad_maximum_fusion.19), channel_id=1, source_target_pairs={{0,16},{2,18},{4,20},{6,22},{8,24},{10,26},{12,28},{14,30},{16,0},... | collective-permute-start | bytes 589832 | tf_op jit(solution)/shard_map/ppermute | solution.py:831
  291.2 15.7 %collective-permute-start.34 = (bf16[128,768]{1,0:T(8,128)(2,1)S(1)}, bf16[128,768]{1,0:T(8,128)(2,1)S(1)}, u32[]{:S(2)}, u32[]{:S(2)}) collective-permute-start(bf16[128,768]{1,0:T(8,128)(2,1)S(1)} %pad_maximum_fusion.18), channel_id=1, source_target_pairs={{0,8},{2,10},{4,12},{6,14},{8,0},{10,2},{12,4},{14,6},{16,24},{18,... | collective-permute-start | bytes 589832 | tf_op jit(solution)/shard_map/ppermute | solution.py:831
  344.2 31.5 %collective-permute-start.39 = (bf16[8,216,384]{2,1,0:T(8,128)(2,1)}, bf16[8,216,384]{2,1,0:T(8,128)(2,1)}, u32[]{:S(2)}, u32[]{:S(2)}) collective-permute-start(bf16[8,216,384]{2,1,0:T(8,128)(2,1)} %get-tuple-element.179), channel_id=1, source_target_pairs={{0,2},{2,0},{4,6},{6,4},{8,10},{10,8},{12,14},{14,12},{16,18},{18,... | collective-permute-start | bytes 3981320 | tf_op jit(solution)/shard_map/ppermute | solution.py:831
  345.2 31.2 %collective-permute-start.40 = (bf16[8,216,384]{2,1,0:T(8,128)(2,1)}, bf16[8,216,384]{2,1,0:T(8,128)(2,1)}, u32[]{:S(2)}, u32[]{:S(2)}) collective-permute-start(bf16[8,216,384]{2,1,0:T(8,128)(2,1)} %get-tuple-element.180), channel_id=1, source_target_pairs={{0,4},{2,6},{4,0},{6,2},{8,12},{10,14},{12,8},{14,10},{16,20},{18,... | collective-permute-start | bytes 3981320 | tf_op jit(solution)/shard_map/ppermute | solution.py:831
  380.7 18.2 %collective-permute-start.51 = (bf16[4,216,384]{2,1,0:T(8,128)(2,1)}, bf16[4,216,384]{2,1,0:T(8,128)(2,1)}, u32[]{:S(2)}, u32[]{:S(2)}) collective-permute-start(bf16[4,216,384]{2,1,0:T(8,128)(2,1)} %add_convert_fusion.6), channel_id=1, source_target_pairs={{0,2},{2,0},{4,6},{6,4},{8,10},{10,8},{12,14},{14,12},{16,18},{18,... | collective-permute-start | bytes 1990664 | tf_op jit(solution)/shard_map/ppermute | solution.py:831
  383.5 18.0 %collective-permute-start.50 = (bf16[4,216,384]{2,1,0:T(8,128)(2,1)S(1)}, bf16[4,216,384]{2,1,0:T(8,128)(2,1)}, u32[]{:S(2)}, u32[]{:S(2)}) collective-permute-start(bf16[4,216,384]{2,1,0:T(8,128)(2,1)S(1)} %add_convert_fusion.7), channel_id=1, source_target_pairs={{0,4},{2,6},{4,0},{6,2},{8,12},{10,14},{12,8},{14,10},{16,20},{18,... | collective-permute-start | bytes 1990664 | tf_op jit(solution)/shard_map/ppermute | solution.py:831
  389.4 24.6 %collective-permute-start.45 = (bf16[8,112,384]{2,1,0:T(8,128)(2,1)}, bf16[8,112,384]{2,1,0:T(8,128)(2,1)}, u32[]{:S(2)}, u32[]{:S(2)}) collective-permute-start(bf16[8,112,384]{2,1,0:T(8,128)(2,1)} %add_convert_fusion.4), channel_id=1, source_target_pairs={{0,4},{2,6},{4,0},{6,2},{8,12},{10,14},{12,8},{14,10},{16,20},{18,... | collective-permute-start | bytes 2064392 | tf_op jit(solution)/shard_map/ppermute | solution.py:831
  390.2 26.1 %collective-permute-start.43 = (bf16[8,112,384]{2,1,0:T(8,128)(2,1)}, bf16[8,112,384]{2,1,0:T(8,128)(2,1)S(1)}, u32[]{:S(2)}, u32[]{:S(2)}) collective-permute-start(bf16[8,112,384]{2,1,0:T(8,128)(2,1)} %add_convert_fusion.5), channel_id=1, source_target_pairs={{0,2},{2,0},{4,6},{6,4},{8,10},{10,8},{12,14},{14,12},{16,18},{18,... | collective-permute-start | bytes 2064392 | tf_op jit(solution)/shard_map/ppermute | solution.py:831
  405.2 24.4 %collective-permute-start.53 = (bf16[216,768]{1,0:T(8,128)(2,1)S(1)}, bf16[216,768]{1,0:T(8,128)(2,1)S(1)}, u32[]{:S(2)}, u32[]{:S(2)}) collective-permute-start(bf16[216,768]{1,0:T(8,128)(2,1)S(1)} %pad_maximum_fusion.12), channel_id=1, source_target_pairs={{0,16},{2,18},{4,20},{6,22},{8,24},{10,26},{12,28},{14,30},{16,0},... | collective-permute-start | bytes 995336 | tf_op jit(solution)/shard_map/ppermute | solution.py:831
  405.3 24.3 %collective-permute-start.52 = (bf16[216,768]{1,0:T(8,128)(2,1)S(1)}, bf16[216,768]{1,0:T(8,128)(2,1)S(1)}, u32[]{:S(2)}, u32[]{:S(2)}) collective-permute-start(bf16[216,768]{1,0:T(8,128)(2,1)S(1)} %pad_maximum_fusion.11), channel_id=1, source_target_pairs={{0,8},{2,10},{4,12},{6,14},{8,0},{10,2},{12,4},{14,6},{16,24},{18,... | collective-permute-start | bytes 995336 | tf_op jit(solution)/shard_map/ppermute | solution.py:831
  415.2 16.0 %collective-permute-start.46 = (bf16[4,112,384]{2,1,0:T(8,128)(2,1)S(1)}, bf16[4,112,384]{2,1,0:T(8,128)(2,1)S(1)}, u32[]{:S(2)}, u32[]{:S(2)}) collective-permute-start(bf16[4,112,384]{2,1,0:T(8,128)(2,1)S(1)} %add_convert_fusion.10), channel_id=1, source_target_pairs={{0,2},{2,0},{4,6},{6,4},{8,10},{10,8},{12,14},{14,12},{16,18},{18,... | collective-permute-start | bytes 1032200 | tf_op jit(solution)/shard_map/ppermute | solution.py:831
  417.4 15.2 %collective-permute-start.44 = (bf16[4,112,384]{2,1,0:T(8,128)(2,1)S(1)}, bf16[4,112,384]{2,1,0:T(8,128)(2,1)S(1)}, u32[]{:S(2)}, u32[]{:S(2)}) collective-permute-start(bf16[4,112,384]{2,1,0:T(8,128)(2,1)S(1)} %add_convert_fusion.11), channel_id=1, source_target_pairs={{0,4},{2,6},{4,0},{6,2},{8,12},{10,14},{12,8},{14,10},{16,20},{18,... | collective-permute-start | bytes 1032200 | tf_op jit(solution)/shard_map/ppermute | solution.py:831
  (53 other events, 577.8 us)
Sparse Core Ops, SparseCore 0:
  11.5 108.2 all-gather.2

commit v5 on v4

--- a/solution.py
+++ b/solution.py
@@ -456,18 +456,20 @@
 
 
 def feed_back_kernel(place, *refs, sizes, share, down_share):
-    up_refs, down_refs = refs[: sizes[0]], refs[sizes[0] : sum(sizes)]
-    (cotangent_ref, picker_ref, picked_ref, summed_ref, vector_ref, own_ref, dense_ref) = refs[
-        sum(sizes) : sum(sizes) + 7
+    up_refs, down_refs = refs[: sizes[0]], refs[sizes[0] : sizes[0] + sizes[1]]
+    head_refs = refs[sizes[0] + sizes[1] : sum(sizes)]
+    (cotangent_ref, picker_ref, summed_ref, vector_ref, own_ref, dense_ref) = refs[
+        sum(sizes) : sum(sizes) + 6
     ]
-    hidden_ref, active_ref, slope_ref, total_ref, sums_ref, *outs = refs[sum(sizes) + 7 : -2]
+    hidden_ref, active_ref, slope_ref, total_ref, sums_ref, *outs = refs[sum(sizes) + 6 : -2]
     low_ref, turned_ref = refs[-2:]
     step = pl.program_id(0)
     width = vector_ref.shape[1]
 
     @pl.when(step == 0)
     def _():
-        grad = to_full(cotangent_ref[...]) + matmul_tn(picker_ref[...], picked_ref[...])
+        picked_grad = to_low(matmul_nt(dense_ref[...], read_weight(head_refs, None)))
+        grad = to_full(cotangent_ref[...]) + matmul_tn(picker_ref[...], picked_grad)
         summed_grad, gain_grad, shift_grad = norm_backward(
             summed_ref[...], vector_ref[6:7, :], grad
         )
@@ -503,14 +505,15 @@
         outs[1][...] = down_grad
 
 
-def feed_backward(place, count, cotangent, picker, picked_grad, summed, vectors, own, dense, hidden, active, slope, weights):
+def feed_backward(place, count, cotangent, picker, summed, vectors, own, dense, hidden, active, slope, weights):
     rows, width = cotangent.shape
     steps = active.shape[1] // width
     share, down_share, chips = width // count, active.shape[1] // count, count // 2
     aligned = share % 8 == 0
     first, first_specs = up_operands_of(weights, steps)
     second, second_specs = weights.operands(steps, None, width, lambda s, c: 0, steps, lambda s, c: s)
-    operands = [cotangent, picker, picked_grad, summed, vectors, own, dense, hidden]
+    third, third_specs = weights.operands(steps + 1, None, width, lambda s, c: 0)
+    operands = [cotangent, picker, summed, vectors, own, dense, hidden]
     block = pl.BlockSpec((rows, width), lambda s, c: (0, s))
     low = jnp.bfloat16
     if aligned:
@@ -533,7 +536,7 @@
     ]
     kernel = functools.partial(
         feed_back_kernel,
-        sizes=[len(first), len(second)],
+        sizes=[len(first), len(second), len(third)],
         share=share,
         down_share=down_share if aligned else 0,
     )
@@ -545,6 +548,7 @@
             in_specs=[
                 *first_specs,
                 *second_specs,
+                *third_specs,
                 *[whole(operand) for operand in operands],
                 block,
                 block,
@@ -555,7 +559,7 @@
         out_shape=[*common, *out_shape],
         compiler_params=pltpu.CompilerParams(dimension_semantics=("arbitrary",)),
         name="feed_backward",
-    )(place, *first, *second, *operands, active, slope)
+    )(place, *first, *second, *third, *operands, active, slope)
     if not aligned:
         away, kept = arranged([*column_blocks(outs[0], width), *outs[1:]], place)
     else:
@@ -1089,7 +1093,7 @@
 def spread(place, places, counts, rows, slots):
     chips = places.shape[0] // 2
     total, width = rows.shape
-    batch = 2
+    batch = 4
     block = pl.BlockSpec((batch, slots, width // 2), lambda i, *_: (i, 0, 0))
     shape = jax.ShapeDtypeStruct((chips, slots, width // 2), jnp.bfloat16)
     outs = pl.pallas_call(
@@ -1279,14 +1283,11 @@
     dense_grad, head_gain_grad, head_shift_grad = tail_back(normed_grad)
     dense_grad_low = to_low(dense_grad)
     dense_bias_grad = jnp.sum(to_full(dense_grad_low), axis=0)
-    dense_full = Weights([gathered_late], later.shares).natural(steps + 1, None)
-    picked_grad = to_low(matmul_nt(dense_grad_low, dense_full))
     hidden_grad, feed_sums, *feed_grads = feed_backward(
         here,
         count,
         cotangent,
         picker_low,
-        picked_grad,
         summed2,
         vectors,
         own_rows,

time: 464 us -> 462 us (level)
  transfers between devices with their start and end apart: 56 -> 56, of which waited for: 27 -> 28; matrix products, arithmetic and copies ran while one was open for 18% -> 18% of each run, Pallas kernels for 14% -> 14%
where the time goes in v5:
time: 462 us; the launch traced here: 457 us
  waiting for transfers between devices  137 us (30%)
  Pallas kernels  123 us (27%)
  other arithmetic  72.9 us (16%)
  starting transfers between devices  62.3 us (13%)
  matrix products  30.4 us (7%)
  between operations  17.5 us (4%)
  local copies, waits for them, and re-layouts  14.5 us (3%)
    ppermute x32, waiting for transfers between devices, along(): lax.ppermute(sent, 'dp', [(chip, chip ^ stride) for chip in range(chips)])  62.9 us
    ppermute x6, waiting for transfers between devices, double(): lax.ppermute(value, 'dp', [(chip, chip ^ stride) for chip in range(chips)])  62 us
    ppermute x32, starting transfers between devices, along(): lax.ppermute(sent, 'dp', [(chip, chip ^ stride) for chip in range(chips)])  41.1 us
    pallas_call x1, Pallas kernels, feed_backward(): pl.pallas_call(kernel, grid_spec=pltpu.PrefetchScalarGridSpec(num_scalar_...  21.7 us
    convert_element_type x12, other arithmetic, to_low(): return values.astype(jnp.bfloat16)  21.6 us
    pallas_call x2, Pallas kernels, attention_backward(): pl.pallas_call(functools.partial(attention_back_kernel, first_head=start...  16.6 us
    pallas_call x1, Pallas kernels, ffn_forward(): pl.pallas_call(functools.partial(ffn_kernel, sizes=[len(first), len(secon...  15.4 us
    pallas_call x1, Pallas kernels, attention_forward(): pl.pallas_call(functools.partial(attention_kernel, sizes=sizes), grid_spe...  14.5 us
  transfers between devices with their start and end apart: 56, of which 28 were waited for; matrix products, arithmetic and copies ran while one was open for 18% of the time, Pallas kernels for 14%

profile of v5, /device:TPU:0, one launch (start us, length us, event | category | flops | bytes accessed | tf_op | source)
XLA Modules:
  0.0 457.3 jit_solution(12011781467529525206)
XLA Ops:
  26.9 22.0 %collective-permute-done.1 = bf16[2,112,768]{2,1,0:T(8,128)(2,1)S(1)} collective-permute-done((bf16[2,112,768]{2,1,0:T(8,128)(2,1)S(1)}, bf16[2,112,768]{2,1,0:T(8,128)(2,1)S(1)}, u32[]{:S(2)}, u32[]{:S(2)}) %collective-permute-start.1) | collective-permute-done | bytes 344096 | tf_op jit(solution)/shard_map/ppermute | solution.py:246
  52.8 10.8 %collective-permute-done.5 = bf16[4,56,768]{2,1,0:T(8,128)(2,1)S(1)} collective-permute-done((bf16[4,56,768]{2,1,0:T(8,128)(2,1)}, bf16[4,56,768]{2,1,0:T(8,128)(2,1)S(1)}, u32[]{:S(2)}, u32[]{:S(2)}) %collective-permute-start.5) | collective-permute-done | bytes 344096 | tf_op jit(solution)/shard_map/ppermute | solution.py:246
  72.0 19.6 %collective-permute-done.6 = bf16[4,2,56,768]{3,2,1,0:T(8,128)(2,1)S(1)} collective-permute-done((bf16[4,2,56,768]{3,2,1,0:T(8,128)(2,1)S(1)}, bf16[4,2,56,768]{3,2,1,0:T(8,128)(2,1)S(1)}, u32[]{:S(2)}, u32[]{:S(2)}) %collective-permute-start.6) | collective-permute-done | bytes 688160 | tf_op jit(solution)/shard_map/ppermute | solution.py:246
  102.1 14.5 %attention_forward.1 = (bf16[512,768]{1,0:T(8,128)(2,1)}, bf16[512,768]{1,0:T(8,128)(2,1)}, bf16[512,768]{1,0:T(8,128)(2,1)}, bf16[512,768]{1,0:T(8,128)(2,1)}, ...) custom-call(s32[1]{0:T(128)} %bitcast.3.core, bf16[16,56,768]{2,1,0:T(8,128)(2,1)} %bitcast.16.refs_0_.refs_2_, ...), custom_call_target="tpu_custom_call" | custom-call | tf_op jit(solution)/shard_map/attention_forward/pallas_call | solution.py:328
  119.8 15.4 %ffn_forward.1 = (bf16[512,3072]{1,0:T(8,128)(2,1)}, f32[512,3072]{1,0:T(8,128)}, f32[512,768]{1,0:T(8,128)}, bf16[512,768]{1,0:T(8,128)(2,1)}) custom-call(bf16[32,224,768]{2,1,0:T(8,128)(2,1)} %bitcast.146, bf16[32,224,768]{2,1,0:T(8,128)(2,1)} %bitcast.147, bf16[512,768]{1,0:T(8,128)(2,1)} %get-tuple-element.115.refs_2_.refs_9_, ...), custom_call_target="tpu_custom_call" | custom-call | tf_op jit(solution)/shard_map/ffn_forward/pallas_call | solution.py:400
  156.4 6.1 %collective-permute-done.9 = bf16[128,768]{1,0:T(8,128)(2,1)S(1)} collective-permute-done((bf16[128,768]{1,0:T(8,128)(2,1)}, bf16[128,768]{1,0:T(8,128)(2,1)S(1)}, u32[]{:S(2)}, u32[]{:S(2)}) %collective-permute-start.9) | collective-permute-done | bytes 196640 | tf_op jit(solution)/shard_map/ppermute | solution.py:835
  176.2 7.8 %fusion.6 = bf16[2048,768]{1,0:T(8,128)(2,1)} fusion(bf16[1568,768]{1,0:T(8,128)(2,1)S(1)} %copy-done, s32[2048]{0:T(1024)S(1)} %bitcast.165), kind=kOutput, calls=%fused_computation.15 | convolution fusion | flops 4937285632 | bytes 5562368 | tf_op jit(solution)/shard_map/dot_general | solution.py:43
  184.0 6.1 %compact_rows.2.refs_0_ = bf16[2048,768]{1,0:T(8,128)(2,1)} custom-call(s32[4]{0:T(128)} %pad_add_fusion.place, s32[32]{0:T(128)} %add.621.places, s32[32]{0:T(128)} %copy-done.18, s32[10]{0:T(128)} %constant.197.clone.indices, bf16[2,10,128,384]{3,2,1,0:T(8,128)(2,1)} %copy-done.3, bf16[2,10,128,384]{3,2,1,0:T(8,128)(2,1)} %collective-permute-done.19.other_ref), custom_call_target="tpu_custom_call" | custom-call | tf_op jit(solution)/shard_map/compact_rows/pallas_call | solution.py:978
  196.8 6.1 %compact_rows.3 = bf16[2048,768]{1,0:T(8,128)(2,1)} custom-call(s32[4]{0:T(128)} %pad_add_fusion.place, s32[32]{0:T(128)} %add.621.places, s32[32]{0:T(128)} %copy-done.18, s32[6]{0:T(128)} %constant.198.clone.indices, bf16[2,6,128,384]{3,2,1,0:T(8,128)(2,1)} %copy-done.4, bf16[2,6,128,384]{3,2,1,0:T(8,128)(2,1)} %collective-permute-done.20.other_ref, ...), custom_call_target="tpu_custom_call" | custom-call | tf_op jit(solution)/shard_map/compact_rows/pallas_call | solution.py:978
  202.9 7.3 %fusion.58 = (f32[2048]{0:T(1024)S(1)}, f32[2048,1568]{0,1:T(8,128)S(1)}) fusion(f32[1568]{0:T(1024)S(1)} %convert_element_type.659, bf16[2048,768]{1,0:T(8,128)(2,1)} %compact_rows.3, bf16[1568,768]{1,0:T(8,128)(2,1)S(1)} %copy-done), kind=kOutput, calls=%fused_computation.203 | convolution fusion | flops 4938921984 | bytes 18413696 | tf_op jit(solution)/shard_map/dot_general | solution.py:53
  236.1 7.1 %spread_rows.1 = (bf16[16,128,384]{2,1,0:T(8,128)(2,1)}, bf16[16,128,384]{2,1,0:T(8,128)(2,1)}, bf16[16,128,384]{2,1,0:T(8,128)(2,1)}, bf16[16,128,384]{2,1,0:T(8,128)(2,1)}) custom-call(s32[4]{0:T(128)} %pad_add_fusion.place, s32[32]{0:T(128)} %add.621.places, s32[32]{0:T(128)} %copy-done.18, bf16[2048,768]{1,0:T(8,128)(2,1)} %pad_maximum_fusion.rows_ref), custom_call_target="tpu_custom_call" | custom-call | tf_op jit(solution)/shard_map/spread_rows/pallas_call | solution.py:1099
  250.9 12.4 %convert_reduce_fusion = (f32[1568]{0:T(1024)}, bf16[2048,1568]{0,1:T(8,128)(2,1)}) fusion(s32[2048]{0:T(1024)S(1)} %bitcast.167, f32[2048,1568]{0,1:T(8,128)} %copy-done.2, f32[2048]{0:T(1024)S(1)} %get-tuple-element.287), kind=kLoop, calls=%fused_computation.2 | loop fusion | flops 22477280 | bytes 19290240 | tf_op jit(solution)/shard_map/reduce_sum | solution.py:1274
  263.3 5.2 %collective-permute-done.29 = bf16[8,128,384]{2,1,0:T(8,128)(2,1)} collective-permute-done((bf16[8,128,384]{2,1,0:T(8,128)(2,1)S(1)}, bf16[8,128,384]{2,1,0:T(8,128)(2,1)}, u32[]{:S(2)}, u32[]{:S(2)}) %collective-permute-start.29) | collective-permute-done | bytes 786464 | tf_op jit(solution)/shard_map/ppermute | solution.py:835
  274.2 8.6 %fusion.59 = f32[1568,768]{1,0:T(8,128)} fusion(bf16[2048,1568]{0,1:T(8,128)(2,1)} %get-tuple-element.142, bf16[2048,768]{1,0:T(8,128)(2,1)S(1)} %copy-done.5), kind=kOutput, calls=%fused_computation.204 | convolution fusion | flops 4932501504 | bytes 14385152 | tf_op jit(solution)/shard_map/dot_general | solution.py:47
  295.5 9.1 %collective-permute-done.35 = bf16[128,768]{1,0:T(8,128)(2,1)S(1)} collective-permute-done((bf16[128,768]{1,0:T(8,128)(2,1)S(1)}, bf16[128,768]{1,0:T(8,128)(2,1)S(1)}, u32[]{:S(2)}, u32[]{:S(2)}) %collective-permute-start.35) | collective-permute-done | bytes 196640 | tf_op jit(solution)/shard_map/ppermute | solution.py:835
  306.2 21.7 %feed_backward.1 = (f32[512,768]{1,0:T(8,128)}, f32[8,768]{1,0:T(8,128)}, bf16[16,216,384]{2,1,0:T(8,128)(2,1)}, bf16[16,216,384]{2,1,0:T(8,128)(2,1)}, bf16[16,...) custom-call(s32[4]{0:T(128)} %pad_add_fusion.place, bf16[32,224,768]{2,1,0:T(8,128)(2,1)} %bitcast.150, ...), custom_call_target="tpu_custom_call" | custom-call | tf_op jit(solution)/shard_map/feed_backward/pallas_call | solution.py:543
  328.4 5.2 %out_backward.1 = (f32[512,768]{1,0:T(8,128)}, bf16[512,768]{1,0:T(8,128)(2,1)}, bf16[512,768]{1,0:T(8,128)(2,1)}, f32[8,768]{1,0:T(8,128)}) custom-call(s32[1]{0:T(128)} %bitcast.3.core, bf16[16,56,768]{2,1,0:T(8,128)(2,1)} %bitcast.23.refs_4_.refs_6_.refs_0_, bf16[16,56,768]{2,1,0:T(8,128)(2,1)} %collective-permute-done.7.refs_5_.refs_7_.refs_1_, ...), custom_call_target="tpu_custom_call" | custom-call | tf_op jit(solution)/shard_map/out_backward/pallas_call | solution.py:596
  344.8 8.2 %attention_backward.2 = (bf16[512,384]{1,0:T(8,128)(2,1)}, bf16[512,384]{1,0:T(8,128)(2,1)}, bf16[512,384]{1,0:T(8,128)(2,1)}, f32[8,384]{1,0:T(8,128)}) custom-call(bf16[512,768]{1,0:T(8,128)(2,1)} %get-tuple-element.172.refs_0_, bf16[512,768]{1,0:T(8,128)(2,1)} %get-tuple-element.160.refs_1_, bf16[512,768]{1,0:T(8,128)(2,1)} %get-tuple-element.161.refs_2_, ...), custom_call_target="tpu_custom_call" | custom-call | tf_op jit(solution)/shard_map/attention_backward/pallas_call | solution.py:656
  352.9 8.4 %attention_backward.3 = (bf16[512,384]{1,0:T(8,128)(2,1)}, bf16[512,384]{1,0:T(8,128)(2,1)}, bf16[512,384]{1,0:T(8,128)(2,1)}, f32[8,384]{1,0:T(8,128)}) custom-call(bf16[512,768]{1,0:T(8,128)(2,1)} %get-tuple-element.172.refs_0_, bf16[512,768]{1,0:T(8,128)(2,1)} %get-tuple-element.160.refs_1_, bf16[512,768]{1,0:T(8,128)(2,1)} %get-tuple-element.161.refs_2_, ...), custom_call_target="tpu_custom_call" | custom-call | tf_op jit(solution)/shard_map/attention_backward/pallas_call | solution.py:656
  361.4 8.9 %last_grads.1 = (bf16[16,112,384]{2,1,0:T(8,128)(2,1)}, bf16[16,112,384]{2,1,0:T(8,128)(2,1)}, bf16[16,112,384]{2,1,0:T(8,128)(2,1)}, bf16[16,112,384]{2,1,0:T(8,128)(2,1)}) custom-call(s32[4]{0:T(128)} %pad_add_fusion.place, bf16[512,768]{1,0:T(8,128)(2,1)} %refs_0_.5, bf16[512,768]{1,0:T(8,128)(2,1)} %get-tuple-element.166.refs_1_, ...), custom_call_target="tpu_custom_call" | custom-call | tf_op jit(solution)/shard_map/last_grads/pallas_call | solution.py:734
  389.0 6.9 %tokens_backward.1 = f32[512,768]{1,0:T(8,128)} custom-call(s32[1]{0:T(128)} %bitcast.3.core, bf16[16,56,768]{2,1,0:T(8,128)(2,1)} %bitcast.16.refs_0_.refs_2_, bf16[16,56,768]{2,1,0:T(8,128)(2,1)} %collective-permute-done.4.refs_1_.refs_3_, bf16[16,56,768]{2,1,0:T(8,128)(2,1)} %bitcast.16.refs_0_.refs_2_, ...), custom_call_target="tpu_custom_call" | custom-call | tf_op jit(solution)/shard_map/tokens_backward/pallas_call | solution.py:774
  405.9 5.5 %collective-permute-done.45 = bf16[8,112,384]{2,1,0:T(8,128)(2,1)} collective-permute-done((bf16[8,112,384]{2,1,0:T(8,128)(2,1)}, bf16[8,112,384]{2,1,0:T(8,128)(2,1)}, u32[]{:S(2)}, u32[]{:S(2)}) %collective-permute-start.45) | collective-permute-done | bytes 688160 | tf_op jit(solution)/shard_map/ppermute | solution.py:835
  416.4 11.1 %collective-permute-done.53 = bf16[216,768]{1,0:T(8,128)(2,1)S(1)} collective-permute-done((bf16[216,768]{1,0:T(8,128)(2,1)S(1)}, bf16[216,768]{1,0:T(8,128)(2,1)S(1)}, u32[]{:S(2)}, u32[]{:S(2)}) %collective-permute-start.53) | collective-permute-done | bytes 331808 | tf_op jit(solution)/shard_map/ppermute | solution.py:835
  440.2 5.3 %collective-permute-done.48 = bf16[112,768]{1,0:T(8,128)(2,1)S(1)} collective-permute-done((bf16[112,768]{1,0:T(8,128)(2,1)S(1)}, bf16[112,768]{1,0:T(8,128)(2,1)S(1)}, u32[]{:S(2)}, u32[]{:S(2)}) %collective-permute-start.48) | collective-permute-done | bytes 172064 | tf_op jit(solution)/shard_map/ppermute | solution.py:835
  (274 shorter events, 200.7 us)
Async XLA Ops:
  7.2 112.6 %all-gather.3.cloned.1.call-start = ((), (), s32[]{:S(2)}) async-start(), calls=%async_computation | async-start | bytes 11354112 | tf_op jit(solution)/shard_map/all_gather | solution.py:1159
  24.0 24.8 %collective-permute-start.1 = (bf16[2,112,768]{2,1,0:T(8,128)(2,1)S(1)}, bf16[2,112,768]{2,1,0:T(8,128)(2,1)S(1)}, u32[]{:S(2)}, u32[]{:S(2)}) collective-permute-start(bf16[2,112,768]{2,1,0:T(8,128)(2,1)S(1)} %maximum_bitcast_fusion), channel_id=1, source_target_pairs={{0,16},{2,18},{4,20},{6,22},{8,24},{10,26},{12,28},{14,30},{16,0},... | collective-permute-start | bytes 1032200 | tf_op jit(solution)/shard_map/ppermute | solution.py:246
  51.3 17.3 %collective-permute-start.2 = (bf16[4,56,768]{2,1,0:T(8,128)(2,1)}, bf16[4,56,768]{2,1,0:T(8,128)(2,1)}, u32[]{:S(2)}, u32[]{:S(2)}) collective-permute-start(bf16[4,56,768]{2,1,0:T(8,128)(2,1)} %get-tuple-element.261), channel_id=1, source_target_pairs={{0,2},{2,0},{4,6},{6,4},{8,10},{10,8},{12,14},{14,12},{16,18},{18,... | collective-permute-start | bytes 1032200 | tf_op jit(solution)/shard_map/ppermute | solution.py:246
  69.8 21.8 %collective-permute-start.6 = (bf16[4,2,56,768]{3,2,1,0:T(8,128)(2,1)S(1)}, bf16[4,2,56,768]{3,2,1,0:T(8,128)(2,1)S(1)}, u32[]{:S(2)}, u32[]{:S(2)}) collective-permute-start(bf16[4,2,56,768]{3,2,1,0:T(8,128)(2,1)S(1)} %pad_maximum_fusion.7), channel_id=1, source_target_pairs={{0,2},{2,0},{4,6},{6,4},{8,10},{10,8},{12,14},{14,12},{16,18},{18,... | collective-permute-start | bytes 2064392 | tf_op jit(solution)/shard_map/ppermute | solution.py:246
  70.3 22.6 %collective-permute-start.3 = (bf16[4,2,56,768]{3,2,0,1:T(8,128)(2,1)S(1)}, bf16[4,2,56,768]{3,2,0,1:T(8,128)(2,1)S(1)}, u32[]{:S(2)}, u32[]{:S(2)}) collective-permute-start(bf16[4,2,56,768]{3,2,0,1:T(8,128)(2,1)S(1)} %pad_maximum_fusion.6), channel_id=1, source_target_pairs={{0,4},{2,6},{4,0},{6,2},{8,12},{10,14},{12,8},{14,10},{16,20},{18,... | collective-permute-start | bytes 2064392 | tf_op jit(solution)/shard_map/ppermute | solution.py:246
  138.3 18.1 %collective-permute-start.10 = (bf16[128,768]{1,0:T(8,128)(2,1)}, bf16[128,768]{1,0:T(8,128)(2,1)S(1)}, u32[]{:S(2)}, u32[]{:S(2)}) collective-permute-start(bf16[128,768]{1,0:T(8,128)(2,1)} %get-tuple-element.119), channel_id=1, source_target_pairs={{0,24},{2,26},{4,28},{6,30},{8,16},{10,18},{12,20},{14,22},{16,8},... | collective-permute-start | bytes 589832 | tf_op jit(solution)/shard_map/ppermute | solution.py:835
  153.5 18.3 %collective-permute-start.18 = (bf16[2,128,384]{2,1,0:T(8,128)(2,1)S(1)}, bf16[2,128,384]{2,1,0:T(8,128)(2,1)S(1)}, u32[]{:S(2)}, u32[]{:S(2)}) collective-permute-start(bf16[2,128,384]{2,1,0:T(8,128)(2,1)S(1)} %pad_maximum_fusion.17), channel_id=1, source_target_pairs={{0,2},{2,0},{4,6},{6,4},{8,10},{10,8},{12,14},{14,12},{16,18},{18,... | collective-permute-start | bytes 589832 | tf_op jit(solution)/shard_map/ppermute | solution.py:835
  155.3 16.6 %collective-permute-start.17 = (bf16[2,128,384]{2,1,0:T(8,128)(2,1)S(1)}, bf16[2,128,384]{2,1,0:T(8,128)(2,1)S(1)}, u32[]{:S(2)}, u32[]{:S(2)}) collective-permute-start(bf16[2,128,384]{2,1,0:T(8,128)(2,1)S(1)} %pad_maximum_fusion.16), channel_id=1, source_target_pairs={{0,4},{2,6},{4,0},{6,2},{8,12},{10,14},{12,8},{14,10},{16,20},{18,... | collective-permute-start | bytes 589832 | tf_op jit(solution)/shard_map/ppermute | solution.py:835
  173.1 17.0 %collective-permute-start.15 = (bf16[6,128,384]{2,1,0:T(8,128)(2,1)S(1)}, bf16[6,128,384]{2,1,0:T(8,128)(2,1)}, u32[]{:S(2)}, u32[]{:S(2)}) collective-permute-start(bf16[6,128,384]{2,1,0:T(8,128)(2,1)S(1)} %pad_maximum_fusion.9), channel_id=1, source_target_pairs={{0,4},{2,6},{4,0},{6,2},{8,12},{10,14},{12,8},{14,10},{16,20},{18,... | collective-permute-start | bytes 1769480 | tf_op jit(solution)/shard_map/ppermute | solution.py:835
  175.8 15.6 %collective-permute-start.16 = (bf16[6,128,384]{2,1,0:T(8,128)(2,1)}, bf16[6,128,384]{2,1,0:T(8,128)(2,1)}, u32[]{:S(2)}, u32[]{:S(2)}) collective-permute-start(bf16[6,128,384]{2,1,0:T(8,128)(2,1)} %pad_maximum_fusion.10), channel_id=1, source_target_pairs={{0,2},{2,0},{4,6},{6,4},{8,10},{10,8},{12,14},{14,12},{16,18},{18,... | collective-permute-start | bytes 1769480 | tf_op jit(solution)/shard_map/ppermute | solution.py:835
  248.7 19.8 %collective-permute-start.29 = (bf16[8,128,384]{2,1,0:T(8,128)(2,1)S(1)}, bf16[8,128,384]{2,1,0:T(8,128)(2,1)}, u32[]{:S(2)}, u32[]{:S(2)}) collective-permute-start(bf16[8,128,384]{2,1,0:T(8,128)(2,1)S(1)} %add_convert_fusion.3), channel_id=1, source_target_pairs={{0,2},{2,0},{4,6},{6,4},{8,10},{10,8},{12,14},{14,12},{16,18},{18,... | collective-permute-start | bytes 2359304 | tf_op jit(solution)/shard_map/ppermute | solution.py:835
  249.9 19.5 %collective-permute-start.31 = (bf16[8,128,384]{2,1,0:T(8,128)(2,1)S(1)}, bf16[8,128,384]{2,1,0:T(8,128)(2,1)}, u32[]{:S(2)}, u32[]{:S(2)}) collective-permute-start(bf16[8,128,384]{2,1,0:T(8,128)(2,1)S(1)} %add_convert_fusion.2), channel_id=1, source_target_pairs={{0,4},{2,6},{4,0},{6,2},{8,12},{10,14},{12,8},{14,10},{16,20},{18,... | collective-permute-start | bytes 2359304 | tf_op jit(solution)/shard_map/ppermute | solution.py:835
  288.1 16.5 %collective-permute-start.35 = (bf16[128,768]{1,0:T(8,128)(2,1)S(1)}, bf16[128,768]{1,0:T(8,128)(2,1)S(1)}, u32[]{:S(2)}, u32[]{:S(2)}) collective-permute-start(bf16[128,768]{1,0:T(8,128)(2,1)S(1)} %pad_maximum_fusion.19), channel_id=1, source_target_pairs={{0,16},{2,18},{4,20},{6,22},{8,24},{10,26},{12,28},{14,30},{16,0},... | collective-permute-start | bytes 589832 | tf_op jit(solution)/shard_map/ppermute | solution.py:835
  289.3 15.3 %collective-permute-start.34 = (bf16[128,768]{1,0:T(8,128)(2,1)S(1)}, bf16[128,768]{1,0:T(8,128)(2,1)S(1)}, u32[]{:S(2)}, u32[]{:S(2)}) collective-permute-start(bf16[128,768]{1,0:T(8,128)(2,1)S(1)} %pad_maximum_fusion.18), channel_id=1, source_target_pairs={{0,8},{2,10},{4,12},{6,14},{8,0},{10,2},{12,4},{14,6},{16,24},{18,... | collective-permute-start | bytes 589832 | tf_op jit(solution)/shard_map/ppermute | solution.py:835
  341.6 31.5 %collective-permute-start.39 = (bf16[8,216,384]{2,1,0:T(8,128)(2,1)}, bf16[8,216,384]{2,1,0:T(8,128)(2,1)}, u32[]{:S(2)}, u32[]{:S(2)}) collective-permute-start(bf16[8,216,384]{2,1,0:T(8,128)(2,1)} %get-tuple-element.179), channel_id=1, source_target_pairs={{0,2},{2,0},{4,6},{6,4},{8,10},{10,8},{12,14},{14,12},{16,18},{18,... | collective-permute-start | bytes 3981320 | tf_op jit(solution)/shard_map/ppermute | solution.py:835
  343.0 31.2 %collective-permute-start.40 = (bf16[8,216,384]{2,1,0:T(8,128)(2,1)}, bf16[8,216,384]{2,1,0:T(8,128)(2,1)}, u32[]{:S(2)}, u32[]{:S(2)}) collective-permute-start(bf16[8,216,384]{2,1,0:T(8,128)(2,1)} %get-tuple-element.180), channel_id=1, source_target_pairs={{0,4},{2,6},{4,0},{6,2},{8,12},{10,14},{12,8},{14,10},{16,20},{18,... | collective-permute-start | bytes 3981320 | tf_op jit(solution)/shard_map/ppermute | solution.py:835
  378.5 18.2 %collective-permute-start.51 = (bf16[4,216,384]{2,1,0:T(8,128)(2,1)}, bf16[4,216,384]{2,1,0:T(8,128)(2,1)}, u32[]{:S(2)}, u32[]{:S(2)}) collective-permute-start(bf16[4,216,384]{2,1,0:T(8,128)(2,1)} %add_convert_fusion.6), channel_id=1, source_target_pairs={{0,2},{2,0},{4,6},{6,4},{8,10},{10,8},{12,14},{14,12},{16,18},{18,... | collective-permute-start | bytes 1990664 | tf_op jit(solution)/shard_map/ppermute | solution.py:835
  381.0 18.0 %collective-permute-start.50 = (bf16[4,216,384]{2,1,0:T(8,128)(2,1)S(1)}, bf16[4,216,384]{2,1,0:T(8,128)(2,1)}, u32[]{:S(2)}, u32[]{:S(2)}) collective-permute-start(bf16[4,216,384]{2,1,0:T(8,128)(2,1)S(1)} %add_convert_fusion.7), channel_id=1, source_target_pairs={{0,4},{2,6},{4,0},{6,2},{8,12},{10,14},{12,8},{14,10},{16,20},{18,... | collective-permute-start | bytes 1990664 | tf_op jit(solution)/shard_map/ppermute | solution.py:835
  387.2 24.2 %collective-permute-start.45 = (bf16[8,112,384]{2,1,0:T(8,128)(2,1)}, bf16[8,112,384]{2,1,0:T(8,128)(2,1)}, u32[]{:S(2)}, u32[]{:S(2)}) collective-permute-start(bf16[8,112,384]{2,1,0:T(8,128)(2,1)} %add_convert_fusion.4), channel_id=1, source_target_pairs={{0,4},{2,6},{4,0},{6,2},{8,12},{10,14},{12,8},{14,10},{16,20},{18,... | collective-permute-start | bytes 2064392 | tf_op jit(solution)/shard_map/ppermute | solution.py:835
  387.6 26.5 %collective-permute-start.43 = (bf16[8,112,384]{2,1,0:T(8,128)(2,1)}, bf16[8,112,384]{2,1,0:T(8,128)(2,1)S(1)}, u32[]{:S(2)}, u32[]{:S(2)}) collective-permute-start(bf16[8,112,384]{2,1,0:T(8,128)(2,1)} %add_convert_fusion.5), channel_id=1, source_target_pairs={{0,2},{2,0},{4,6},{6,4},{8,10},{10,8},{12,14},{14,12},{16,18},{18,... | collective-permute-start | bytes 2064392 | tf_op jit(solution)/shard_map/ppermute | solution.py:835
  402.7 24.7 %collective-permute-start.53 = (bf16[216,768]{1,0:T(8,128)(2,1)S(1)}, bf16[216,768]{1,0:T(8,128)(2,1)S(1)}, u32[]{:S(2)}, u32[]{:S(2)}) collective-permute-start(bf16[216,768]{1,0:T(8,128)(2,1)S(1)} %pad_maximum_fusion.12), channel_id=1, source_target_pairs={{0,16},{2,18},{4,20},{6,22},{8,24},{10,26},{12,28},{14,30},{16,0},... | collective-permute-start | bytes 995336 | tf_op jit(solution)/shard_map/ppermute | solution.py:835
  402.8 24.6 %collective-permute-start.52 = (bf16[216,768]{1,0:T(8,128)(2,1)S(1)}, bf16[216,768]{1,0:T(8,128)(2,1)S(1)}, u32[]{:S(2)}, u32[]{:S(2)}) collective-permute-start(bf16[216,768]{1,0:T(8,128)(2,1)S(1)} %pad_maximum_fusion.11), channel_id=1, source_target_pairs={{0,8},{2,10},{4,12},{6,14},{8,0},{10,2},{12,4},{14,6},{16,24},{18,... | collective-permute-start | bytes 995336 | tf_op jit(solution)/shard_map/ppermute | solution.py:835
  412.6 16.4 %collective-permute-start.46 = (bf16[4,112,384]{2,1,0:T(8,128)(2,1)S(1)}, bf16[4,112,384]{2,1,0:T(8,128)(2,1)S(1)}, u32[]{:S(2)}, u32[]{:S(2)}) collective-permute-start(bf16[4,112,384]{2,1,0:T(8,128)(2,1)S(1)} %add_convert_fusion.10), channel_id=1, source_target_pairs={{0,2},{2,0},{4,6},{6,4},{8,10},{10,8},{12,14},{14,12},{16,18},{18,... | collective-permute-start | bytes 1032200 | tf_op jit(solution)/shard_map/ppermute | solution.py:835
  415.2 15.2 %collective-permute-start.44 = (bf16[4,112,384]{2,1,0:T(8,128)(2,1)S(1)}, bf16[4,112,384]{2,1,0:T(8,128)(2,1)S(1)}, u32[]{:S(2)}, u32[]{:S(2)}) collective-permute-start(bf16[4,112,384]{2,1,0:T(8,128)(2,1)S(1)} %add_convert_fusion.11), channel_id=1, source_target_pairs={{0,4},{2,6},{4,0},{6,2},{8,12},{10,14},{12,8},{14,10},{16,20},{18,... | collective-permute-start | bytes 1032200 | tf_op jit(solution)/shard_map/ppermute | solution.py:835
  (52 other events, 592.5 us)
Sparse Core Ops, SparseCore 0:
  11.5 108.2 all-gather.2

commit v6 on v5

--- a/solution.py
+++ b/solution.py
@@ -1334,7 +1334,9 @@
     second.add(second.arrived)
     second.start(second.sends())
     second.add(second.arrived)
-    second.start_levels(second.level_sends())
+    sent = second.level_sends()
+    first.arrived[0] = tie(first.arrived[0], *sent)[0]
+    second.start_levels(sent)
     first, second = first.result(first.arrived), second.result(second.arrived)
     up_pieces = [first[share * k : share * (k + 1)] for k in range(steps)]
     down_piece = first[up_share * steps : up_share * steps + down_share]

time: 462 us -> 459 us (level)
  starting transfers between devices: 62.3 us -> 56.3 us
    ppermute x32, starting transfers between devices: 41.1 us -> 35 us  [along(): lax.ppermute(sent, 'dp', [(chip, chip ^ stride) for chip in range(chips)])]
  transfers between devices with their start and end apart: 56 -> 56, of which waited for: 28 -> 30; matrix products, arithmetic and copies ran while one was open for 18% -> 19% of each run, Pallas kernels for 14% -> 14%
where the time goes in v6:
time: 459 us; the launch traced here: 455 us
  waiting for transfers between devices  140 us (31%)
  Pallas kernels  123 us (27%)
  other arithmetic  73.1 us (16%)
  starting transfers between devices  56.3 us (12%)
  matrix products  30.4 us (7%)
  between operations  17.5 us (4%)
  local copies, waits for them, and re-layouts  14.5 us (3%)
    ppermute x32, waiting for transfers between devices, along(): lax.ppermute(sent, 'dp', [(chip, chip ^ stride) for chip in range(chips)])  66.3 us
    ppermute x6, waiting for transfers between devices, double(): lax.ppermute(value, 'dp', [(chip, chip ^ stride) for chip in range(chips)])  62 us
    ppermute x32, starting transfers between devices, along(): lax.ppermute(sent, 'dp', [(chip, chip ^ stride) for chip in range(chips)])  35 us
    convert_element_type x12, other arithmetic, to_low(): return values.astype(jnp.bfloat16)  22.4 us
    pallas_call x1, Pallas kernels, feed_backward(): pl.pallas_call(kernel, grid_spec=pltpu.PrefetchScalarGridSpec(num_scalar_...  21.7 us
    pallas_call x2, Pallas kernels, attention_backward(): pl.pallas_call(functools.partial(attention_back_kernel, first_head=start...  16.6 us
    pallas_call x1, Pallas kernels, ffn_forward(): pl.pallas_call(functools.partial(ffn_kernel, sizes=[len(first), len(secon...  15.4 us
    pallas_call x1, Pallas kernels, attention_forward(): pl.pallas_call(functools.partial(attention_kernel, sizes=sizes), grid_spe...  14.5 us
  transfers between devices with their start and end apart: 56, of which 30 were waited for; matrix products, arithmetic and copies ran while one was open for 19% of the time, Pallas kernels for 14%

profile of v6, /device:TPU:0, one launch (start us, length us, event | category | flops | bytes accessed | tf_op | source)
XLA Modules:
  0.0 454.8 jit_solution(17286693238768301110)
XLA Ops:
  26.9 22.0 %collective-permute-done.1 = bf16[2,112,768]{2,1,0:T(8,128)(2,1)S(1)} collective-permute-done((bf16[2,112,768]{2,1,0:T(8,128)(2,1)S(1)}, bf16[2,112,768]{2,1,0:T(8,128)(2,1)S(1)}, u32[]{:S(2)}, u32[]{:S(2)}) %collective-permute-start.1) | collective-permute-done | bytes 344096 | tf_op jit(solution)/shard_map/ppermute | solution.py:246
  52.8 10.8 %collective-permute-done.5 = bf16[4,56,768]{2,1,0:T(8,128)(2,1)S(1)} collective-permute-done((bf16[4,56,768]{2,1,0:T(8,128)(2,1)}, bf16[4,56,768]{2,1,0:T(8,128)(2,1)S(1)}, u32[]{:S(2)}, u32[]{:S(2)}) %collective-permute-start.5) | collective-permute-done | bytes 344096 | tf_op jit(solution)/shard_map/ppermute | solution.py:246
  72.0 19.6 %collective-permute-done.6 = bf16[4,2,56,768]{3,2,1,0:T(8,128)(2,1)S(1)} collective-permute-done((bf16[4,2,56,768]{3,2,1,0:T(8,128)(2,1)S(1)}, bf16[4,2,56,768]{3,2,1,0:T(8,128)(2,1)S(1)}, u32[]{:S(2)}, u32[]{:S(2)}) %collective-permute-start.6) | collective-permute-done | bytes 688160 | tf_op jit(solution)/shard_map/ppermute | solution.py:246
  102.1 14.5 %attention_forward.1 = (bf16[512,768]{1,0:T(8,128)(2,1)}, bf16[512,768]{1,0:T(8,128)(2,1)}, bf16[512,768]{1,0:T(8,128)(2,1)}, bf16[512,768]{1,0:T(8,128)(2,1)}, ...) custom-call(s32[1]{0:T(128)} %bitcast.3.core, bf16[16,56,768]{2,1,0:T(8,128)(2,1)} %bitcast.16.refs_0_.refs_2_, ...), custom_call_target="tpu_custom_call" | custom-call | tf_op jit(solution)/shard_map/attention_forward/pallas_call | solution.py:328
  119.8 15.4 %ffn_forward.1 = (bf16[512,3072]{1,0:T(8,128)(2,1)}, f32[512,3072]{1,0:T(8,128)}, f32[512,768]{1,0:T(8,128)}, bf16[512,768]{1,0:T(8,128)(2,1)}) custom-call(bf16[32,224,768]{2,1,0:T(8,128)(2,1)} %bitcast.146, bf16[32,224,768]{2,1,0:T(8,128)(2,1)} %bitcast.147, bf16[512,768]{1,0:T(8,128)(2,1)} %get-tuple-element.116.refs_2_.refs_9_, ...), custom_call_target="tpu_custom_call" | custom-call | tf_op jit(solution)/shard_map/ffn_forward/pallas_call | solution.py:400
  156.4 6.1 %collective-permute-done.9 = bf16[128,768]{1,0:T(8,128)(2,1)S(1)} collective-permute-done((bf16[128,768]{1,0:T(8,128)(2,1)}, bf16[128,768]{1,0:T(8,128)(2,1)S(1)}, u32[]{:S(2)}, u32[]{:S(2)}) %collective-permute-start.9) | collective-permute-done | bytes 196640 | tf_op jit(solution)/shard_map/ppermute | solution.py:835
  176.2 7.8 %fusion.6 = bf16[2048,768]{1,0:T(8,128)(2,1)} fusion(bf16[1568,768]{1,0:T(8,128)(2,1)S(1)} %copy-done, s32[2048]{0:T(1024)S(1)} %bitcast.165), kind=kOutput, calls=%fused_computation.15 | convolution fusion | flops 4937285632 | bytes 5562368 | tf_op jit(solution)/shard_map/dot_general | solution.py:43
  184.0 6.1 %compact_rows.2.refs_0_ = bf16[2048,768]{1,0:T(8,128)(2,1)} custom-call(s32[4]{0:T(128)} %pad_add_fusion.place, s32[32]{0:T(128)} %add.621.places, s32[32]{0:T(128)} %copy-done.18, s32[10]{0:T(128)} %constant.197.clone.indices, bf16[2,10,128,384]{3,2,1,0:T(8,128)(2,1)} %copy-done.3, bf16[2,10,128,384]{3,2,1,0:T(8,128)(2,1)} %collective-permute-done.19.other_ref), custom_call_target="tpu_custom_call" | custom-call | tf_op jit(solution)/shard_map/compact_rows/pallas_call | solution.py:978
  196.8 6.1 %compact_rows.3 = bf16[2048,768]{1,0:T(8,128)(2,1)} custom-call(s32[4]{0:T(128)} %pad_add_fusion.place, s32[32]{0:T(128)} %add.621.places, s32[32]{0:T(128)} %copy-done.18, s32[6]{0:T(128)} %constant.198.clone.indices, bf16[2,6,128,384]{3,2,1,0:T(8,128)(2,1)} %copy-done.4, bf16[2,6,128,384]{3,2,1,0:T(8,128)(2,1)} %collective-permute-done.20.other_ref, ...), custom_call_target="tpu_custom_call" | custom-call | tf_op jit(solution)/shard_map/compact_rows/pallas_call | solution.py:978
  202.9 7.3 %fusion.58 = (f32[2048]{0:T(1024)S(1)}, f32[2048,1568]{0,1:T(8,128)S(1)}) fusion(f32[1568]{0:T(1024)S(1)} %convert_element_type.659, bf16[2048,768]{1,0:T(8,128)(2,1)} %compact_rows.3, bf16[1568,768]{1,0:T(8,128)(2,1)S(1)} %copy-done), kind=kOutput, calls=%fused_computation.203 | convolution fusion | flops 4938921984 | bytes 18413696 | tf_op jit(solution)/shard_map/dot_general | solution.py:53
  236.1 7.1 %spread_rows.1 = (bf16[16,128,384]{2,1,0:T(8,128)(2,1)}, bf16[16,128,384]{2,1,0:T(8,128)(2,1)}, bf16[16,128,384]{2,1,0:T(8,128)(2,1)}, bf16[16,128,384]{2,1,0:T(8,128)(2,1)}) custom-call(s32[4]{0:T(128)} %pad_add_fusion.place, s32[32]{0:T(128)} %add.621.places, s32[32]{0:T(128)} %copy-done.18, bf16[2048,768]{1,0:T(8,128)(2,1)} %pad_maximum_fusion.rows_ref), custom_call_target="tpu_custom_call" | custom-call | tf_op jit(solution)/shard_map/spread_rows/pallas_call | solution.py:1099
  250.9 12.3 %convert_reduce_fusion = (f32[1568]{0:T(1024)}, bf16[2048,1568]{0,1:T(8,128)(2,1)}) fusion(s32[2048]{0:T(1024)S(1)} %bitcast.167, f32[2048,1568]{0,1:T(8,128)} %copy-done.2, f32[2048]{0:T(1024)S(1)} %get-tuple-element.289), kind=kLoop, calls=%fused_computation.2 | loop fusion | flops 22477280 | bytes 19290240 | tf_op jit(solution)/shard_map/reduce_sum | solution.py:1274
  263.2 5.3 %collective-permute-done.29 = bf16[8,128,384]{2,1,0:T(8,128)(2,1)} collective-permute-done((bf16[8,128,384]{2,1,0:T(8,128)(2,1)S(1)}, bf16[8,128,384]{2,1,0:T(8,128)(2,1)}, u32[]{:S(2)}, u32[]{:S(2)}) %collective-permute-start.29) | collective-permute-done | bytes 786464 | tf_op jit(solution)/shard_map/ppermute | solution.py:835
  274.2 8.6 %fusion.59 = f32[1568,768]{1,0:T(8,128)} fusion(bf16[2048,1568]{0,1:T(8,128)(2,1)} %get-tuple-element.143, bf16[2048,768]{1,0:T(8,128)(2,1)S(1)} %copy-done.5), kind=kOutput, calls=%fused_computation.204 | convolution fusion | flops 4932501504 | bytes 14385152 | tf_op jit(solution)/shard_map/dot_general | solution.py:47
  290.5 5.1 %collective-permute-done.36 = bf16[128,768]{1,0:T(8,128)(2,1)S(1)} collective-permute-done((bf16[128,768]{1,0:T(8,128)(2,1)S(1)}, bf16[128,768]{1,0:T(8,128)(2,1)S(1)}, u32[]{:S(2)}, u32[]{:S(2)}) %collective-permute-start.36) | collective-permute-done | bytes 196640 | tf_op jit(solution)/shard_map/ppermute | solution.py:835
  295.5 9.1 %collective-permute-done.35 = bf16[128,768]{1,0:T(8,128)(2,1)S(1)} collective-permute-done((bf16[128,768]{1,0:T(8,128)(2,1)S(1)}, bf16[128,768]{1,0:T(8,128)(2,1)S(1)}, u32[]{:S(2)}, u32[]{:S(2)}) %collective-permute-start.35) | collective-permute-done | bytes 196640 | tf_op jit(solution)/shard_map/ppermute | solution.py:835
  306.2 21.7 %feed_backward.1 = (f32[512,768]{1,0:T(8,128)}, f32[8,768]{1,0:T(8,128)}, bf16[16,216,384]{2,1,0:T(8,128)(2,1)}, bf16[16,216,384]{2,1,0:T(8,128)(2,1)}, bf16[16,...) custom-call(s32[4]{0:T(128)} %pad_add_fusion.place, bf16[32,224,768]{2,1,0:T(8,128)(2,1)} %bitcast.150, ...), custom_call_target="tpu_custom_call" | custom-call | tf_op jit(solution)/shard_map/feed_backward/pallas_call | solution.py:543
  328.4 5.3 %out_backward.1 = (f32[512,768]{1,0:T(8,128)}, bf16[512,768]{1,0:T(8,128)(2,1)}, bf16[512,768]{1,0:T(8,128)(2,1)}, f32[8,768]{1,0:T(8,128)}) custom-call(s32[1]{0:T(128)} %bitcast.3.core, bf16[16,56,768]{2,1,0:T(8,128)(2,1)} %bitcast.23.refs_4_.refs_6_.refs_0_, bf16[16,56,768]{2,1,0:T(8,128)(2,1)} %collective-permute-done.7.refs_5_.refs_7_.refs_1_, ...), custom_call_target="tpu_custom_call" | custom-call | tf_op jit(solution)/shard_map/out_backward/pallas_call | solution.py:596
  344.8 8.2 %attention_backward.2 = (bf16[512,384]{1,0:T(8,128)(2,1)}, bf16[512,384]{1,0:T(8,128)(2,1)}, bf16[512,384]{1,0:T(8,128)(2,1)}, f32[8,384]{1,0:T(8,128)}) custom-call(bf16[512,768]{1,0:T(8,128)(2,1)} %get-tuple-element.173.refs_0_, bf16[512,768]{1,0:T(8,128)(2,1)} %get-tuple-element.161.refs_1_, bf16[512,768]{1,0:T(8,128)(2,1)} %get-tuple-element.162.refs_2_, ...), custom_call_target="tpu_custom_call" | custom-call | tf_op jit(solution)/shard_map/attention_backward/pallas_call | solution.py:656
  353.0 8.5 %attention_backward.3 = (bf16[512,384]{1,0:T(8,128)(2,1)}, bf16[512,384]{1,0:T(8,128)(2,1)}, bf16[512,384]{1,0:T(8,128)(2,1)}, f32[8,384]{1,0:T(8,128)}) custom-call(bf16[512,768]{1,0:T(8,128)(2,1)} %get-tuple-element.173.refs_0_, bf16[512,768]{1,0:T(8,128)(2,1)} %get-tuple-element.161.refs_1_, bf16[512,768]{1,0:T(8,128)(2,1)} %get-tuple-element.162.refs_2_, ...), custom_call_target="tpu_custom_call" | custom-call | tf_op jit(solution)/shard_map/attention_backward/pallas_call | solution.py:656
  361.4 8.8 %last_grads.1 = (bf16[16,112,384]{2,1,0:T(8,128)(2,1)}, bf16[16,112,384]{2,1,0:T(8,128)(2,1)}, bf16[16,112,384]{2,1,0:T(8,128)(2,1)}, bf16[16,112,384]{2,1,0:T(8,128)(2,1)}) custom-call(s32[4]{0:T(128)} %pad_add_fusion.place, bf16[512,768]{1,0:T(8,128)(2,1)} %refs_0_.5, bf16[512,768]{1,0:T(8,128)(2,1)} %get-tuple-element.167.refs_1_, ...), custom_call_target="tpu_custom_call" | custom-call | tf_op jit(solution)/shard_map/last_grads/pallas_call | solution.py:734
  389.9 6.9 %tokens_backward.1 = f32[512,768]{1,0:T(8,128)} custom-call(s32[1]{0:T(128)} %bitcast.3.core, bf16[16,56,768]{2,1,0:T(8,128)(2,1)} %bitcast.16.refs_0_.refs_2_, bf16[16,56,768]{2,1,0:T(8,128)(2,1)} %collective-permute-done.4.refs_1_.refs_3_, bf16[16,56,768]{2,1,0:T(8,128)(2,1)} %bitcast.16.refs_0_.refs_2_, ...), custom_call_target="tpu_custom_call" | custom-call | tf_op jit(solution)/shard_map/tokens_backward/pallas_call | solution.py:774
  403.8 8.6 %collective-permute-done.45 = bf16[8,112,384]{2,1,0:T(8,128)(2,1)S(1)} collective-permute-done((bf16[8,112,384]{2,1,0:T(8,128)(2,1)}, bf16[8,112,384]{2,1,0:T(8,128)(2,1)S(1)}, u32[]{:S(2)}, u32[]{:S(2)}) %collective-permute-start.45) | collective-permute-done | bytes 688160 | tf_op jit(solution)/shard_map/ppermute | solution.py:835
  426.4 7.9 %collective-permute-done.52 = bf16[216,768]{1,0:T(8,128)(2,1)S(1)} collective-permute-done((bf16[216,768]{1,0:T(8,128)(2,1)S(1)}, bf16[216,768]{1,0:T(8,128)(2,1)S(1)}, u32[]{:S(2)}, u32[]{:S(2)}) %collective-permute-start.52) | collective-permute-done | bytes 331808 | tf_op jit(solution)/shard_map/ppermute | solution.py:835
  (274 shorter events, 198.5 us)
Async XLA Ops:
  7.2 112.6 %all-gather.3.cloned.1.call-start = ((), (), s32[]{:S(2)}) async-start(), calls=%async_computation | async-start | bytes 11354112 | tf_op jit(solution)/shard_map/all_gather | solution.py:1159
  24.0 24.8 %collective-permute-start.1 = (bf16[2,112,768]{2,1,0:T(8,128)(2,1)S(1)}, bf16[2,112,768]{2,1,0:T(8,128)(2,1)S(1)}, u32[]{:S(2)}, u32[]{:S(2)}) collective-permute-start(bf16[2,112,768]{2,1,0:T(8,128)(2,1)S(1)} %maximum_bitcast_fusion), channel_id=1, source_target_pairs={{0,16},{2,18},{4,20},{6,22},{8,24},{10,26},{12,28},{14,30},{16,0},... | collective-permute-start | bytes 1032200 | tf_op jit(solution)/shard_map/ppermute | solution.py:246
  51.3 17.3 %collective-permute-start.2 = (bf16[4,56,768]{2,1,0:T(8,128)(2,1)}, bf16[4,56,768]{2,1,0:T(8,128)(2,1)}, u32[]{:S(2)}, u32[]{:S(2)}) collective-permute-start(bf16[4,56,768]{2,1,0:T(8,128)(2,1)} %get-tuple-element.263), channel_id=1, source_target_pairs={{0,2},{2,0},{4,6},{6,4},{8,10},{10,8},{12,14},{14,12},{16,18},{18,... | collective-permute-start | bytes 1032200 | tf_op jit(solution)/shard_map/ppermute | solution.py:246
  69.8 21.8 %collective-permute-start.6 = (bf16[4,2,56,768]{3,2,1,0:T(8,128)(2,1)S(1)}, bf16[4,2,56,768]{3,2,1,0:T(8,128)(2,1)S(1)}, u32[]{:S(2)}, u32[]{:S(2)}) collective-permute-start(bf16[4,2,56,768]{3,2,1,0:T(8,128)(2,1)S(1)} %pad_maximum_fusion.7), channel_id=1, source_target_pairs={{0,2},{2,0},{4,6},{6,4},{8,10},{10,8},{12,14},{14,12},{16,18},{18,... | collective-permute-start | bytes 2064392 | tf_op jit(solution)/shard_map/ppermute | solution.py:246
  70.3 22.6 %collective-permute-start.3 = (bf16[4,2,56,768]{3,2,0,1:T(8,128)(2,1)S(1)}, bf16[4,2,56,768]{3,2,0,1:T(8,128)(2,1)S(1)}, u32[]{:S(2)}, u32[]{:S(2)}) collective-permute-start(bf16[4,2,56,768]{3,2,0,1:T(8,128)(2,1)S(1)} %pad_maximum_fusion.6), channel_id=1, source_target_pairs={{0,4},{2,6},{4,0},{6,2},{8,12},{10,14},{12,8},{14,10},{16,20},{18,... | collective-permute-start | bytes 2064392 | tf_op jit(solution)/shard_map/ppermute | solution.py:246
  138.3 18.1 %collective-permute-start.10 = (bf16[128,768]{1,0:T(8,128)(2,1)}, bf16[128,768]{1,0:T(8,128)(2,1)S(1)}, u32[]{:S(2)}, u32[]{:S(2)}) collective-permute-start(bf16[128,768]{1,0:T(8,128)(2,1)} %get-tuple-element.120), channel_id=1, source_target_pairs={{0,24},{2,26},{4,28},{6,30},{8,16},{10,18},{12,20},{14,22},{16,8},... | collective-permute-start | bytes 589832 | tf_op jit(solution)/shard_map/ppermute | solution.py:835
  153.5 18.3 %collective-permute-start.18 = (bf16[2,128,384]{2,1,0:T(8,128)(2,1)S(1)}, bf16[2,128,384]{2,1,0:T(8,128)(2,1)S(1)}, u32[]{:S(2)}, u32[]{:S(2)}) collective-permute-start(bf16[2,128,384]{2,1,0:T(8,128)(2,1)S(1)} %pad_maximum_fusion.17), channel_id=1, source_target_pairs={{0,2},{2,0},{4,6},{6,4},{8,10},{10,8},{12,14},{14,12},{16,18},{18,... | collective-permute-start | bytes 589832 | tf_op jit(solution)/shard_map/ppermute | solution.py:835
  155.3 16.6 %collective-permute-start.17 = (bf16[2,128,384]{2,1,0:T(8,128)(2,1)S(1)}, bf16[2,128,384]{2,1,0:T(8,128)(2,1)S(1)}, u32[]{:S(2)}, u32[]{:S(2)}) collective-permute-start(bf16[2,128,384]{2,1,0:T(8,128)(2,1)S(1)} %pad_maximum_fusion.16), channel_id=1, source_target_pairs={{0,4},{2,6},{4,0},{6,2},{8,12},{10,14},{12,8},{14,10},{16,20},{18,... | collective-permute-start | bytes 589832 | tf_op jit(solution)/shard_map/ppermute | solution.py:835
  173.1 17.0 %collective-permute-start.15 = (bf16[6,128,384]{2,1,0:T(8,128)(2,1)S(1)}, bf16[6,128,384]{2,1,0:T(8,128)(2,1)}, u32[]{:S(2)}, u32[]{:S(2)}) collective-permute-start(bf16[6,128,384]{2,1,0:T(8,128)(2,1)S(1)} %pad_maximum_fusion.9), channel_id=1, source_target_pairs={{0,4},{2,6},{4,0},{6,2},{8,12},{10,14},{12,8},{14,10},{16,20},{18,... | collective-permute-start | bytes 1769480 | tf_op jit(solution)/shard_map/ppermute | solution.py:835
  175.8 15.6 %collective-permute-start.16 = (bf16[6,128,384]{2,1,0:T(8,128)(2,1)}, bf16[6,128,384]{2,1,0:T(8,128)(2,1)}, u32[]{:S(2)}, u32[]{:S(2)}) collective-permute-start(bf16[6,128,384]{2,1,0:T(8,128)(2,1)} %pad_maximum_fusion.10), channel_id=1, source_target_pairs={{0,2},{2,0},{4,6},{6,4},{8,10},{10,8},{12,14},{14,12},{16,18},{18,... | collective-permute-start | bytes 1769480 | tf_op jit(solution)/shard_map/ppermute | solution.py:835
  248.8 19.8 %collective-permute-start.29 = (bf16[8,128,384]{2,1,0:T(8,128)(2,1)S(1)}, bf16[8,128,384]{2,1,0:T(8,128)(2,1)}, u32[]{:S(2)}, u32[]{:S(2)}) collective-permute-start(bf16[8,128,384]{2,1,0:T(8,128)(2,1)S(1)} %add_convert_fusion.3), channel_id=1, source_target_pairs={{0,2},{2,0},{4,6},{6,4},{8,10},{10,8},{12,14},{14,12},{16,18},{18,... | collective-permute-start | bytes 2359304 | tf_op jit(solution)/shard_map/ppermute | solution.py:835
  249.9 19.5 %collective-permute-start.31 = (bf16[8,128,384]{2,1,0:T(8,128)(2,1)S(1)}, bf16[8,128,384]{2,1,0:T(8,128)(2,1)}, u32[]{:S(2)}, u32[]{:S(2)}) collective-permute-start(bf16[8,128,384]{2,1,0:T(8,128)(2,1)S(1)} %add_convert_fusion.2), channel_id=1, source_target_pairs={{0,4},{2,6},{4,0},{6,2},{8,12},{10,14},{12,8},{14,10},{16,20},{18,... | collective-permute-start | bytes 2359304 | tf_op jit(solution)/shard_map/ppermute | solution.py:835
  288.1 16.5 %collective-permute-start.35 = (bf16[128,768]{1,0:T(8,128)(2,1)S(1)}, bf16[128,768]{1,0:T(8,128)(2,1)S(1)}, u32[]{:S(2)}, u32[]{:S(2)}) collective-permute-start(bf16[128,768]{1,0:T(8,128)(2,1)S(1)} %pad_maximum_fusion.19), channel_id=1, source_target_pairs={{0,16},{2,18},{4,20},{6,22},{8,24},{10,26},{12,28},{14,30},{16,0},... | collective-permute-start | bytes 589832 | tf_op jit(solution)/shard_map/ppermute | solution.py:835
  341.6 31.5 %collective-permute-start.39 = (bf16[8,216,384]{2,1,0:T(8,128)(2,1)}, bf16[8,216,384]{2,1,0:T(8,128)(2,1)}, u32[]{:S(2)}, u32[]{:S(2)}) collective-permute-start(bf16[8,216,384]{2,1,0:T(8,128)(2,1)} %get-tuple-element.180), channel_id=1, source_target_pairs={{0,2},{2,0},{4,6},{6,4},{8,10},{10,8},{12,14},{14,12},{16,18},{18,... | collective-permute-start | bytes 3981320 | tf_op jit(solution)/shard_map/ppermute | solution.py:835
  343.0 31.2 %collective-permute-start.40 = (bf16[8,216,384]{2,1,0:T(8,128)(2,1)}, bf16[8,216,384]{2,1,0:T(8,128)(2,1)}, u32[]{:S(2)}, u32[]{:S(2)}) collective-permute-start(bf16[8,216,384]{2,1,0:T(8,128)(2,1)} %get-tuple-element.181), channel_id=1, source_target_pairs={{0,4},{2,6},{4,0},{6,2},{8,12},{10,14},{12,8},{14,10},{16,20},{18,... | collective-permute-start | bytes 3981320 | tf_op jit(solution)/shard_map/ppermute | solution.py:835
  379.4 18.2 %collective-permute-start.51 = (bf16[4,216,384]{2,1,0:T(8,128)(2,1)}, bf16[4,216,384]{2,1,0:T(8,128)(2,1)}, u32[]{:S(2)}, u32[]{:S(2)}) collective-permute-start(bf16[4,216,384]{2,1,0:T(8,128)(2,1)} %add_convert_fusion.6), channel_id=1, source_target_pairs={{0,2},{2,0},{4,6},{6,4},{8,10},{10,8},{12,14},{14,12},{16,18},{18,... | collective-permute-start | bytes 1990664 | tf_op jit(solution)/shard_map/ppermute | solution.py:835
  381.8 18.2 %collective-permute-start.50 = (bf16[4,216,384]{2,1,0:T(8,128)(2,1)}, bf16[4,216,384]{2,1,0:T(8,128)(2,1)}, u32[]{:S(2)}, u32[]{:S(2)}) collective-permute-start(bf16[4,216,384]{2,1,0:T(8,128)(2,1)} %add_convert_fusion.7), channel_id=1, source_target_pairs={{0,4},{2,6},{4,0},{6,2},{8,12},{10,14},{12,8},{14,10},{16,20},{18,... | collective-permute-start | bytes 1990664 | tf_op jit(solution)/shard_map/ppermute | solution.py:835
  388.1 24.3 %collective-permute-start.45 = (bf16[8,112,384]{2,1,0:T(8,128)(2,1)}, bf16[8,112,384]{2,1,0:T(8,128)(2,1)S(1)}, u32[]{:S(2)}, u32[]{:S(2)}) collective-permute-start(bf16[8,112,384]{2,1,0:T(8,128)(2,1)} %add_convert_fusion.4), channel_id=1, source_target_pairs={{0,4},{2,6},{4,0},{6,2},{8,12},{10,14},{12,8},{14,10},{16,20},{18,... | collective-permute-start | bytes 2064392 | tf_op jit(solution)/shard_map/ppermute | solution.py:835
  388.5 26.5 %collective-permute-start.43 = (bf16[8,112,384]{2,1,0:T(8,128)(2,1)}, bf16[8,112,384]{2,1,0:T(8,128)(2,1)S(1)}, u32[]{:S(2)}, u32[]{:S(2)}) collective-permute-start(bf16[8,112,384]{2,1,0:T(8,128)(2,1)} %add_convert_fusion.5), channel_id=1, source_target_pairs={{0,2},{2,0},{4,6},{6,4},{8,10},{10,8},{12,14},{14,12},{16,18},{18,... | collective-permute-start | bytes 2064392 | tf_op jit(solution)/shard_map/ppermute | solution.py:835
  402.2 32.1 %collective-permute-start.54 = (bf16[216,768]{1,0:T(8,128)(2,1)S(1)}, bf16[216,768]{1,0:T(8,128)(2,1)S(1)}, u32[]{:S(2)}, u32[]{:S(2)}) collective-permute-start(bf16[216,768]{1,0:T(8,128)(2,1)S(1)} %pad_maximum_fusion.13), channel_id=1, source_target_pairs={{0,24},{2,26},{4,28},{6,30},{8,16},{10,18},{12,20},{14,22},{16,8},... | collective-permute-start | bytes 995336 | tf_op jit(solution)/shard_map/ppermute | solution.py:835
  403.7 35.6 %collective-permute-start.53 = (bf16[216,768]{1,0:T(8,128)(2,1)S(1)}, bf16[216,768]{1,0:T(8,128)(2,1)S(1)}, u32[]{:S(2)}, u32[]{:S(2)}) collective-permute-start(bf16[216,768]{1,0:T(8,128)(2,1)S(1)} %pad_maximum_fusion.12), channel_id=1, source_target_pairs={{0,16},{2,18},{4,20},{6,22},{8,24},{10,26},{12,28},{14,30},{16,0},... | collective-permute-start | bytes 995336 | tf_op jit(solution)/shard_map/ppermute | solution.py:835
  417.2 17.1 %collective-permute-start.52 = (bf16[216,768]{1,0:T(8,128)(2,1)S(1)}, bf16[216,768]{1,0:T(8,128)(2,1)S(1)}, u32[]{:S(2)}, u32[]{:S(2)}) collective-permute-start(bf16[216,768]{1,0:T(8,128)(2,1)S(1)} %pad_maximum_fusion.11), channel_id=1, source_target_pairs={{0,8},{2,10},{4,12},{6,14},{8,0},{10,2},{12,4},{14,6},{16,24},{18,... | collective-permute-start | bytes 995336 | tf_op jit(solution)/shard_map/ppermute | solution.py:835
  424.8 16.9 %collective-permute-start.49 = (bf16[112,768]{1,0:T(8,128)(2,1)S(1)}, bf16[112,768]{1,0:T(8,128)(2,1)S(1)}, u32[]{:S(2)}, u32[]{:S(2)}) collective-permute-start(bf16[112,768]{1,0:T(8,128)(2,1)S(1)} %pad_maximum_fusion.23), channel_id=1, source_target_pairs={{0,24},{2,26},{4,28},{6,30},{8,16},{10,18},{12,20},{14,22},{16,8},... | collective-permute-start | bytes 516104 | tf_op jit(solution)/shard_map/ppermute | solution.py:835
  426.2 16.8 %collective-permute-start.48 = (bf16[112,768]{1,0:T(8,128)(2,1)S(1)}, bf16[112,768]{1,0:T(8,128)(2,1)S(1)}, u32[]{:S(2)}, u32[]{:S(2)}) collective-permute-start(bf16[112,768]{1,0:T(8,128)(2,1)S(1)} %pad_maximum_fusion.22), channel_id=1, source_target_pairs={{0,16},{2,18},{4,20},{6,22},{8,24},{10,26},{12,28},{14,30},{16,0},... | collective-permute-start | bytes 516104 | tf_op jit(solution)/shard_map/ppermute | solution.py:835
  (52 other events, 577.3 us)
Sparse Core Ops, SparseCore 0:
  11.5 108.2 all-gather.2

commit v7 on v6

--- a/solution.py
+++ b/solution.py
@@ -1093,7 +1093,7 @@
 def spread(place, places, counts, rows, slots):
     chips = places.shape[0] // 2
     total, width = rows.shape
-    batch = 4
+    batch = 8
     block = pl.BlockSpec((batch, slots, width // 2), lambda i, *_: (i, 0, 0))
     shape = jax.ShapeDtypeStruct((chips, slots, width // 2), jnp.bfloat16)
     outs = pl.pallas_call(

time: 459 us -> 459 us (level)
  no operation moved by 1% of the time
where the time goes in v7:
time: 459 us; the launch traced here: 455 us
  waiting for transfers between devices  140 us (31%)
  Pallas kernels  123 us (27%)
  other arithmetic  73.1 us (16%)
  starting transfers between devices  56.3 us (12%)
  matrix products  30.4 us (7%)
  between operations  17.5 us (4%)
  local copies, waits for them, and re-layouts  14.5 us (3%)
    ppermute x32, waiting for transfers between devices, along(): lax.ppermute(sent, 'dp', [(chip, chip ^ stride) for chip in range(chips)])  66.3 us
    ppermute x6, waiting for transfers between devices, double(): lax.ppermute(value, 'dp', [(chip, chip ^ stride) for chip in range(chips)])  62 us
    ppermute x32, starting transfers between devices, along(): lax.ppermute(sent, 'dp', [(chip, chip ^ stride) for chip in range(chips)])  35 us
    convert_element_type x12, other arithmetic, to_low(): return values.astype(jnp.bfloat16)  22.4 us
    pallas_call x1, Pallas kernels, feed_backward(): pl.pallas_call(kernel, grid_spec=pltpu.PrefetchScalarGridSpec(num_scalar_...  21.7 us
    pallas_call x2, Pallas kernels, attention_backward(): pl.pallas_call(functools.partial(attention_back_kernel, first_head=start...  16.6 us
    pallas_call x1, Pallas kernels, ffn_forward(): pl.pallas_call(functools.partial(ffn_kernel, sizes=[len(first), len(secon...  15.4 us
    pallas_call x1, Pallas kernels, attention_forward(): pl.pallas_call(functools.partial(attention_kernel, sizes=sizes), grid_spe...  14.5 us
  transfers between devices with their start and end apart: 56, of which 30 were waited for; matrix products, arithmetic and copies ran while one was open for 19% of the time, Pallas kernels for 14%

profile of v7, /device:TPU:0, one launch (start us, length us, event | category | flops | bytes accessed | tf_op | source)
XLA Modules:
  0.0 454.7 jit_solution(15092985190036537571)
XLA Ops:
  26.9 22.0 %collective-permute-done.1 = bf16[2,112,768]{2,1,0:T(8,128)(2,1)S(1)} collective-permute-done((bf16[2,112,768]{2,1,0:T(8,128)(2,1)S(1)}, bf16[2,112,768]{2,1,0:T(8,128)(2,1)S(1)}, u32[]{:S(2)}, u32[]{:S(2)}) %collective-permute-start.1) | collective-permute-done | bytes 344096 | tf_op jit(solution)/shard_map/ppermute | solution.py:246
  52.8 10.8 %collective-permute-done.5 = bf16[4,56,768]{2,1,0:T(8,128)(2,1)S(1)} collective-permute-done((bf16[4,56,768]{2,1,0:T(8,128)(2,1)}, bf16[4,56,768]{2,1,0:T(8,128)(2,1)S(1)}, u32[]{:S(2)}, u32[]{:S(2)}) %collective-permute-start.5) | collective-permute-done | bytes 344096 | tf_op jit(solution)/shard_map/ppermute | solution.py:246
  72.0 19.6 %collective-permute-done.6 = bf16[4,2,56,768]{3,2,1,0:T(8,128)(2,1)S(1)} collective-permute-done((bf16[4,2,56,768]{3,2,1,0:T(8,128)(2,1)S(1)}, bf16[4,2,56,768]{3,2,1,0:T(8,128)(2,1)S(1)}, u32[]{:S(2)}, u32[]{:S(2)}) %collective-permute-start.6) | collective-permute-done | bytes 688160 | tf_op jit(solution)/shard_map/ppermute | solution.py:246
  102.1 14.5 %attention_forward.1 = (bf16[512,768]{1,0:T(8,128)(2,1)}, bf16[512,768]{1,0:T(8,128)(2,1)}, bf16[512,768]{1,0:T(8,128)(2,1)}, bf16[512,768]{1,0:T(8,128)(2,1)}, ...) custom-call(s32[1]{0:T(128)} %bitcast.3.core, bf16[16,56,768]{2,1,0:T(8,128)(2,1)} %bitcast.16.refs_0_.refs_2_, ...), custom_call_target="tpu_custom_call" | custom-call | tf_op jit(solution)/shard_map/attention_forward/pallas_call | solution.py:328
  119.8 15.4 %ffn_forward.1 = (bf16[512,3072]{1,0:T(8,128)(2,1)}, f32[512,3072]{1,0:T(8,128)}, f32[512,768]{1,0:T(8,128)}, bf16[512,768]{1,0:T(8,128)(2,1)}) custom-call(bf16[32,224,768]{2,1,0:T(8,128)(2,1)} %bitcast.146, bf16[32,224,768]{2,1,0:T(8,128)(2,1)} %bitcast.147, bf16[512,768]{1,0:T(8,128)(2,1)} %get-tuple-element.116.refs_2_.refs_9_, ...), custom_call_target="tpu_custom_call" | custom-call | tf_op jit(solution)/shard_map/ffn_forward/pallas_call | solution.py:400
  156.4 6.1 %collective-permute-done.9 = bf16[128,768]{1,0:T(8,128)(2,1)S(1)} collective-permute-done((bf16[128,768]{1,0:T(8,128)(2,1)}, bf16[128,768]{1,0:T(8,128)(2,1)S(1)}, u32[]{:S(2)}, u32[]{:S(2)}) %collective-permute-start.9) | collective-permute-done | bytes 196640 | tf_op jit(solution)/shard_map/ppermute | solution.py:835
  176.2 7.8 %fusion.6 = bf16[2048,768]{1,0:T(8,128)(2,1)} fusion(bf16[1568,768]{1,0:T(8,128)(2,1)S(1)} %copy-done, s32[2048]{0:T(1024)S(1)} %bitcast.165), kind=kOutput, calls=%fused_computation.15 | convolution fusion | flops 4937285632 | bytes 5562368 | tf_op jit(solution)/shard_map/dot_general | solution.py:43
  184.0 6.1 %compact_rows.2.refs_0_ = bf16[2048,768]{1,0:T(8,128)(2,1)} custom-call(s32[4]{0:T(128)} %pad_add_fusion.place, s32[32]{0:T(128)} %add.621.places, s32[32]{0:T(128)} %copy-done.18, s32[10]{0:T(128)} %constant.197.clone.indices, bf16[2,10,128,384]{3,2,1,0:T(8,128)(2,1)} %copy-done.3, bf16[2,10,128,384]{3,2,1,0:T(8,128)(2,1)} %collective-permute-done.19.other_ref), custom_call_target="tpu_custom_call" | custom-call | tf_op jit(solution)/shard_map/compact_rows/pallas_call | solution.py:978
  196.8 6.1 %compact_rows.3 = bf16[2048,768]{1,0:T(8,128)(2,1)} custom-call(s32[4]{0:T(128)} %pad_add_fusion.place, s32[32]{0:T(128)} %add.621.places, s32[32]{0:T(128)} %copy-done.18, s32[6]{0:T(128)} %constant.198.clone.indices, bf16[2,6,128,384]{3,2,1,0:T(8,128)(2,1)} %copy-done.4, bf16[2,6,128,384]{3,2,1,0:T(8,128)(2,1)} %collective-permute-done.20.other_ref, ...), custom_call_target="tpu_custom_call" | custom-call | tf_op jit(solution)/shard_map/compact_rows/pallas_call | solution.py:978
  202.9 7.3 %fusion.58 = (f32[2048]{0:T(1024)S(1)}, f32[2048,1568]{0,1:T(8,128)S(1)}) fusion(f32[1568]{0:T(1024)S(1)} %convert_element_type.659, bf16[2048,768]{1,0:T(8,128)(2,1)} %compact_rows.3, bf16[1568,768]{1,0:T(8,128)(2,1)S(1)} %copy-done), kind=kOutput, calls=%fused_computation.203 | convolution fusion | flops 4938921984 | bytes 18413696 | tf_op jit(solution)/shard_map/dot_general | solution.py:53
  236.1 6.9 %spread_rows.1 = (bf16[16,128,384]{2,1,0:T(8,128)(2,1)}, bf16[16,128,384]{2,1,0:T(8,128)(2,1)}, bf16[16,128,384]{2,1,0:T(8,128)(2,1)}, bf16[16,128,384]{2,1,0:T(8,128)(2,1)}) custom-call(s32[4]{0:T(128)} %pad_add_fusion.place, s32[32]{0:T(128)} %add.621.places, s32[32]{0:T(128)} %copy-done.18, bf16[2048,768]{1,0:T(8,128)(2,1)} %pad_maximum_fusion.rows_ref), custom_call_target="tpu_custom_call" | custom-call | tf_op jit(solution)/shard_map/spread_rows/pallas_call | solution.py:1099
  250.8 12.3 %convert_reduce_fusion = (f32[1568]{0:T(1024)}, bf16[2048,1568]{0,1:T(8,128)(2,1)}) fusion(s32[2048]{0:T(1024)S(1)} %bitcast.167, f32[2048,1568]{0,1:T(8,128)} %copy-done.2, f32[2048]{0:T(1024)S(1)} %get-tuple-element.289), kind=kLoop, calls=%fused_computation.2 | loop fusion | flops 22477280 | bytes 19290240 | tf_op jit(solution)/shard_map/reduce_sum | solution.py:1274
  263.1 5.3 %collective-permute-done.29 = bf16[8,128,384]{2,1,0:T(8,128)(2,1)} collective-permute-done((bf16[8,128,384]{2,1,0:T(8,128)(2,1)S(1)}, bf16[8,128,384]{2,1,0:T(8,128)(2,1)}, u32[]{:S(2)}, u32[]{:S(2)}) %collective-permute-start.29) | collective-permute-done | bytes 786464 | tf_op jit(solution)/shard_map/ppermute | solution.py:835
  274.1 8.6 %fusion.59 = f32[1568,768]{1,0:T(8,128)} fusion(bf16[2048,1568]{0,1:T(8,128)(2,1)} %get-tuple-element.143, bf16[2048,768]{1,0:T(8,128)(2,1)S(1)} %copy-done.5), kind=kOutput, calls=%fused_computation.204 | convolution fusion | flops 4932501504 | bytes 14385152 | tf_op jit(solution)/shard_map/dot_general | solution.py:47
  290.3 5.1 %collective-permute-done.36 = bf16[128,768]{1,0:T(8,128)(2,1)S(1)} collective-permute-done((bf16[128,768]{1,0:T(8,128)(2,1)S(1)}, bf16[128,768]{1,0:T(8,128)(2,1)S(1)}, u32[]{:S(2)}, u32[]{:S(2)}) %collective-permute-start.36) | collective-permute-done | bytes 196640 | tf_op jit(solution)/shard_map/ppermute | solution.py:835
  295.4 9.1 %collective-permute-done.35 = bf16[128,768]{1,0:T(8,128)(2,1)S(1)} collective-permute-done((bf16[128,768]{1,0:T(8,128)(2,1)S(1)}, bf16[128,768]{1,0:T(8,128)(2,1)S(1)}, u32[]{:S(2)}, u32[]{:S(2)}) %collective-permute-start.35) | collective-permute-done | bytes 196640 | tf_op jit(solution)/shard_map/ppermute | solution.py:835
  306.1 21.7 %feed_backward.1 = (f32[512,768]{1,0:T(8,128)}, f32[8,768]{1,0:T(8,128)}, bf16[16,216,384]{2,1,0:T(8,128)(2,1)}, bf16[16,216,384]{2,1,0:T(8,128)(2,1)}, bf16[16,...) custom-call(s32[4]{0:T(128)} %pad_add_fusion.place, bf16[32,224,768]{2,1,0:T(8,128)(2,1)} %bitcast.150, ...), custom_call_target="tpu_custom_call" | custom-call | tf_op jit(solution)/shard_map/feed_backward/pallas_call | solution.py:543
  328.3 5.3 %out_backward.1 = (f32[512,768]{1,0:T(8,128)}, bf16[512,768]{1,0:T(8,128)(2,1)}, bf16[512,768]{1,0:T(8,128)(2,1)}, f32[8,768]{1,0:T(8,128)}) custom-call(s32[1]{0:T(128)} %bitcast.3.core, bf16[16,56,768]{2,1,0:T(8,128)(2,1)} %bitcast.23.refs_4_.refs_6_.refs_0_, bf16[16,56,768]{2,1,0:T(8,128)(2,1)} %collective-permute-done.7.refs_5_.refs_7_.refs_1_, ...), custom_call_target="tpu_custom_call" | custom-call | tf_op jit(solution)/shard_map/out_backward/pallas_call | solution.py:596
  344.6 8.2 %attention_backward.2 = (bf16[512,384]{1,0:T(8,128)(2,1)}, bf16[512,384]{1,0:T(8,128)(2,1)}, bf16[512,384]{1,0:T(8,128)(2,1)}, f32[8,384]{1,0:T(8,128)}) custom-call(bf16[512,768]{1,0:T(8,128)(2,1)} %get-tuple-element.173.refs_0_, bf16[512,768]{1,0:T(8,128)(2,1)} %get-tuple-element.161.refs_1_, bf16[512,768]{1,0:T(8,128)(2,1)} %get-tuple-element.162.refs_2_, ...), custom_call_target="tpu_custom_call" | custom-call | tf_op jit(solution)/shard_map/attention_backward/pallas_call | solution.py:656
  352.8 8.5 %attention_backward.3 = (bf16[512,384]{1,0:T(8,128)(2,1)}, bf16[512,384]{1,0:T(8,128)(2,1)}, bf16[512,384]{1,0:T(8,128)(2,1)}, f32[8,384]{1,0:T(8,128)}) custom-call(bf16[512,768]{1,0:T(8,128)(2,1)} %get-tuple-element.173.refs_0_, bf16[512,768]{1,0:T(8,128)(2,1)} %get-tuple-element.161.refs_1_, bf16[512,768]{1,0:T(8,128)(2,1)} %get-tuple-element.162.refs_2_, ...), custom_call_target="tpu_custom_call" | custom-call | tf_op jit(solution)/shard_map/attention_backward/pallas_call | solution.py:656
  361.3 8.8 %last_grads.1 = (bf16[16,112,384]{2,1,0:T(8,128)(2,1)}, bf16[16,112,384]{2,1,0:T(8,128)(2,1)}, bf16[16,112,384]{2,1,0:T(8,128)(2,1)}, bf16[16,112,384]{2,1,0:T(8,128)(2,1)}) custom-call(s32[4]{0:T(128)} %pad_add_fusion.place, bf16[512,768]{1,0:T(8,128)(2,1)} %refs_0_.5, bf16[512,768]{1,0:T(8,128)(2,1)} %get-tuple-element.167.refs_1_, ...), custom_call_target="tpu_custom_call" | custom-call | tf_op jit(solution)/shard_map/last_grads/pallas_call | solution.py:734
  389.7 6.9 %tokens_backward.1 = f32[512,768]{1,0:T(8,128)} custom-call(s32[1]{0:T(128)} %bitcast.3.core, bf16[16,56,768]{2,1,0:T(8,128)(2,1)} %bitcast.16.refs_0_.refs_2_, bf16[16,56,768]{2,1,0:T(8,128)(2,1)} %collective-permute-done.4.refs_1_.refs_3_, bf16[16,56,768]{2,1,0:T(8,128)(2,1)} %bitcast.16.refs_0_.refs_2_, ...), custom_call_target="tpu_custom_call" | custom-call | tf_op jit(solution)/shard_map/tokens_backward/pallas_call | solution.py:774
  403.7 8.6 %collective-permute-done.45 = bf16[8,112,384]{2,1,0:T(8,128)(2,1)S(1)} collective-permute-done((bf16[8,112,384]{2,1,0:T(8,128)(2,1)}, bf16[8,112,384]{2,1,0:T(8,128)(2,1)S(1)}, u32[]{:S(2)}, u32[]{:S(2)}) %collective-permute-start.45) | collective-permute-done | bytes 688160 | tf_op jit(solution)/shard_map/ppermute | solution.py:835
  426.2 7.9 %collective-permute-done.52 = bf16[216,768]{1,0:T(8,128)(2,1)S(1)} collective-permute-done((bf16[216,768]{1,0:T(8,128)(2,1)S(1)}, bf16[216,768]{1,0:T(8,128)(2,1)S(1)}, u32[]{:S(2)}, u32[]{:S(2)}) %collective-permute-start.52) | collective-permute-done | bytes 331808 | tf_op jit(solution)/shard_map/ppermute | solution.py:835
  (274 shorter events, 198.5 us)
Async XLA Ops:
  7.2 112.6 %all-gather.3.cloned.1.call-start = ((), (), s32[]{:S(2)}) async-start(), calls=%async_computation | async-start | bytes 11354112 | tf_op jit(solution)/shard_map/all_gather | solution.py:1159
  24.0 24.8 %collective-permute-start.1 = (bf16[2,112,768]{2,1,0:T(8,128)(2,1)S(1)}, bf16[2,112,768]{2,1,0:T(8,128)(2,1)S(1)}, u32[]{:S(2)}, u32[]{:S(2)}) collective-permute-start(bf16[2,112,768]{2,1,0:T(8,128)(2,1)S(1)} %maximum_bitcast_fusion), channel_id=1, source_target_pairs={{0,16},{2,18},{4,20},{6,22},{8,24},{10,26},{12,28},{14,30},{16,0},... | collective-permute-start | bytes 1032200 | tf_op jit(solution)/shard_map/ppermute | solution.py:246
  51.3 17.3 %collective-permute-start.2 = (bf16[4,56,768]{2,1,0:T(8,128)(2,1)}, bf16[4,56,768]{2,1,0:T(8,128)(2,1)}, u32[]{:S(2)}, u32[]{:S(2)}) collective-permute-start(bf16[4,56,768]{2,1,0:T(8,128)(2,1)} %get-tuple-element.263), channel_id=1, source_target_pairs={{0,2},{2,0},{4,6},{6,4},{8,10},{10,8},{12,14},{14,12},{16,18},{18,... | collective-permute-start | bytes 1032200 | tf_op jit(solution)/shard_map/ppermute | solution.py:246
  69.8 21.8 %collective-permute-start.6 = (bf16[4,2,56,768]{3,2,1,0:T(8,128)(2,1)S(1)}, bf16[4,2,56,768]{3,2,1,0:T(8,128)(2,1)S(1)}, u32[]{:S(2)}, u32[]{:S(2)}) collective-permute-start(bf16[4,2,56,768]{3,2,1,0:T(8,128)(2,1)S(1)} %pad_maximum_fusion.7), channel_id=1, source_target_pairs={{0,2},{2,0},{4,6},{6,4},{8,10},{10,8},{12,14},{14,12},{16,18},{18,... | collective-permute-start | bytes 2064392 | tf_op jit(solution)/shard_map/ppermute | solution.py:246
  70.3 22.6 %collective-permute-start.3 = (bf16[4,2,56,768]{3,2,0,1:T(8,128)(2,1)S(1)}, bf16[4,2,56,768]{3,2,0,1:T(8,128)(2,1)S(1)}, u32[]{:S(2)}, u32[]{:S(2)}) collective-permute-start(bf16[4,2,56,768]{3,2,0,1:T(8,128)(2,1)S(1)} %pad_maximum_fusion.6), channel_id=1, source_target_pairs={{0,4},{2,6},{4,0},{6,2},{8,12},{10,14},{12,8},{14,10},{16,20},{18,... | collective-permute-start | bytes 2064392 | tf_op jit(solution)/shard_map/ppermute | solution.py:246
  138.3 18.1 %collective-permute-start.10 = (bf16[128,768]{1,0:T(8,128)(2,1)}, bf16[128,768]{1,0:T(8,128)(2,1)S(1)}, u32[]{:S(2)}, u32[]{:S(2)}) collective-permute-start(bf16[128,768]{1,0:T(8,128)(2,1)} %get-tuple-element.120), channel_id=1, source_target_pairs={{0,24},{2,26},{4,28},{6,30},{8,16},{10,18},{12,20},{14,22},{16,8},... | collective-permute-start | bytes 589832 | tf_op jit(solution)/shard_map/ppermute | solution.py:835
  153.5 18.3 %collective-permute-start.18 = (bf16[2,128,384]{2,1,0:T(8,128)(2,1)S(1)}, bf16[2,128,384]{2,1,0:T(8,128)(2,1)S(1)}, u32[]{:S(2)}, u32[]{:S(2)}) collective-permute-start(bf16[2,128,384]{2,1,0:T(8,128)(2,1)S(1)} %pad_maximum_fusion.17), channel_id=1, source_target_pairs={{0,2},{2,0},{4,6},{6,4},{8,10},{10,8},{12,14},{14,12},{16,18},{18,... | collective-permute-start | bytes 589832 | tf_op jit(solution)/shard_map/ppermute | solution.py:835
  155.3 16.6 %collective-permute-start.17 = (bf16[2,128,384]{2,1,0:T(8,128)(2,1)S(1)}, bf16[2,128,384]{2,1,0:T(8,128)(2,1)S(1)}, u32[]{:S(2)}, u32[]{:S(2)}) collective-permute-start(bf16[2,128,384]{2,1,0:T(8,128)(2,1)S(1)} %pad_maximum_fusion.16), channel_id=1, source_target_pairs={{0,4},{2,6},{4,0},{6,2},{8,12},{10,14},{12,8},{14,10},{16,20},{18,... | collective-permute-start | bytes 589832 | tf_op jit(solution)/shard_map/ppermute | solution.py:835
  173.1 17.0 %collective-permute-start.15 = (bf16[6,128,384]{2,1,0:T(8,128)(2,1)S(1)}, bf16[6,128,384]{2,1,0:T(8,128)(2,1)}, u32[]{:S(2)}, u32[]{:S(2)}) collective-permute-start(bf16[6,128,384]{2,1,0:T(8,128)(2,1)S(1)} %pad_maximum_fusion.9), channel_id=1, source_target_pairs={{0,4},{2,6},{4,0},{6,2},{8,12},{10,14},{12,8},{14,10},{16,20},{18,... | collective-permute-start | bytes 1769480 | tf_op jit(solution)/shard_map/ppermute | solution.py:835
  175.8 15.6 %collective-permute-start.16 = (bf16[6,128,384]{2,1,0:T(8,128)(2,1)}, bf16[6,128,384]{2,1,0:T(8,128)(2,1)}, u32[]{:S(2)}, u32[]{:S(2)}) collective-permute-start(bf16[6,128,384]{2,1,0:T(8,128)(2,1)} %pad_maximum_fusion.10), channel_id=1, source_target_pairs={{0,2},{2,0},{4,6},{6,4},{8,10},{10,8},{12,14},{14,12},{16,18},{18,... | collective-permute-start | bytes 1769480 | tf_op jit(solution)/shard_map/ppermute | solution.py:835
  248.6 19.8 %collective-permute-start.29 = (bf16[8,128,384]{2,1,0:T(8,128)(2,1)S(1)}, bf16[8,128,384]{2,1,0:T(8,128)(2,1)}, u32[]{:S(2)}, u32[]{:S(2)}) collective-permute-start(bf16[8,128,384]{2,1,0:T(8,128)(2,1)S(1)} %add_convert_fusion.3), channel_id=1, source_target_pairs={{0,2},{2,0},{4,6},{6,4},{8,10},{10,8},{12,14},{14,12},{16,18},{18,... | collective-permute-start | bytes 2359304 | tf_op jit(solution)/shard_map/ppermute | solution.py:835
  249.8 19.5 %collective-permute-start.31 = (bf16[8,128,384]{2,1,0:T(8,128)(2,1)S(1)}, bf16[8,128,384]{2,1,0:T(8,128)(2,1)}, u32[]{:S(2)}, u32[]{:S(2)}) collective-permute-start(bf16[8,128,384]{2,1,0:T(8,128)(2,1)S(1)} %add_convert_fusion.2), channel_id=1, source_target_pairs={{0,4},{2,6},{4,0},{6,2},{8,12},{10,14},{12,8},{14,10},{16,20},{18,... | collective-permute-start | bytes 2359304 | tf_op jit(solution)/shard_map/ppermute | solution.py:835
  288.0 16.5 %collective-permute-start.35 = (bf16[128,768]{1,0:T(8,128)(2,1)S(1)}, bf16[128,768]{1,0:T(8,128)(2,1)S(1)}, u32[]{:S(2)}, u32[]{:S(2)}) collective-permute-start(bf16[128,768]{1,0:T(8,128)(2,1)S(1)} %pad_maximum_fusion.19), channel_id=1, source_target_pairs={{0,16},{2,18},{4,20},{6,22},{8,24},{10,26},{12,28},{14,30},{16,0},... | collective-permute-start | bytes 589832 | tf_op jit(solution)/shard_map/ppermute | solution.py:835
  341.5 31.5 %collective-permute-start.39 = (bf16[8,216,384]{2,1,0:T(8,128)(2,1)}, bf16[8,216,384]{2,1,0:T(8,128)(2,1)}, u32[]{:S(2)}, u32[]{:S(2)}) collective-permute-start(bf16[8,216,384]{2,1,0:T(8,128)(2,1)} %get-tuple-element.180), channel_id=1, source_target_pairs={{0,2},{2,0},{4,6},{6,4},{8,10},{10,8},{12,14},{14,12},{16,18},{18,... | collective-permute-start | bytes 3981320 | tf_op jit(solution)/shard_map/ppermute | solution.py:835
  342.9 31.2 %collective-permute-start.40 = (bf16[8,216,384]{2,1,0:T(8,128)(2,1)}, bf16[8,216,384]{2,1,0:T(8,128)(2,1)}, u32[]{:S(2)}, u32[]{:S(2)}) collective-permute-start(bf16[8,216,384]{2,1,0:T(8,128)(2,1)} %get-tuple-element.181), channel_id=1, source_target_pairs={{0,4},{2,6},{4,0},{6,2},{8,12},{10,14},{12,8},{14,10},{16,20},{18,... | collective-permute-start | bytes 3981320 | tf_op jit(solution)/shard_map/ppermute | solution.py:835
  379.2 18.2 %collective-permute-start.51 = (bf16[4,216,384]{2,1,0:T(8,128)(2,1)}, bf16[4,216,384]{2,1,0:T(8,128)(2,1)}, u32[]{:S(2)}, u32[]{:S(2)}) collective-permute-start(bf16[4,216,384]{2,1,0:T(8,128)(2,1)} %add_convert_fusion.6), channel_id=1, source_target_pairs={{0,2},{2,0},{4,6},{6,4},{8,10},{10,8},{12,14},{14,12},{16,18},{18,... | collective-permute-start | bytes 1990664 | tf_op jit(solution)/shard_map/ppermute | solution.py:835
  381.7 18.2 %collective-permute-start.50 = (bf16[4,216,384]{2,1,0:T(8,128)(2,1)}, bf16[4,216,384]{2,1,0:T(8,128)(2,1)}, u32[]{:S(2)}, u32[]{:S(2)}) collective-permute-start(bf16[4,216,384]{2,1,0:T(8,128)(2,1)} %add_convert_fusion.7), channel_id=1, source_target_pairs={{0,4},{2,6},{4,0},{6,2},{8,12},{10,14},{12,8},{14,10},{16,20},{18,... | collective-permute-start | bytes 1990664 | tf_op jit(solution)/shard_map/ppermute | solution.py:835
  387.9 24.3 %collective-permute-start.45 = (bf16[8,112,384]{2,1,0:T(8,128)(2,1)}, bf16[8,112,384]{2,1,0:T(8,128)(2,1)S(1)}, u32[]{:S(2)}, u32[]{:S(2)}) collective-permute-start(bf16[8,112,384]{2,1,0:T(8,128)(2,1)} %add_convert_fusion.4), channel_id=1, source_target_pairs={{0,4},{2,6},{4,0},{6,2},{8,12},{10,14},{12,8},{14,10},{16,20},{18,... | collective-permute-start | bytes 2064392 | tf_op jit(solution)/shard_map/ppermute | solution.py:835
  388.3 26.5 %collective-permute-start.43 = (bf16[8,112,384]{2,1,0:T(8,128)(2,1)}, bf16[8,112,384]{2,1,0:T(8,128)(2,1)S(1)}, u32[]{:S(2)}, u32[]{:S(2)}) collective-permute-start(bf16[8,112,384]{2,1,0:T(8,128)(2,1)} %add_convert_fusion.5), channel_id=1, source_target_pairs={{0,2},{2,0},{4,6},{6,4},{8,10},{10,8},{12,14},{14,12},{16,18},{18,... | collective-permute-start | bytes 2064392 | tf_op jit(solution)/shard_map/ppermute | solution.py:835
  402.1 32.1 %collective-permute-start.54 = (bf16[216,768]{1,0:T(8,128)(2,1)S(1)}, bf16[216,768]{1,0:T(8,128)(2,1)S(1)}, u32[]{:S(2)}, u32[]{:S(2)}) collective-permute-start(bf16[216,768]{1,0:T(8,128)(2,1)S(1)} %pad_maximum_fusion.13), channel_id=1, source_target_pairs={{0,24},{2,26},{4,28},{6,30},{8,16},{10,18},{12,20},{14,22},{16,8},... | collective-permute-start | bytes 995336 | tf_op jit(solution)/shard_map/ppermute | solution.py:835
  403.6 35.6 %collective-permute-start.53 = (bf16[216,768]{1,0:T(8,128)(2,1)S(1)}, bf16[216,768]{1,0:T(8,128)(2,1)S(1)}, u32[]{:S(2)}, u32[]{:S(2)}) collective-permute-start(bf16[216,768]{1,0:T(8,128)(2,1)S(1)} %pad_maximum_fusion.12), channel_id=1, source_target_pairs={{0,16},{2,18},{4,20},{6,22},{8,24},{10,26},{12,28},{14,30},{16,0},... | collective-permute-start | bytes 995336 | tf_op jit(solution)/shard_map/ppermute | solution.py:835
  417.1 17.1 %collective-permute-start.52 = (bf16[216,768]{1,0:T(8,128)(2,1)S(1)}, bf16[216,768]{1,0:T(8,128)(2,1)S(1)}, u32[]{:S(2)}, u32[]{:S(2)}) collective-permute-start(bf16[216,768]{1,0:T(8,128)(2,1)S(1)} %pad_maximum_fusion.11), channel_id=1, source_target_pairs={{0,8},{2,10},{4,12},{6,14},{8,0},{10,2},{12,4},{14,6},{16,24},{18,... | collective-permute-start | bytes 995336 | tf_op jit(solution)/shard_map/ppermute | solution.py:835
  424.7 16.9 %collective-permute-start.49 = (bf16[112,768]{1,0:T(8,128)(2,1)S(1)}, bf16[112,768]{1,0:T(8,128)(2,1)S(1)}, u32[]{:S(2)}, u32[]{:S(2)}) collective-permute-start(bf16[112,768]{1,0:T(8,128)(2,1)S(1)} %pad_maximum_fusion.23), channel_id=1, source_target_pairs={{0,24},{2,26},{4,28},{6,30},{8,16},{10,18},{12,20},{14,22},{16,8},... | collective-permute-start | bytes 516104 | tf_op jit(solution)/shard_map/ppermute | solution.py:835
  426.1 16.8 %collective-permute-start.48 = (bf16[112,768]{1,0:T(8,128)(2,1)S(1)}, bf16[112,768]{1,0:T(8,128)(2,1)S(1)}, u32[]{:S(2)}, u32[]{:S(2)}) collective-permute-start(bf16[112,768]{1,0:T(8,128)(2,1)S(1)} %pad_maximum_fusion.22), channel_id=1, source_target_pairs={{0,16},{2,18},{4,20},{6,22},{8,24},{10,26},{12,28},{14,30},{16,0},... | collective-permute-start | bytes 516104 | tf_op jit(solution)/shard_map/ppermute | solution.py:835
  (52 other events, 577.2 us)
Sparse Core Ops, SparseCore 0:
  11.5 108.2 all-gather.2
